TPU v7x, 32 devices: a whole 2x2x4 slice. The times are simulated.
32 devices in a mesh: gx: 4 (over y, core), gy: 2 (over x), ch: 4 (over z).
Axes of the slice: x: 2, y: 2, z: 4, core: 2. Of those that a mesh axis runs over, the one named last changes fastest.
Arguments:
- density: bfloat16 [4, 32, 128, 128], P('gx', 'gy', 'ch'), may hold values from -6 to 6
- first_kernel: bfloat16 [3, 3, 3, 128, 128], P(None, None, None, 'ch'), may hold values from -0.109375 to 0.109375
- first_bias: float32 [128], P('ch'), may hold values from -3 to 3
- second_kernel: bfloat16 [3, 3, 3, 128, 128], P(None, None, None, 'ch'), may hold values from -0.109375 to 0.109375
- second_bias: float32 [128], P('ch'), may hold values from -3 to 3
Outputs:
- features: bfloat16 [4, 32, 128, 128], P('gx', 'gy', 'ch')
All inputs are finite; a program needn't handle non-finite values.
Results may differ from a plain program's by a relative error of at most 0.0045.
Values may be sent and summed in bfloat16 or wider, within the bound.
No kernel may reach another device: no remote copies, remote signals or barrier semaphores. Data moves between devices by JAX's collectives and lax.ppermute only.
A program may use at most 64 MiB of HBM per device.

v0:
```python
import jax
import jax.numpy as jnp
from jax import lax
from jax.sharding import PartitionSpec as P


def with_halo(block, sides, width):
    for axis, dim in sides:
        count = lax.axis_size(axis)
        forward = [(i, i + 1) for i in range(count - 1)]
        backward = [(target, source) for source, target in forward]
        low = lax.ppermute(
            lax.slice_in_dim(block, block.shape[dim] - width, None, axis=dim), axis, forward
        )
        high = lax.ppermute(lax.slice_in_dim(block, 0, width, axis=dim), axis, backward)
        block = jnp.concatenate([low, block, high], axis=dim)
    return block


def conv_taps(padded, kernel):
    result = lax.conv_general_dilated(
        padded[None],
        kernel,
        (1, 1, 1),
        "VALID",
        dimension_numbers=("NHWCD", "HWDOI", "NHWCD"),
        preferred_element_type=jnp.float32,
    )
    return result[0]


def finish(total, bias):
    return jnp.maximum(total + bias.reshape(1, 1, -1, 1), 0.0).astype(jnp.bfloat16)


def pad_depth(field):
    return jnp.pad(field, ((0, 0), (0, 0), (0, 0), (1, 1)))


def layer_channels(field, kernel, bias):
    whole = lax.all_gather(field, "ch", axis=2, tiled=True)
    padded = with_halo(pad_depth(whole), (("gx", 0), ("gy", 1)), 1)
    total = conv_taps(padded, kernel)
    return finish(total, bias)


def per_device(density, first_kernel, first_bias, second_kernel, second_bias):
    hidden = layer_channels(density, first_kernel, first_bias)
    return layer_channels(hidden, second_kernel, second_bias)


def solution(mesh):
    placed = (
        P("gx", "gy", "ch", None),
        P(None, None, None, "ch", None),
        P("ch"),
        P(None, None, None, "ch", None),
        P("ch"),
    )
    return jax.shard_map(
        per_device, mesh=mesh, in_specs=placed, out_specs=P("gx", "gy", "ch", None), check_vma=False
    )
```

profile of v0, /device:TPU:1, one launch (start us, length us, event | category | flops | bytes accessed | tf_op | source)
XLA Modules:
  0.0 125.0 jit_solution(12742077173878891672)
XLA Ops:
  0.0 1.0 copy.78
  1.0 15.3 %all_gather.6 = bf16[1,16,128,128]{3,1,0,2:T(8,128)(2,1)S(1)} all-gather(bf16[1,16,32,128]{3,1,0,2:T(8,128)(2,1)S(1)} %copy.78), channel_id=1, replica_groups=mesh['gx'=4,'gy'=2,'ch'=4] {'ch'}, dimensions={2}, use_global_device_ids=true | all-gather | bytes 655360 | tf_op jit(solution)/shard_map/all_gather | solution.py:41
  16.3 0.4 pad.7
  16.7 1.2 copy.79
  17.9 4.0 %collective-permute-start.1 = (bf16[1,16,128,130]{2,1,3,0:T(8,128)(2,1)S(1)}, bf16[1,16,128,130]{2,1,3,0:T(8,128)(2,1)S(1)}, u32[]{:S(2)}, u32[]{:S(2)}) collective-permute-start(bf16[1,16,128,130]{2,1,3,0:T(8,128)(2,1)S(1)} %copy.79), channel_id=1, source_target_pairs={{8,0},{16,8},{24,16},{9,1},{17,9},{25,17},{10,2},{18,10},{26,18},{... | collective-permute-start | bytes 1597448 | tf_op jit(solution)/shard_map/ppermute | solution.py:15
  21.9 3.0 %collective-permute-start = (bf16[1,16,128,130]{2,1,3,0:T(8,128)(2,1)S(1)}, bf16[1,16,128,130]{2,1,3,0:T(8,128)(2,1)S(1)}, u32[]{:S(2)}, u32[]{:S(2)}) collective-permute-start(bf16[1,16,128,130]{2,1,3,0:T(8,128)(2,1)S(1)} %copy.79), channel_id=1, source_target_pairs={{0,8},{8,16},{16,24},{1,9},{9,17},{17,25},{2,10},{10,18},{18,26},{... | collective-permute-start | bytes 1597448 | tf_op jit(solution)/shard_map/ppermute | solution.py:12
  25.0 5.0 %collective-permute-done.1 = bf16[1,16,128,130]{2,1,3,0:T(8,128)(2,1)S(1)} collective-permute-done((bf16[1,16,128,130]{2,1,3,0:T(8,128)(2,1)S(1)}, bf16[1,16,128,130]{2,1,3,0:T(8,128)(2,1)S(1)}, u32[]{:S(2)}, u32[]{:S(2)}) %collective-permute-start.1) | collective-permute-done | bytes 532512 | tf_op jit(solution)/shard_map/ppermute | solution.py:15
  30.0 1.8 %copy.82 = bf16[1,16,128,130]{3,1,0,2:T(8,128)(2,1)} copy(bf16[1,16,128,130]{2,1,3,0:T(8,128)(2,1)S(1)} %collective-permute-done.1) | data formatting | bytes 1064960 | tf_op jit(solution)/shard_map/ppermute | solution.py:15
  31.8 1.8 %copy.81 = bf16[1,16,128,130]{3,1,0,2:T(8,128)(2,1)} copy(bf16[1,16,128,130]{2,1,3,0:T(8,128)(2,1)S(1)} %collective-permute-done) | data formatting | bytes 1064960 | tf_op jit(solution)/shard_map/ppermute | solution.py:12
  33.7 2.4 %pad_maximum_fusion = bf16[3,16,128,130]{3,1,0,2:T(8,128)(2,1)S(1)} fusion(bf16[1,16,128,130]{3,1,0,2:T(8,128)(2,1)} %copy.82, bf16[1,16,128,130]{3,1,0,2:T(8,128)(2,1)} %copy-done.1, bf16[1,16,128,130]{3,1,0,2:T(8,128)(2,1)} %copy.81), kind=kLoop, calls=%fused_computation.3 | loop fusion | flops 1597440 | bytes 3194880 | tf_op jit(solution)/shard_map/concatenate | solution.py:16
  36.1 1.5 %fusion.35 = (bf16[3,1,128,130]{3,1,0,2:T(2,128)(2,1)}, bf16[3,1,128,130]{3,1,0,2:T(2,128)(2,1)}) fusion(bf16[3,16,128,130]{3,1,0,2:T(8,128)(2,1)S(1)} %pad_maximum_fusion), kind=kLoop, calls=%fused_computation.36 | loop fusion | bytes 399360 | tf_op jit(solution)/shard_map/slice | solution.py:13
  37.6 1.2 copy.83
  38.8 1.8 %copy.84 = bf16[3,1,128,130]{2,3,1,0:T(8,128)(2,1)} copy(bf16[3,1,128,130]{3,1,0,2:T(2,128)(2,1)} %get-tuple-element.8) | data formatting | bytes 199680 | tf_op jit(solution)/shard_map/slice | solution.py:15
  40.6 1.3 %collective-permute-start.3 = (bf16[3,1,128,130]{2,3,1,0:T(8,128)(2,1)}, bf16[3,1,128,130]{2,3,1,0:T(8,128)(2,1)}, u32[]{:S(2)}, u32[]{:S(2)}) collective-permute-start(bf16[3,1,128,130]{2,3,1,0:T(8,128)(2,1)} %copy.84), channel_id=1, source_target_pairs={{4,0},{5,1},{6,2},{7,3},{12,8},{13,9},{14,10},{15,11},{20,16},{21,... | collective-permute-start | bytes 299528 | tf_op jit(solution)/shard_map/ppermute | solution.py:15
  41.9 5.3 %collective-permute-start.2 = (bf16[3,1,128,130]{2,3,1,0:T(8,128)(2,1)S(1)}, bf16[3,1,128,130]{2,3,1,0:T(8,128)(2,1)}, u32[]{:S(2)}, u32[]{:S(2)}) collective-permute-start(bf16[3,1,128,130]{2,3,1,0:T(8,128)(2,1)S(1)} %copy.83), channel_id=1, source_target_pairs={{0,4},{1,5},{2,6},{3,7},{8,12},{9,13},{10,14},{11,15},{16,20},{17,... | collective-permute-start | bytes 299528 | tf_op jit(solution)/shard_map/ppermute | solution.py:12
  47.2 3.2 %copy.85 = bf16[3,16,128,130]{2,3,1,0:T(8,128)(2,1)} copy(bf16[3,16,128,130]{3,1,0,2:T(8,128)(2,1)S(1)} %pad_maximum_fusion) | data formatting | bytes 3194880 | tf_op jit(solution)/shard_map/concatenate | solution.py:16
  50.3 1.7 %maximum_bitcast_fusion = bf16[3,18,128,1,130]{2,4,1,0,3:T(8,128)(2,1)S(1)} fusion(bf16[3,1,128,130]{2,3,1,0:T(8,128)(2,1)} %collective-permute-done.3, bf16[3,16,128,130]{2,3,1,0:T(8,128)(2,1)} %copy.85, bf16[3,1,128,130]{2,3,1,0:T(8,128)(2,1)} %collective-permute-done.2), kind=kLoop, calls=%fused_computation.17 | loop fusion | flops 1797120 | bytes 3594240 | tf_op jit(solution)/shard_map/broadcast_in_dim | solution.py:22
  52.1 1.4 %pad.9 = bf16[3,18,128,1,136]{2,4,1,0,3:T(8,128)(2,1)} pad(bf16[3,18,128,1,130]{2,4,1,0,3:T(8,128)(2,1)S(1)} %maximum_bitcast_fusion, bf16[]{:T(256)} %constant.1.clone.1), padding=0_0x0_0x0_0x0_0x0_6 | pad | bytes 3677186 | tf_op jit(solution)/shard_map/broadcast_in_dim | solution.py:22
  53.5 3.3 %reshape.50 = bf16[3,18,128,1,8,17]{2,5,4,1,0,3:T(8,128)(2,1)S(1)} reshape(bf16[3,18,128,1,136]{2,4,1,0,3:T(8,128)(2,1)} %pad.9) | data formatting | bytes 3760128 | tf_op jit(solution)/shard_map/conv_general_dilated | solution.py:21
  56.8 0.3 copy.87
  57.2 0.3 copy-done.6
  57.5 4.2 %fusion.19 = f32[1,16,8,17,32]{4,2,3,1,0:T(8,128)S(1)} fusion(bf16[3,3,3,32,128]{4,3,2,1,0:T(8,128)(2,1)S(1)} %copy-done, bf16[3,18,128,1,7,2]{2,4,5,1,0,3:T(8,128)(2,1)S(1)} %slice.22, bf16[3,18,128,1,8,17]{2,4,5,1,0,3:T(8,128)(2,1)S(1)} %copy.87, pred[8,17]{0,1:T(8,128)(4,1)S(1)} %copy-done.6), kind=kOutput, calls=%fused_computation.20 | convolution fusion | flops 487669760 | bytes 2573448 | tf_op jit(solution)/shard_map/conv_general_dilated | solution.py:21
  61.8 0.2 copy.88
  62.1 0.4 copy.102
  62.8 12.7 %all_gather.7 = bf16[1,16,128,128]{3,1,0,2:T(8,128)(2,1)S(1)} all-gather(bf16[1,16,32,128]{3,1,0,2:T(8,128)(2,1)S(1)} %copy.90), channel_id=1, replica_groups=mesh['gx'=4,'gy'=2,'ch'=4] {'ch'}, dimensions={2}, use_global_device_ids=true | all-gather | bytes 655360 | tf_op jit(solution)/shard_map/all_gather | solution.py:41
  75.5 0.4 pad.8
  75.9 1.2 copy.91
  77.1 1.9 %collective-permute-start.5 = (bf16[1,16,128,130]{2,1,3,0:T(8,128)(2,1)S(1)}, bf16[1,16,128,130]{2,1,3,0:T(8,128)(2,1)S(1)}, u32[]{:S(2)}, u32[]{:S(2)}) collective-permute-start(bf16[1,16,128,130]{2,1,3,0:T(8,128)(2,1)S(1)} %copy.91), channel_id=1, source_target_pairs={{8,0},{16,8},{24,16},{9,1},{17,9},{25,17},{10,2},{18,10},{26,18},{... | collective-permute-start | bytes 1597448 | tf_op jit(solution)/shard_map/ppermute | solution.py:15
  79.1 6.8 %collective-permute-start.4 = (bf16[1,16,128,130]{2,1,3,0:T(8,128)(2,1)S(1)}, bf16[1,16,128,130]{2,1,3,0:T(8,128)(2,1)S(1)}, u32[]{:S(2)}, u32[]{:S(2)}) collective-permute-start(bf16[1,16,128,130]{2,1,3,0:T(8,128)(2,1)S(1)} %copy.91), channel_id=1, source_target_pairs={{0,8},{8,16},{16,24},{1,9},{9,17},{17,25},{2,10},{10,18},{18,26},{... | collective-permute-start | bytes 1597448 | tf_op jit(solution)/shard_map/ppermute | solution.py:12
  85.9 4.8 %collective-permute-done.5 = bf16[1,16,128,130]{2,1,3,0:T(8,128)(2,1)S(1)} collective-permute-done((bf16[1,16,128,130]{2,1,3,0:T(8,128)(2,1)S(1)}, bf16[1,16,128,130]{2,1,3,0:T(8,128)(2,1)S(1)}, u32[]{:S(2)}, u32[]{:S(2)}) %collective-permute-start.5) | collective-permute-done | bytes 532512 | tf_op jit(solution)/shard_map/ppermute | solution.py:15
  90.7 1.8 %copy.94 = bf16[1,16,128,130]{3,1,0,2:T(8,128)(2,1)} copy(bf16[1,16,128,130]{2,1,3,0:T(8,128)(2,1)S(1)} %collective-permute-done.5) | data formatting | bytes 1064960 | tf_op jit(solution)/shard_map/ppermute | solution.py:15
  92.6 1.8 %copy.93 = bf16[1,16,128,130]{3,1,0,2:T(8,128)(2,1)} copy(bf16[1,16,128,130]{2,1,3,0:T(8,128)(2,1)S(1)} %collective-permute-done.4) | data formatting | bytes 1064960 | tf_op jit(solution)/shard_map/ppermute | solution.py:12
  94.4 2.4 %pad_maximum_fusion.1 = bf16[3,16,128,130]{3,1,0,2:T(8,128)(2,1)S(1)} fusion(bf16[1,16,128,130]{3,1,0,2:T(8,128)(2,1)} %copy.94, bf16[1,16,128,130]{3,1,0,2:T(8,128)(2,1)} %copy-done.2, bf16[1,16,128,130]{3,1,0,2:T(8,128)(2,1)} %copy.93), kind=kLoop, calls=%fused_computation.4 | loop fusion | flops 1597440 | bytes 3194880 | tf_op jit(solution)/shard_map/concatenate | solution.py:16
  96.9 1.5 %fusion.34 = (bf16[3,1,128,130]{3,1,0,2:T(2,128)(2,1)}, bf16[3,1,128,130]{3,1,0,2:T(2,128)(2,1)}) fusion(bf16[3,16,128,130]{3,1,0,2:T(8,128)(2,1)S(1)} %pad_maximum_fusion.1), kind=kLoop, calls=%fused_computation.35 | loop fusion | bytes 399360 | tf_op jit(solution)/shard_map/slice | solution.py:13
  98.4 3.3 %collective-permute-start.6 = (bf16[3,1,128,130]{3,1,0,2:T(2,128)(2,1)}, bf16[3,1,128,130]{3,1,0,2:T(2,128)(2,1)}, u32[]{:S(2)}, u32[]{:S(2)}) collective-permute-start(bf16[3,1,128,130]{3,1,0,2:T(2,128)(2,1)} %get-tuple-element.5), channel_id=1, source_target_pairs={{0,4},{1,5},{2,6},{3,7},{8,12},{9,13},{10,14},{11,15},{16,20},{17,... | collective-permute-start | bytes 299528 | tf_op jit(solution)/shard_map/ppermute | solution.py:12
  101.7 1.3 %collective-permute-start.7 = (bf16[3,1,128,130]{3,1,0,2:T(2,128)(2,1)}, bf16[3,1,128,130]{3,1,0,2:T(2,128)(2,1)}, u32[]{:S(2)}, u32[]{:S(2)}) collective-permute-start(bf16[3,1,128,130]{3,1,0,2:T(2,128)(2,1)} %get-tuple-element.6), channel_id=1, source_target_pairs={{4,0},{5,1},{6,2},{7,3},{12,8},{13,9},{14,10},{15,11},{20,16},{21,... | collective-permute-start | bytes 299528 | tf_op jit(solution)/shard_map/ppermute | solution.py:15
  103.0 3.2 %copy.96 = bf16[3,16,128,130]{2,3,1,0:T(8,128)(2,1)} copy(bf16[3,16,128,130]{3,1,0,2:T(8,128)(2,1)S(1)} %pad_maximum_fusion.1) | data formatting | bytes 3194880 | tf_op jit(solution)/shard_map/concatenate | solution.py:16
  106.1 1.2 copy.95
  107.4 3.1 %collective-permute-done.7 = bf16[3,1,128,130]{3,1,0,2:T(2,128)(2,1)} collective-permute-done((bf16[3,1,128,130]{3,1,0,2:T(2,128)(2,1)}, bf16[3,1,128,130]{3,1,0,2:T(2,128)(2,1)}, u32[]{:S(2)}, u32[]{:S(2)}) %collective-permute-start.7) | collective-permute-done | bytes 99872 | tf_op jit(solution)/shard_map/ppermute | solution.py:15
  110.5 1.2 copy.97
  111.7 1.7 %maximum_bitcast_fusion.1 = bf16[3,18,128,1,130]{2,4,1,0,3:T(8,128)(2,1)S(1)} fusion(bf16[3,1,128,130]{2,3,1,0:T(8,128)(2,1)S(1)} %copy.97, bf16[3,16,128,130]{2,3,1,0:T(8,128)(2,1)} %copy.96, bf16[3,1,128,130]{2,3,1,0:T(8,128)(2,1)S(1)} %copy.95), kind=kLoop, calls=%fused_computation.18 | loop fusion | flops 1797120 | bytes 3594240 | tf_op jit(solution)/shard_map/broadcast_in_dim | solution.py:22
  113.4 1.4 %pad.11 = bf16[3,18,128,1,136]{2,4,1,0,3:T(8,128)(2,1)} pad(bf16[3,18,128,1,130]{2,4,1,0,3:T(8,128)(2,1)S(1)} %maximum_bitcast_fusion.1, bf16[]{:T(256)} %constant.1.clone.1), padding=0_0x0_0x0_0x0_0x0_6 | pad | bytes 3677186 | tf_op jit(solution)/shard_map/broadcast_in_dim | solution.py:22
  114.8 3.3 %reshape.57 = bf16[3,18,128,1,8,17]{2,5,4,1,0,3:T(8,128)(2,1)S(1)} reshape(bf16[3,18,128,1,136]{2,4,1,0,3:T(8,128)(2,1)} %pad.11) | data formatting | bytes 3760128 | tf_op jit(solution)/shard_map/conv_general_dilated | solution.py:21
  118.2 0.3 copy.99
  118.5 0.6 copy-done.5
  119.1 4.2 %fusion.16 = f32[1,16,8,17,32]{4,2,3,1,0:T(8,128)S(1)} fusion(bf16[3,3,3,32,128]{4,3,2,1,0:T(8,128)(2,1)S(1)} %copy-done.5, bf16[3,18,128,1,7,2]{2,4,5,1,0,3:T(8,128)(2,1)S(1)} %slice.26, bf16[3,18,128,1,8,17]{2,4,5,1,0,3:T(8,128)(2,1)S(1)} %copy.99, pred[8,17]{0,1:T(8,128)(4,1)S(1)} %copy-done.6), kind=kOutput, calls=%fused_computation.19 | convolution fusion | flops 487669760 | bytes 2573448 | tf_op jit(solution)/shard_map/conv_general_dilated | solution.py:21
  123.7 0.4 copy.103
  124.3 0.8 fusion.25
  (24 shorter events, 1.0 us)
Async XLA Ops:
  0.0 57.2 %copy-start = (bf16[3,3,3,32,128]{4,3,2,1,0:T(8,128)(2,1)S(1)}, bf16[3,3,3,32,128]{4,3,2,1,0:T(8,128)(2,1)}, u32[]{:S(2)}) copy-start(bf16[3,3,3,32,128]{4,3,2,1,0:T(8,128)(2,1)} %param.6) | copy-start | bytes 663556
  16.7 15.1 %copy-start.1 = (bf16[1,16,128,130]{3,1,0,2:T(8,128)(2,1)}, bf16[1,16,128,130]{3,1,0,2:T(8,128)(2,1)S(1)}, u32[]{:S(2)}) copy-start(bf16[1,16,128,130]{3,1,0,2:T(8,128)(2,1)S(1)} %pad.7) | copy-start | bytes 1597444
  17.9 12.1 %collective-permute-start.1 = (bf16[1,16,128,130]{2,1,3,0:T(8,128)(2,1)S(1)}, bf16[1,16,128,130]{2,1,3,0:T(8,128)(2,1)S(1)}, u32[]{:S(2)}, u32[]{:S(2)}) collective-permute-start(bf16[1,16,128,130]{2,1,3,0:T(8,128)(2,1)S(1)} %copy.79), channel_id=1, source_target_pairs={{8,0},{16,8},{24,16},{9,1},{17,9},{25,17},{10,2},{18,10},{26,18},{... | collective-permute-start | bytes 1597448 | tf_op jit(solution)/shard_map/ppermute | solution.py:15
  21.9 9.9 %collective-permute-start = (bf16[1,16,128,130]{2,1,3,0:T(8,128)(2,1)S(1)}, bf16[1,16,128,130]{2,1,3,0:T(8,128)(2,1)S(1)}, u32[]{:S(2)}, u32[]{:S(2)}) collective-permute-start(bf16[1,16,128,130]{2,1,3,0:T(8,128)(2,1)S(1)} %copy.79), channel_id=1, source_target_pairs={{0,8},{8,16},{16,24},{1,9},{9,17},{17,25},{2,10},{10,18},{18,26},{... | collective-permute-start | bytes 1597448 | tf_op jit(solution)/shard_map/ppermute | solution.py:12
  40.6 9.7 %collective-permute-start.3 = (bf16[3,1,128,130]{2,3,1,0:T(8,128)(2,1)}, bf16[3,1,128,130]{2,3,1,0:T(8,128)(2,1)}, u32[]{:S(2)}, u32[]{:S(2)}) collective-permute-start(bf16[3,1,128,130]{2,3,1,0:T(8,128)(2,1)} %copy.84), channel_id=1, source_target_pairs={{4,0},{5,1},{6,2},{7,3},{12,8},{13,9},{14,10},{15,11},{20,16},{21,... | collective-permute-start | bytes 299528 | tf_op jit(solution)/shard_map/ppermute | solution.py:15
  41.9 8.4 %collective-permute-start.2 = (bf16[3,1,128,130]{2,3,1,0:T(8,128)(2,1)S(1)}, bf16[3,1,128,130]{2,3,1,0:T(8,128)(2,1)}, u32[]{:S(2)}, u32[]{:S(2)}) collective-permute-start(bf16[3,1,128,130]{2,3,1,0:T(8,128)(2,1)S(1)} %copy.83), channel_id=1, source_target_pairs={{0,4},{1,5},{2,6},{3,7},{8,12},{9,13},{10,14},{11,15},{16,20},{17,... | collective-permute-start | bytes 299528 | tf_op jit(solution)/shard_map/ppermute | solution.py:12
  56.8 0.7 copy-start.6
  62.0 0.7 copy-start.3
  75.9 16.7 %copy-start.2 = (bf16[1,16,128,130]{3,1,0,2:T(8,128)(2,1)}, bf16[1,16,128,130]{3,1,0,2:T(8,128)(2,1)S(1)}, u32[]{:S(2)}) copy-start(bf16[1,16,128,130]{3,1,0,2:T(8,128)(2,1)S(1)} %pad.8) | copy-start | bytes 1597444
  77.1 13.6 %collective-permute-start.5 = (bf16[1,16,128,130]{2,1,3,0:T(8,128)(2,1)S(1)}, bf16[1,16,128,130]{2,1,3,0:T(8,128)(2,1)S(1)}, u32[]{:S(2)}, u32[]{:S(2)}) collective-permute-start(bf16[1,16,128,130]{2,1,3,0:T(8,128)(2,1)S(1)} %copy.91), channel_id=1, source_target_pairs={{8,0},{16,8},{24,16},{9,1},{17,9},{25,17},{10,2},{18,10},{26,18},{... | collective-permute-start | bytes 1597448 | tf_op jit(solution)/shard_map/ppermute | solution.py:15
  79.1 13.5 %collective-permute-start.4 = (bf16[1,16,128,130]{2,1,3,0:T(8,128)(2,1)S(1)}, bf16[1,16,128,130]{2,1,3,0:T(8,128)(2,1)S(1)}, u32[]{:S(2)}, u32[]{:S(2)}) collective-permute-start(bf16[1,16,128,130]{2,1,3,0:T(8,128)(2,1)S(1)} %copy.91), channel_id=1, source_target_pairs={{0,8},{8,16},{16,24},{1,9},{9,17},{17,25},{2,10},{10,18},{18,26},{... | collective-permute-start | bytes 1597448 | tf_op jit(solution)/shard_map/ppermute | solution.py:12
  98.4 7.8 %collective-permute-start.6 = (bf16[3,1,128,130]{3,1,0,2:T(2,128)(2,1)}, bf16[3,1,128,130]{3,1,0,2:T(2,128)(2,1)}, u32[]{:S(2)}, u32[]{:S(2)}) collective-permute-start(bf16[3,1,128,130]{3,1,0,2:T(2,128)(2,1)} %get-tuple-element.5), channel_id=1, source_target_pairs={{0,4},{1,5},{2,6},{3,7},{8,12},{9,13},{10,14},{11,15},{16,20},{17,... | collective-permute-start | bytes 299528 | tf_op jit(solution)/shard_map/ppermute | solution.py:12
  101.7 8.8 %collective-permute-start.7 = (bf16[3,1,128,130]{3,1,0,2:T(2,128)(2,1)}, bf16[3,1,128,130]{3,1,0,2:T(2,128)(2,1)}, u32[]{:S(2)}, u32[]{:S(2)}) collective-permute-start(bf16[3,1,128,130]{3,1,0,2:T(2,128)(2,1)} %get-tuple-element.6), channel_id=1, source_target_pairs={{4,0},{5,1},{6,2},{7,3},{12,8},{13,9},{14,10},{15,11},{20,16},{21,... | collective-permute-start | bytes 299528 | tf_op jit(solution)/shard_map/ppermute | solution.py:15
  118.2 0.9 copy-start.5
  123.6 0.7 copy-start.4
where the time goes:
time: 127 us; the launch traced here: 125 us
  local copies, waits for them, and re-layouts  39.1 us (31%)
  blocking collectives  28 us (22%)
  starting transfers between devices  27 us (21%)
  waiting for transfers between devices  13 us (10%)
  other arithmetic  9.15 us (7%)
  matrix products  8.49 us (7%)
    all_gather x2, blocking collectives, layer_channels(): whole = lax.all_gather(field, 'ch', axis=2, tiled=True)  28 us
    ppermute x4, starting transfers between devices, with_halo(): lax.ppermute(lax.slice_in_dim(block, block.shape[dim] - width, None, axis...  18.5 us
    ppermute x4, waiting for transfers between devices, with_halo(): lax.ppermute(lax.slice_in_dim(block, 0, width, axis=dim), axis, backward)  13 us
    ppermute x4, starting transfers between devices, with_halo(): lax.ppermute(lax.slice_in_dim(block, 0, width, axis=dim), axis, backward)  8.51 us
    conv_general_dilated x2, matrix products, conv_taps(): lax.conv_general_dilated(padded[None], kernel, (1, 1, 1), 'VALID', dimens...  8.49 us
    conv_general_dilated x10, local copies, waits for them, and re-layouts, conv_taps(): lax.conv_general_dilated(padded[None], kernel, (1, 1, 1), 'VALID', dimens...  7.88 us
    concatenate x2, local copies, waits for them, and re-layouts, with_halo(): block = jnp.concatenate([low, block, high], axis=dim)  6.33 us
    ppermute x3, local copies, waits for them, and re-layouts, with_halo(): lax.ppermute(lax.slice_in_dim(block, block.shape[dim] - width, None, axis...  4.91 us
  transfers between devices with their start and end apart: 8, of which 3 were waited for; matrix products, arithmetic and copies ran while one was open for 9% of the time, Pallas kernels for 0%

commit v1 on v0

v1 whole, which is shorter than its diff:
```python
import functools

import jax
import jax.numpy as jnp
from jax import lax
from jax.experimental import pallas as pl
from jax.experimental.pallas import tpu as pltpu
from jax.sharding import PartitionSpec as P


def shifted(block, axis, step):
    count = lax.axis_size(axis)
    pairs = [(i, i + step) for i in range(count) if 0 <= i + step < count]
    return lax.ppermute(block, axis, pairs)


def gathered(block, axis):
    count = lax.axis_size(axis)
    return [block] + [
        lax.ppermute(block, axis, [(i, (i + step) % count) for i in range(count)])
        for step in range(1, count)
    ]


def taps_kernel(count, place_ref, kernel_ref, *refs):
    blocks, (below_ref, center_ref, above_ref, volume, weights) = refs[:count], refs[count:]
    rows, outputs, depth = center_ref.shape
    part = blocks[0].shape[1]
    inputs = part * count
    place = place_ref[0]
    for step, block in enumerate(blocks):
        source = lax.rem(place - step + count, count)
        volume[:, pl.ds(pl.multiple_of(source * part, part), part), :] = block[...]
    for a in range(3):
        for b in range(3):
            for c in range(3):
                first = (a * 3 + c) * outputs
                weights[first : first + outputs, b * inputs : (b + 1) * inputs] = kernel_ref[a, b, c]
    lane = lax.broadcasted_iota(jnp.int32, (outputs, depth), 1)
    taps = weights[...]
    for y in range(0, rows, 2):
        window = jnp.concatenate(
            [volume[y + i : y + i + 3].reshape(3 * inputs, depth) for i in range(2)], axis=1
        )
        product = jnp.dot(taps, window, preferred_element_type=jnp.float32)
        for i in range(2):
            for a, out in enumerate((above_ref, center_ref, below_ref)):
                first, middle, last = (
                    product[(a * 3 + c) * outputs : (a * 3 + c + 1) * outputs, i * depth : (i + 1) * depth]
                    for c in range(3)
                )
                total = (
                    middle
                    + jnp.where(lane == 0, 0.0, pltpu.roll(first, 1, 1))
                    + jnp.where(lane == depth - 1, 0.0, pltpu.roll(last, depth - 1, 1))
                )
                out[y + i] = total.astype(out.dtype)


def plane_terms(blocks, kernel):
    count = len(blocks)
    rows, part, depth = blocks[0].shape
    rows, outputs = rows - 2, kernel.shape[3]
    place = lax.axis_index("ch").astype(jnp.int32).reshape(1)
    vmem = pl.BlockSpec(memory_space=pltpu.VMEM)
    return pl.pallas_call(
        functools.partial(taps_kernel, count),
        out_shape=[
            jax.ShapeDtypeStruct((rows, outputs, depth), dtype)
            for dtype in (jnp.bfloat16, jnp.float32, jnp.bfloat16)
        ],
        in_specs=[pl.BlockSpec(memory_space=pltpu.SMEM)] + [vmem] * (count + 1),
        out_specs=[vmem] * 3,
        scratch_shapes=[
            pltpu.VMEM((rows + 2, part * count, depth), jnp.bfloat16),
            pltpu.VMEM((9 * outputs, 3 * part * count), jnp.bfloat16),
        ],
        name="taps",
    )(place, kernel, *blocks)


def layer(field, kernel, bias):
    before = shifted(field[-1:], "gy", 1)
    after = shifted(field[:1], "gy", -1)
    padded = jnp.concatenate([before, field, after], axis=0)
    below, center, above = plane_terms(gathered(padded, "ch"), kernel)
    total = center + shifted(above, "gx", 1).astype(jnp.float32) + shifted(below, "gx", -1).astype(jnp.float32)
    return jnp.maximum(total + bias.reshape(1, -1, 1), 0.0).astype(jnp.bfloat16)


def per_device(density, first_kernel, first_bias, second_kernel, second_bias):
    hidden = layer(density[0], first_kernel, first_bias)
    return layer(hidden, second_kernel, second_bias)[None]


def solution(mesh):
    placed = (
        P("gx", "gy", "ch", None),
        P(None, None, None, "ch", None),
        P("ch"),
        P(None, None, None, "ch", None),
        P("ch"),
    )
    return jax.shard_map(
        per_device, mesh=mesh, in_specs=placed, out_specs=P("gx", "gy", "ch", None), check_vma=False
    )
```

time: 127 us -> 76.6 us (0.60); the launches traced: 125 us -> 76.2 us
  local copies, waits for them, and re-layouts: 39.1 us -> 2.73 us
  blocking collectives: 28 us -> 0 us
  waiting for transfers between devices: 13 us -> 37.6 us
  matrix products: 8.49 us -> 0 us
  Pallas kernels: 0 us -> 5.85 us
  other arithmetic: 9.15 us -> 3.69 us
    all_gather x2 -> x0, blocking collectives: 28 us -> none  [layer_channels(): whole = lax.all_gather(field, 'ch', axis=2, tiled=True)]
    ppermute x8 -> x14, waiting for transfers between devices: 13 us -> 37.6 us  [the longest x6 22.8 us: gathered(): lax.ppermute(block, axis, [(i, (i + step) % count) for i in range(count)])]
    ppermute x6 -> x0, local copies, waits for them, and re-layouts: 9.81 us -> none  [the longest x3 4.91 us: with_halo(): lax.ppermute(lax.slice_in_dim(block, block.shape[dim] - width, None, axis...]
    conv_general_dilated x2 -> x0, matrix products: 8.49 us -> none  [conv_taps(): lax.conv_general_dilated(padded[None], kernel, (1, 1, 1), 'VALID', dimens...]
    conv_general_dilated x10 -> x0, local copies, waits for them, and re-layouts: 7.88 us -> none  [conv_taps(): lax.conv_general_dilated(padded[None], kernel, (1, 1, 1), 'VALID', dimens...]
    concatenate x2 -> x0, local copies, waits for them, and re-layouts: 6.33 us -> none  [with_halo(): block = jnp.concatenate([low, block, high], axis=dim)]
    pallas_call x0 -> x2, Pallas kernels: none -> 5.85 us  [plane_terms(): pl.pallas_call(functools.partial(taps_kernel, count), out_shape=[jax.Shap...]
    slice x4 -> x2, local copies, waits for them, and re-layouts: 5.99 us -> 0.73 us  [layer(): before = shifted(field[-1:], 'gy', 1)]
  transfers between devices with their start and end apart: 8 -> 14, of which waited for: 3 -> 9; matrix products, arithmetic and copies ran while one was open for 9% -> 0% of each run, Pallas kernels for 0% -> 0%
where the time goes in v1:
time: 76.6 us; the launch traced here: 76.2 us
  waiting for transfers between devices  37.6 us (49%)
  starting transfers between devices  26.1 us (34%)
  Pallas kernels  5.85 us (8%)
  other arithmetic  3.69 us (5%)
  local copies, waits for them, and re-layouts  2.73 us (4%)
    ppermute x6, waiting for transfers between devices, gathered(): lax.ppermute(block, axis, [(i, (i + step) % count) for i in range(count)])  22.8 us
    ppermute x8, starting transfers between devices, shifted(): return lax.ppermute(block, axis, pairs)  19 us
    ppermute x8, waiting for transfers between devices, shifted(): return lax.ppermute(block, axis, pairs)  14.8 us
    ppermute x6, starting transfers between devices, gathered(): lax.ppermute(block, axis, [(i, (i + step) % count) for i in range(count)])  7.13 us
    pallas_call x2, Pallas kernels, plane_terms(): pl.pallas_call(functools.partial(taps_kernel, count), out_shape=[jax.Shap...  5.85 us
    unnamed x20, local copies, waits for them, and re-layouts  2.01 us
    broadcast_in_dim x1, other arithmetic, per_device(): return layer(hidden, second_kernel, second_bias)[None]  1.7 us
  transfers between devices with their start and end apart: 14, of which 9 were waited for; matrix products, arithmetic and copies ran while one was open for 0% of the time, Pallas kernels for 0%

profile of v1, /device:TPU:1, one launch (start us, length us, event | category | flops | bytes accessed | tf_op | source)
XLA Modules:
  0.0 76.2 jit_solution(918591581025245658)
XLA Ops:
  0.0 0.7 slice_bitcast_fusion.1
  0.7 3.9 %collective-permute-start = (bf16[1,32,128]{2,1,0:T(8,128)(2,1)S(1)}, bf16[1,32,128]{2,1,0:T(8,128)(2,1)S(1)}, u32[]{:S(2)}, u32[]{:S(2)}) collective-permute-start(bf16[1,32,128]{2,1,0:T(8,128)(2,1)S(1)} %get-tuple-element.19), channel_id=1, source_target_pairs={{0,4},{1,5},{2,6},{3,7},{8,12},{9,13},{10,14},{11,15},{16,20},{17,... | collective-permute-start | bytes 24584 | tf_op jit(solution)/shard_map/ppermute | solution.py:14
  4.7 1.3 %collective-permute-start.1 = (bf16[1,32,128]{2,1,0:T(8,128)(2,1)S(1)}, bf16[1,32,128]{2,1,0:T(8,128)(2,1)S(1)}, u32[]{:S(2)}, u32[]{:S(2)}) collective-permute-start(bf16[1,32,128]{2,1,0:T(8,128)(2,1)S(1)} %get-tuple-element.20), channel_id=1, source_target_pairs={{4,0},{5,1},{6,2},{7,3},{12,8},{13,9},{14,10},{15,11},{20,16},{21,... | collective-permute-start | bytes 24584 | tf_op jit(solution)/shard_map/ppermute | solution.py:14
  6.0 0.0 collective-permute-done
  6.0 3.1 %collective-permute-done.1 = bf16[1,32,128]{2,1,0:T(8,128)(2,1)S(1)} collective-permute-done((bf16[1,32,128]{2,1,0:T(8,128)(2,1)S(1)}, bf16[1,32,128]{2,1,0:T(8,128)(2,1)S(1)}, u32[]{:S(2)}, u32[]{:S(2)}) %collective-permute-start.1) | collective-permute-done | bytes 8224 | tf_op jit(solution)/shard_map/ppermute | solution.py:14
  9.1 0.9 %pad_maximum_fusion.refs_0_ = bf16[18,32,128]{2,1,0:T(8,128)(2,1)S(1)} fusion(bf16[1,32,128]{2,1,0:T(8,128)(2,1)S(1)} %collective-permute-done.1, bf16[16,32,128]{2,1,0:T(8,128)(2,1)} %bitcast.8, bf16[1,32,128]{2,1,0:T(8,128)(2,1)S(1)} %collective-permute-done), kind=kLoop, calls=%fused_computation.2 | loop fusion | flops 147456 | bytes 294912 | tf_op jit(solution)/shard_map/concatenate | solution.py:85
  10.0 0.0 copy-start
  10.0 3.4 %collective-permute-start.4 = (bf16[18,32,128]{2,1,0:T(8,128)(2,1)S(1)}, bf16[18,32,128]{2,1,0:T(8,128)(2,1)S(1)}, u32[]{:S(2)}, u32[]{:S(2)}) collective-permute-start(bf16[18,32,128]{2,1,0:T(8,128)(2,1)S(1)} %pad_maximum_fusion.refs_0_), channel_id=1, source_target_pairs={{0,3},{1,0},{2,1},{3,2},{4,7},{5,4},{6,5},{7,6},{8,11},{9,8},{10,9... | collective-permute-start | bytes 442376 | tf_op jit(solution)/shard_map/ppermute | solution.py:20
  13.4 0.0 collective-permute-start.3
  13.4 0.5 collective-permute-start.2
  13.8 1.7 %collective-permute-done.4.refs_3_ = bf16[18,32,128]{2,1,0:T(8,128)(2,1)S(1)} collective-permute-done((bf16[18,32,128]{2,1,0:T(8,128)(2,1)S(1)}, bf16[18,32,128]{2,1,0:T(8,128)(2,1)S(1)}, u32[]{:S(2)}, u32[]{:S(2)}) %collective-permute-start.4) | collective-permute-done | bytes 147488 | tf_op jit(solution)/shard_map/ppermute | solution.py:20
  15.5 10.4 %collective-permute-done.3.refs_2_ = bf16[18,32,128]{2,1,0:T(8,128)(2,1)S(1)} collective-permute-done((bf16[18,32,128]{2,1,0:T(8,128)(2,1)S(1)}, bf16[18,32,128]{2,1,0:T(8,128)(2,1)S(1)}, u32[]{:S(2)}, u32[]{:S(2)}) %collective-permute-start.3) | collective-permute-done | bytes 147488 | tf_op jit(solution)/shard_map/ppermute | solution.py:20
  25.9 0.0 collective-permute-done.2.refs_1_
  26.0 0.0 copy-done
  26.0 0.0 copy-done.2
  26.0 0.6 copy-done.3
  26.6 0.0 copy-done.5
  26.6 2.9 %taps.2 = (bf16[16,32,128]{2,1,0:T(8,128)(2,1)}, f32[16,32,128]{2,1,0:T(8,128)}, bf16[16,32,128]{2,1,0:T(8,128)(2,1)}) custom-call(s32[1]{0:T(128)} %bitcast.place_ref, bf16[3,3,3,32,128]{4,3,2,1,0:T(8,128)(2,1)} %kernel_ref.2, bf16[18,32,128]{2,1,0:T(8,128)(2,1)} %copy-done, bf16[18,32,128]{2,1,0:T(8,128)(2,1)} %copy-done.5, ...), custom_call_target="tpu_custom_call" | custom-call | tf_op jit(solution)/shard_map/taps/pallas_call | solution.py:66
  29.6 4.9 %collective-permute-start.5 = (bf16[16,32,128]{2,1,0:T(8,128)(2,1)}, bf16[16,32,128]{2,1,0:T(8,128)(2,1)S(1)}, u32[]{:S(2)}, u32[]{:S(2)}) collective-permute-start(bf16[16,32,128]{2,1,0:T(8,128)(2,1)} %get-tuple-element.12), channel_id=1, source_target_pairs={{0,8},{8,16},{16,24},{1,9},{9,17},{17,25},{2,10},{10,18},{18,26},{... | collective-permute-start | bytes 393224 | tf_op jit(solution)/shard_map/ppermute | solution.py:14
  34.5 0.0 copy-start.8
  34.5 1.9 %collective-permute-start.6 = (bf16[16,32,128]{2,1,0:T(8,128)(2,1)}, bf16[16,32,128]{2,1,0:T(8,128)(2,1)S(1)}, u32[]{:S(2)}, u32[]{:S(2)}) collective-permute-start(bf16[16,32,128]{2,1,0:T(8,128)(2,1)} %get-tuple-element.13), channel_id=1, source_target_pairs={{8,0},{16,8},{24,16},{9,1},{17,9},{25,17},{10,2},{18,10},{26,18},{... | collective-permute-start | bytes 393224 | tf_op jit(solution)/shard_map/ppermute | solution.py:14
  36.4 0.3 collective-permute-done.5
  36.7 4.3 %collective-permute-done.6 = bf16[16,32,128]{2,1,0:T(8,128)(2,1)S(1)} collective-permute-done((bf16[16,32,128]{2,1,0:T(8,128)(2,1)}, bf16[16,32,128]{2,1,0:T(8,128)(2,1)S(1)}, u32[]{:S(2)}, u32[]{:S(2)}) %collective-permute-start.6) | collective-permute-done | bytes 131104 | tf_op jit(solution)/shard_map/ppermute | solution.py:14
  41.0 0.0 copy-done.8
  41.0 1.0 %maximum_convert_fusion.1 = bf16[16,32,128]{2,1,0:T(8,128)(2,1)S(1)} fusion(bf16[16,32,128]{2,1,0:T(8,128)(2,1)S(1)} %collective-permute-done.6, f32[16,32,128]{2,1,0:T(8,128)} %get-tuple-element.11, bf16[16,32,128]{2,1,0:T(8,128)(2,1)S(1)} %collective-permute-done.5, f32[32]{0:T(128)S(1)} %copy-done.8), kind=kLoop, calls=%fused_computation.1 | loop fusion | flops 458752 | bytes 655488 | tf_op jit(solution)/shard_map/convert_element_type | solution.py:88
  42.0 1.4 %collective-permute-start.7 = (bf16[1,32,128]{2,1,0:T(8,128)(2,1)S(1)}, bf16[1,32,128]{2,1,0:T(8,128)(2,1)S(1)}, u32[]{:S(2)}, u32[]{:S(2)}) collective-permute-start(bf16[1,32,128]{2,1,0:T(8,128)(2,1)S(1)} %get-tuple-element.17), channel_id=1, source_target_pairs={{0,4},{1,5},{2,6},{3,7},{8,12},{9,13},{10,14},{11,15},{16,20},{17,... | collective-permute-start | bytes 24584 | tf_op jit(solution)/shard_map/ppermute | solution.py:14
  43.4 1.3 %collective-permute-start.8 = (bf16[1,32,128]{2,1,0:T(8,128)(2,1)S(1)}, bf16[1,32,128]{2,1,0:T(8,128)(2,1)S(1)}, u32[]{:S(2)}, u32[]{:S(2)}) collective-permute-start(bf16[1,32,128]{2,1,0:T(8,128)(2,1)S(1)} %get-tuple-element.18), channel_id=1, source_target_pairs={{4,0},{5,1},{6,2},{7,3},{12,8},{13,9},{14,10},{15,11},{20,16},{21,... | collective-permute-start | bytes 24584 | tf_op jit(solution)/shard_map/ppermute | solution.py:14
  44.7 0.0 collective-permute-done.7
  44.7 3.1 %collective-permute-done.8 = bf16[1,32,128]{2,1,0:T(8,128)(2,1)S(1)} collective-permute-done((bf16[1,32,128]{2,1,0:T(8,128)(2,1)S(1)}, bf16[1,32,128]{2,1,0:T(8,128)(2,1)S(1)}, u32[]{:S(2)}, u32[]{:S(2)}) %collective-permute-start.8) | collective-permute-done | bytes 8224 | tf_op jit(solution)/shard_map/ppermute | solution.py:14
  47.8 0.0 copy-start.1
  47.8 0.5 collective-permute-start.11
  48.3 1.4 %collective-permute-start.10 = (bf16[18,32,128]{2,1,0:T(8,128)(2,1)S(1)}, bf16[18,32,128]{2,1,0:T(8,128)(2,1)S(1)}, u32[]{:S(2)}, u32[]{:S(2)}) collective-permute-start(bf16[18,32,128]{2,1,0:T(8,128)(2,1)S(1)} %pad_maximum_fusion.1.refs_0_), channel_id=1, source_target_pairs={{0,2},{1,3},{2,0},{3,1},{4,6},{5,7},{6,4},{7,5},{8,10},{9,11},{10,... | collective-permute-start | bytes 442376 | tf_op jit(solution)/shard_map/ppermute | solution.py:20
  49.7 1.4 %collective-permute-start.9 = (bf16[18,32,128]{2,1,0:T(8,128)(2,1)S(1)}, bf16[18,32,128]{2,1,0:T(8,128)(2,1)S(1)}, u32[]{:S(2)}, u32[]{:S(2)}) collective-permute-start(bf16[18,32,128]{2,1,0:T(8,128)(2,1)S(1)} %pad_maximum_fusion.1.refs_0_), channel_id=1, source_target_pairs={{0,1},{1,2},{2,3},{3,0},{4,5},{5,6},{6,7},{7,4},{8,9},{9,10},{10,1... | collective-permute-start | bytes 442376 | tf_op jit(solution)/shard_map/ppermute | solution.py:20
  51.1 2.5 %collective-permute-done.11.refs_3_ = bf16[18,32,128]{2,1,0:T(8,128)(2,1)S(1)} collective-permute-done((bf16[18,32,128]{2,1,0:T(8,128)(2,1)S(1)}, bf16[18,32,128]{2,1,0:T(8,128)(2,1)S(1)}, u32[]{:S(2)}, u32[]{:S(2)}) %collective-permute-start.11) | collective-permute-done | bytes 147488 | tf_op jit(solution)/shard_map/ppermute | solution.py:20
  53.7 8.2 %collective-permute-done.10.refs_2_ = bf16[18,32,128]{2,1,0:T(8,128)(2,1)S(1)} collective-permute-done((bf16[18,32,128]{2,1,0:T(8,128)(2,1)S(1)}, bf16[18,32,128]{2,1,0:T(8,128)(2,1)S(1)}, u32[]{:S(2)}, u32[]{:S(2)}) %collective-permute-start.10) | collective-permute-done | bytes 147488 | tf_op jit(solution)/shard_map/ppermute | solution.py:20
  61.8 0.0 collective-permute-done.9.refs_1_
  61.8 0.0 copy-done.1
  61.8 0.0 copy-done.4
  61.9 0.6 copy-done.6
  62.5 0.7 copy-done.7
  63.2 2.9 %taps.3 = (bf16[16,32,128]{2,1,0:T(8,128)(2,1)}, f32[16,32,128]{2,1,0:T(8,128)}, bf16[16,32,128]{2,1,0:T(8,128)(2,1)}) custom-call(s32[1]{0:T(128)} %bitcast.place_ref, bf16[3,3,3,32,128]{4,3,2,1,0:T(8,128)(2,1)} %kernel_ref.3, bf16[18,32,128]{2,1,0:T(8,128)(2,1)} %copy-done.1, bf16[18,32,128]{2,1,0:T(8,128)(2,1)} %copy-done.7, ...), custom_call_target="tpu_custom_call" | custom-call | tf_op jit(solution)/shard_map/taps/pallas_call | solution.py:66
  66.1 1.9 %collective-permute-start.12 = (bf16[16,32,128]{2,1,0:T(8,128)(2,1)}, bf16[16,32,128]{2,1,0:T(8,128)(2,1)S(1)}, u32[]{:S(2)}, u32[]{:S(2)}) collective-permute-start(bf16[16,32,128]{2,1,0:T(8,128)(2,1)} %get-tuple-element.15), channel_id=1, source_target_pairs={{0,8},{8,16},{16,24},{1,9},{9,17},{17,25},{2,10},{10,18},{18,26},{... | collective-permute-start | bytes 393224 | tf_op jit(solution)/shard_map/ppermute | solution.py:14
  68.0 0.0 copy-start.9
  68.0 2.4 %collective-permute-start.13 = (bf16[16,32,128]{2,1,0:T(8,128)(2,1)}, bf16[16,32,128]{2,1,0:T(8,128)(2,1)S(1)}, u32[]{:S(2)}, u32[]{:S(2)}) collective-permute-start(bf16[16,32,128]{2,1,0:T(8,128)(2,1)} %get-tuple-element.16), channel_id=1, source_target_pairs={{8,0},{16,8},{24,16},{9,1},{17,9},{25,17},{10,2},{18,10},{26,18},{... | collective-permute-start | bytes 393224 | tf_op jit(solution)/shard_map/ppermute | solution.py:14
  70.4 0.0 collective-permute-done.12
  70.4 4.1 %collective-permute-done.13 = bf16[16,32,128]{2,1,0:T(8,128)(2,1)S(1)} collective-permute-done((bf16[16,32,128]{2,1,0:T(8,128)(2,1)}, bf16[16,32,128]{2,1,0:T(8,128)(2,1)S(1)}, u32[]{:S(2)}, u32[]{:S(2)}) %collective-permute-start.13) | collective-permute-done | bytes 131104 | tf_op jit(solution)/shard_map/ppermute | solution.py:14
  74.5 0.0 copy-done.9
  74.5 1.7 %fusion = bf16[1,16,32,128]{3,2,1,0:T(8,128)(2,1)} fusion(bf16[16,32,128]{2,1,0:T(8,128)(2,1)S(1)} %collective-permute-done.13, f32[16,32,128]{2,1,0:T(8,128)} %get-tuple-element.14, bf16[16,32,128]{2,1,0:T(8,128)(2,1)S(1)} %collective-permute-done.12, f32[32]{0:T(128)S(1)} %copy-done.9), kind=kLoop, calls=%fused_computation.4 | loop fusion | flops 458752 | bytes 655488 | tf_op jit(solution)/shard_map/broadcast_in_dim | solution.py:93
  (8 shorter events, 0.0 us)
Async XLA Ops:
  0.7 5.2 %collective-permute-start = (bf16[1,32,128]{2,1,0:T(8,128)(2,1)S(1)}, bf16[1,32,128]{2,1,0:T(8,128)(2,1)S(1)}, u32[]{:S(2)}, u32[]{:S(2)}) collective-permute-start(bf16[1,32,128]{2,1,0:T(8,128)(2,1)S(1)} %get-tuple-element.19), channel_id=1, source_target_pairs={{0,4},{1,5},{2,6},{3,7},{8,12},{9,13},{10,14},{11,15},{16,20},{17,... | collective-permute-start | bytes 24584 | tf_op jit(solution)/shard_map/ppermute | solution.py:14
  4.7 4.4 %collective-permute-start.1 = (bf16[1,32,128]{2,1,0:T(8,128)(2,1)S(1)}, bf16[1,32,128]{2,1,0:T(8,128)(2,1)S(1)}, u32[]{:S(2)}, u32[]{:S(2)}) collective-permute-start(bf16[1,32,128]{2,1,0:T(8,128)(2,1)S(1)} %get-tuple-element.20), channel_id=1, source_target_pairs={{4,0},{5,1},{6,2},{7,3},{12,8},{13,9},{14,10},{15,11},{20,16},{21,... | collective-permute-start | bytes 24584 | tf_op jit(solution)/shard_map/ppermute | solution.py:14
  10.0 16.0 %copy-start = (bf16[18,32,128]{2,1,0:T(8,128)(2,1)}, bf16[18,32,128]{2,1,0:T(8,128)(2,1)S(1)}, u32[]{:S(2)}) copy-start(bf16[18,32,128]{2,1,0:T(8,128)(2,1)S(1)} %pad_maximum_fusion.refs_0_) | copy-start | bytes 442372
  10.0 5.5 %collective-permute-start.4 = (bf16[18,32,128]{2,1,0:T(8,128)(2,1)S(1)}, bf16[18,32,128]{2,1,0:T(8,128)(2,1)S(1)}, u32[]{:S(2)}, u32[]{:S(2)}) collective-permute-start(bf16[18,32,128]{2,1,0:T(8,128)(2,1)S(1)} %pad_maximum_fusion.refs_0_), channel_id=1, source_target_pairs={{0,3},{1,0},{2,1},{3,2},{4,7},{5,4},{6,5},{7,6},{8,11},{9,8},{10,9... | collective-permute-start | bytes 442376 | tf_op jit(solution)/shard_map/ppermute | solution.py:20
  13.4 12.6 %collective-permute-start.3 = (bf16[18,32,128]{2,1,0:T(8,128)(2,1)S(1)}, bf16[18,32,128]{2,1,0:T(8,128)(2,1)S(1)}, u32[]{:S(2)}, u32[]{:S(2)}) collective-permute-start(bf16[18,32,128]{2,1,0:T(8,128)(2,1)S(1)} %pad_maximum_fusion.refs_0_), channel_id=1, source_target_pairs={{0,2},{1,3},{2,0},{3,1},{4,6},{5,7},{6,4},{7,5},{8,10},{9,11},{10,... | collective-permute-start | bytes 442376 | tf_op jit(solution)/shard_map/ppermute | solution.py:20
  13.4 12.6 %collective-permute-start.2 = (bf16[18,32,128]{2,1,0:T(8,128)(2,1)S(1)}, bf16[18,32,128]{2,1,0:T(8,128)(2,1)S(1)}, u32[]{:S(2)}, u32[]{:S(2)}) collective-permute-start(bf16[18,32,128]{2,1,0:T(8,128)(2,1)S(1)} %pad_maximum_fusion.refs_0_), channel_id=1, source_target_pairs={{0,1},{1,2},{2,3},{3,0},{4,5},{5,6},{6,7},{7,4},{8,9},{9,10},{10,1... | collective-permute-start | bytes 442376 | tf_op jit(solution)/shard_map/ppermute | solution.py:20
  15.5 10.5 %copy-start.2 = (bf16[18,32,128]{2,1,0:T(8,128)(2,1)}, bf16[18,32,128]{2,1,0:T(8,128)(2,1)S(1)}, u32[]{:S(2)}) copy-start(bf16[18,32,128]{2,1,0:T(8,128)(2,1)S(1)} %collective-permute-done.4.refs_3_) | copy-start | bytes 442372
  25.9 0.7 copy-start.3
  25.9 0.7 copy-start.5
  29.6 7.1 %collective-permute-start.5 = (bf16[16,32,128]{2,1,0:T(8,128)(2,1)}, bf16[16,32,128]{2,1,0:T(8,128)(2,1)S(1)}, u32[]{:S(2)}, u32[]{:S(2)}) collective-permute-start(bf16[16,32,128]{2,1,0:T(8,128)(2,1)} %get-tuple-element.12), channel_id=1, source_target_pairs={{0,8},{8,16},{16,24},{1,9},{9,17},{17,25},{2,10},{10,18},{18,26},{... | collective-permute-start | bytes 393224 | tf_op jit(solution)/shard_map/ppermute | solution.py:14
  34.5 6.5 %copy-start.8 = (f32[32]{0:T(128)S(1)}, f32[32]{0:T(128)}, u32[]{:S(2)}) copy-start(f32[32]{0:T(128)} %param.7) | copy-start | bytes 388
  34.5 6.5 %collective-permute-start.6 = (bf16[16,32,128]{2,1,0:T(8,128)(2,1)}, bf16[16,32,128]{2,1,0:T(8,128)(2,1)S(1)}, u32[]{:S(2)}, u32[]{:S(2)}) collective-permute-start(bf16[16,32,128]{2,1,0:T(8,128)(2,1)} %get-tuple-element.13), channel_id=1, source_target_pairs={{8,0},{16,8},{24,16},{9,1},{17,9},{25,17},{10,2},{18,10},{26,18},{... | collective-permute-start | bytes 393224 | tf_op jit(solution)/shard_map/ppermute | solution.py:14
  42.0 2.7 %collective-permute-start.7 = (bf16[1,32,128]{2,1,0:T(8,128)(2,1)S(1)}, bf16[1,32,128]{2,1,0:T(8,128)(2,1)S(1)}, u32[]{:S(2)}, u32[]{:S(2)}) collective-permute-start(bf16[1,32,128]{2,1,0:T(8,128)(2,1)S(1)} %get-tuple-element.17), channel_id=1, source_target_pairs={{0,4},{1,5},{2,6},{3,7},{8,12},{9,13},{10,14},{11,15},{16,20},{17,... | collective-permute-start | bytes 24584 | tf_op jit(solution)/shard_map/ppermute | solution.py:14
  43.4 4.4 %collective-permute-start.8 = (bf16[1,32,128]{2,1,0:T(8,128)(2,1)S(1)}, bf16[1,32,128]{2,1,0:T(8,128)(2,1)S(1)}, u32[]{:S(2)}, u32[]{:S(2)}) collective-permute-start(bf16[1,32,128]{2,1,0:T(8,128)(2,1)S(1)} %get-tuple-element.18), channel_id=1, source_target_pairs={{4,0},{5,1},{6,2},{7,3},{12,8},{13,9},{14,10},{15,11},{20,16},{21,... | collective-permute-start | bytes 24584 | tf_op jit(solution)/shard_map/ppermute | solution.py:14
  47.8 14.0 %copy-start.1 = (bf16[18,32,128]{2,1,0:T(8,128)(2,1)}, bf16[18,32,128]{2,1,0:T(8,128)(2,1)S(1)}, u32[]{:S(2)}) copy-start(bf16[18,32,128]{2,1,0:T(8,128)(2,1)S(1)} %pad_maximum_fusion.1.refs_0_) | copy-start | bytes 442372
  47.8 5.8 %collective-permute-start.11 = (bf16[18,32,128]{2,1,0:T(8,128)(2,1)S(1)}, bf16[18,32,128]{2,1,0:T(8,128)(2,1)S(1)}, u32[]{:S(2)}, u32[]{:S(2)}) collective-permute-start(bf16[18,32,128]{2,1,0:T(8,128)(2,1)S(1)} %pad_maximum_fusion.1.refs_0_), channel_id=1, source_target_pairs={{0,3},{1,0},{2,1},{3,2},{4,7},{5,4},{6,5},{7,6},{8,11},{9,8},{10,9... | collective-permute-start | bytes 442376 | tf_op jit(solution)/shard_map/ppermute | solution.py:20
  48.3 13.5 %collective-permute-start.10 = (bf16[18,32,128]{2,1,0:T(8,128)(2,1)S(1)}, bf16[18,32,128]{2,1,0:T(8,128)(2,1)S(1)}, u32[]{:S(2)}, u32[]{:S(2)}) collective-permute-start(bf16[18,32,128]{2,1,0:T(8,128)(2,1)S(1)} %pad_maximum_fusion.1.refs_0_), channel_id=1, source_target_pairs={{0,2},{1,3},{2,0},{3,1},{4,6},{5,7},{6,4},{7,5},{8,10},{9,11},{10,... | collective-permute-start | bytes 442376 | tf_op jit(solution)/shard_map/ppermute | solution.py:20
  49.7 12.1 %collective-permute-start.9 = (bf16[18,32,128]{2,1,0:T(8,128)(2,1)S(1)}, bf16[18,32,128]{2,1,0:T(8,128)(2,1)S(1)}, u32[]{:S(2)}, u32[]{:S(2)}) collective-permute-start(bf16[18,32,128]{2,1,0:T(8,128)(2,1)S(1)} %pad_maximum_fusion.1.refs_0_), channel_id=1, source_target_pairs={{0,1},{1,2},{2,3},{3,0},{4,5},{5,6},{6,7},{7,4},{8,9},{9,10},{10,1... | collective-permute-start | bytes 442376 | tf_op jit(solution)/shard_map/ppermute | solution.py:20
  53.7 8.2 %copy-start.4 = (bf16[18,32,128]{2,1,0:T(8,128)(2,1)}, bf16[18,32,128]{2,1,0:T(8,128)(2,1)S(1)}, u32[]{:S(2)}) copy-start(bf16[18,32,128]{2,1,0:T(8,128)(2,1)S(1)} %collective-permute-done.11.refs_3_) | copy-start | bytes 442372
  61.8 0.7 copy-start.6
  62.5 0.7 copy-start.7
  66.1 4.3 %collective-permute-start.12 = (bf16[16,32,128]{2,1,0:T(8,128)(2,1)}, bf16[16,32,128]{2,1,0:T(8,128)(2,1)S(1)}, u32[]{:S(2)}, u32[]{:S(2)}) collective-permute-start(bf16[16,32,128]{2,1,0:T(8,128)(2,1)} %get-tuple-element.15), channel_id=1, source_target_pairs={{0,8},{8,16},{16,24},{1,9},{9,17},{17,25},{2,10},{10,18},{18,26},{... | collective-permute-start | bytes 393224 | tf_op jit(solution)/shard_map/ppermute | solution.py:14
  68.0 6.5 %copy-start.9 = (f32[32]{0:T(128)S(1)}, f32[32]{0:T(128)}, u32[]{:S(2)}) copy-start(f32[32]{0:T(128)} %param.9) | copy-start | bytes 388
  68.0 6.5 %collective-permute-start.13 = (bf16[16,32,128]{2,1,0:T(8,128)(2,1)}, bf16[16,32,128]{2,1,0:T(8,128)(2,1)S(1)}, u32[]{:S(2)}, u32[]{:S(2)}) collective-permute-start(bf16[16,32,128]{2,1,0:T(8,128)(2,1)} %get-tuple-element.16), channel_id=1, source_target_pairs={{8,0},{16,8},{24,16},{9,1},{17,9},{25,17},{10,2},{18,10},{26,18},{... | collective-permute-start | bytes 393224 | tf_op jit(solution)/shard_map/ppermute | solution.py:14

commit v2 on v1

v2 whole, which is shorter than its diff:
```python
import functools

import jax
import jax.numpy as jnp
from jax import lax
from jax.experimental import pallas as pl
from jax.experimental.pallas import tpu as pltpu
from jax.sharding import PartitionSpec as P

VMEM_BYTES = 12 << 20


def on_chip(array):
    return pltpu.with_memory_space_constraint(array, pltpu.VMEM)


def call(kernel, name, out_shape, scratch, *operands):
    vmem = pl.BlockSpec(memory_space=pltpu.VMEM)
    return pl.pallas_call(
        kernel,
        out_shape=out_shape,
        in_specs=[vmem] * len(operands),
        out_specs=jax.tree.map(lambda _: vmem, out_shape),
        scratch_shapes=scratch,
        compiler_params=pltpu.CompilerParams(vmem_limit_bytes=VMEM_BYTES),
        name=name,
    )(*operands)


def partners(count):
    return [[(i, i ^ step) for i in range(count)] for step in range(count)]


def channel_swaps(block):
    steps = partners(lax.axis_size("ch"))
    return [block] + [lax.ppermute(block, "ch", pairs) for pairs in steps[1:]]


def edge_moves(edge, rows_step):
    rows, channels = lax.axis_size("gy"), lax.axis_size("ch")
    moved = []
    for pairs in partners(channels):
        if rows == 2:
            along = [(0, 1), (1, 0)]
        else:
            along = [(i, i + rows_step) for i in range(rows) if 0 <= i + rows_step < rows]
        both = [(i * channels + c, j * channels + d) for i, j in along for c, d in pairs]
        moved.append(lax.ppermute(edge, ("gy", "ch"), both))
    return moved


def taps_kernel(count, kernel_ref, *refs):
    blocks, refs = refs[:count], refs[count:]
    edges, (near_ref, center_ref, far_ref, volume, weights) = refs[:-5], refs[-5:]
    befores, afters = edges[:count], edges[-count:]
    rows, outputs, depth = center_ref.shape
    part = blocks[0].shape[1]
    inputs = part * count
    place = lax.axis_index("ch")
    gy, gx = lax.axis_index("gy"), lax.axis_index("gx")
    has_before = jnp.full((1, part, depth), gy > 0)
    has_after = jnp.full((1, part, depth), gy < lax.axis_size("gy") - 1)
    for step in range(count):
        source = jnp.bitwise_xor(place, step)
        here = pl.ds(pl.multiple_of(source * part, part), part)
        volume[1 : rows + 1, here, :] = blocks[step][...]
        volume[0:1, here, :] = jnp.where(has_before, befores[step][...], 0.0)
        volume[rows + 1 : rows + 2, here, :] = jnp.where(has_after, afters[step][...], 0.0)
    even = gx % 2 == 0
    near = jnp.where(even, 0, 2)
    outer = jnp.full((outputs, inputs), (gx == 0) | (gx == lax.axis_size("gx") - 1))
    for slot, a in enumerate((near, 1, 2 - near)):
        for b in range(3):
            for c in range(3):
                first = (slot * 3 + c) * outputs
                tap = kernel_ref[a, b, c]
                if slot == 2:
                    tap = jnp.where(outer, 0.0, tap)
                weights[first : first + outputs, b * inputs : (b + 1) * inputs] = tap
    lane = lax.broadcasted_iota(jnp.int32, (outputs, depth), 1)
    taps = weights[...]
    for y in range(0, rows, 2):
        window = jnp.concatenate(
            [volume[y + i : y + i + 3].reshape(3 * inputs, depth) for i in range(2)], axis=1
        )
        product = jnp.dot(taps, window, preferred_element_type=jnp.float32)
        for i in range(2):
            for slot, out in enumerate((near_ref, center_ref, far_ref)):
                first, middle, last = (
                    product[(slot * 3 + c) * outputs : (slot * 3 + c + 1) * outputs, i * depth : (i + 1) * depth]
                    for c in range(3)
                )
                total = (
                    middle
                    + jnp.where(lane == 0, 0.0, pltpu.roll(first, 1, 1))
                    + jnp.where(lane == depth - 1, 0.0, pltpu.roll(last, depth - 1, 1))
                )
                out[y + i] = total.astype(out.dtype)


def finish_kernel(near_ref, center_ref, far_ref, bias_ref, out_ref, *edge_refs):
    total = center_ref[...] + near_ref[...].astype(jnp.float32) + far_ref[...].astype(jnp.float32)
    out_ref[...] = jnp.maximum(total + bias_ref[...][None], 0.0).astype(out_ref.dtype)
    rows = out_ref.shape[0]
    if len(edge_refs) == 1:
        edge_refs[0][0] = out_ref[jnp.where(lax.axis_index("gy") == 0, rows - 1, 0)]
    if len(edge_refs) == 2:
        edge_refs[0][0] = out_ref[rows - 1]
        edge_refs[1][0] = out_ref[0]


def layer(field, edges, kernel, bias, last):
    rows, part, depth = field.shape
    outputs = kernel.shape[3]
    count = lax.axis_size("ch")
    blocks = channel_swaps(field)
    halos = [moved for edge, step in zip(edges, (1, -1)) for moved in edge_moves(edge, step)]
    near, center, far = call(
        functools.partial(taps_kernel, count),
        "taps",
        [pltpu.VMEM((rows, outputs, depth), dtype) for dtype in (jnp.bfloat16, jnp.float32, jnp.bfloat16)],
        [
            pltpu.VMEM((rows + 2, part * count, depth), jnp.bfloat16),
            pltpu.VMEM((9 * outputs, 3 * part * count), jnp.bfloat16),
        ],
        on_chip(kernel),
        *[on_chip(block) for block in blocks],
        *[on_chip(halo) for halo in halos],
    )
    planes = lax.axis_size("gx")
    near = lax.ppermute(near, "gx", [(i, i ^ 1) for i in range(planes)])
    outer = [(0, 0), (planes - 1, planes - 1)]
    inner = [(i, i + 1) for i in range(1, planes - 1, 2)]
    far = lax.ppermute(far, "gx", outer + inner + [(j, i) for i, j in inner])
    if last:
        out_shape = [jax.ShapeDtypeStruct((rows, outputs, depth), jnp.bfloat16)]
    else:
        out_shape = [pltpu.VMEM((rows, outputs, depth), jnp.bfloat16)]
        out_shape += [pltpu.VMEM((1, outputs, depth), jnp.bfloat16)] * len(edges)
    return call(
        finish_kernel, "finish", out_shape, [], on_chip(near), on_chip(center), on_chip(far), on_chip(bias)
    )


def per_device(density, first_kernel, first_bias, second_kernel, second_bias):
    density = density[0]
    if lax.axis_size("gy") == 2:
        row = jnp.where(lax.axis_index("gy") == 0, density.shape[0] - 1, 0)
        edges = [lax.dynamic_slice_in_dim(density, row, 1, 0)]
    else:
        edges = [density[-1:], density[:1]]
    first_bias, second_bias = first_bias.reshape(-1, 1), second_bias.reshape(-1, 1)
    hidden, *edges = layer(density, edges, first_kernel, first_bias, False)
    return layer(hidden, edges, second_kernel, second_bias, True)[0][None]


def solution(mesh):
    placed = (
        P("gx", "gy", "ch", None),
        P(None, None, None, "ch", None),
        P("ch"),
        P(None, None, None, "ch", None),
        P("ch"),
    )
    return jax.shard_map(
        per_device, mesh=mesh, in_specs=placed, out_specs=P("gx", "gy", "ch", None), check_vma=False
    )
```

time: 76.6 us -> 53.3 us (0.70)
  waiting for transfers between devices: 37.6 us -> 15.9 us
  starting transfers between devices: 26.1 us -> 31.6 us
  other arithmetic: 3.69 us -> 0 us
  Pallas kernels: 5.85 us -> 2.71 us
    ppermute x14 -> x18, waiting for transfers between devices: 37.6 us -> 15.9 us  [the longest x8 9.78 us: edge_moves(): moved.append(lax.ppermute(edge, ('gy', 'ch'), both))]
    ppermute x14 -> x18, starting transfers between devices: 26.1 us -> 31.6 us  [the longest x8 13.7 us: edge_moves(): moved.append(lax.ppermute(edge, ('gy', 'ch'), both))]
    pallas_call x2 -> x4, Pallas kernels: 5.85 us -> 2.71 us  [call(): pl.pallas_call(kernel, out_shape=out_shape, in_specs=[vmem] * len(operand...]
    broadcast_in_dim x1 -> x0, other arithmetic: 1.7 us -> none  [per_device(): return layer(hidden, second_kernel, second_bias)[None]]
    convert_element_type x1 -> x0, other arithmetic: 1.05 us -> none  [layer(): return jnp.maximum(total + bias.reshape(1, -1, 1), 0.0).astype(jnp.bfloat16)]
    concatenate x2 -> x0, other arithmetic: 0.95 us -> none  [layer(): padded = jnp.concatenate([before, field, after], axis=0)]
    unnamed x20 -> x10, local copies, waits for them, and re-layouts: 2.01 us -> 1.85 us
  transfers between devices with their start and end apart: 14 -> 18, of which waited for: 9 -> 7; matrix products, arithmetic and copies ran while one was open for 0% -> 2% of each run, Pallas kernels for 0% -> 0%
where the time goes in v2:
time: 53.3 us; the launch traced here: 53.1 us
  starting transfers between devices  31.6 us (59%)
  waiting for transfers between devices  15.9 us (30%)
  local copies, waits for them, and re-layouts  2.79 us (5%)
  Pallas kernels  2.71 us (5%)
    ppermute x8, starting transfers between devices, edge_moves(): moved.append(lax.ppermute(edge, ('gy', 'ch'), both))  13.7 us
    ppermute x8, waiting for transfers between devices, edge_moves(): moved.append(lax.ppermute(edge, ('gy', 'ch'), both))  9.78 us
    ppermute x6, starting transfers between devices, channel_swaps(): return [block] + [lax.ppermute(block, 'ch', pairs) for pairs in steps[1:]]  7.65 us
    ppermute x2, starting transfers between devices, layer(): far = lax.ppermute(far, 'gx', outer + inner + [(j, i) for i, j in inner])  7.48 us
    ppermute x2, waiting for transfers between devices, layer(): far = lax.ppermute(far, 'gx', outer + inner + [(j, i) for i, j in inner])  6.07 us
    ppermute x2, starting transfers between devices, layer(): near = lax.ppermute(near, 'gx', [(i, i ^ 1) for i in range(planes)])  2.76 us
    pallas_call x4, Pallas kernels, call(): pl.pallas_call(kernel, out_shape=out_shape, in_specs=[vmem] * len(operand...  2.71 us
    unnamed x10, local copies, waits for them, and re-layouts  1.85 us
  transfers between devices with their start and end apart: 18, of which 7 were waited for; matrix products, arithmetic and copies ran while one was open for 2% of the time, Pallas kernels for 0%

profile of v2, /device:TPU:1, one launch (start us, length us, event | category | flops | bytes accessed | tf_op | source)
XLA Modules:
  0.0 53.1 jit_solution(6815960725312854771)
XLA Ops:
  0.0 2.1 %collective-permute-start = (bf16[16,32,128]{2,1,0:T(8,128)(2,1)}, bf16[16,32,128]{2,1,0:T(8,128)(2,1)S(1)}, u32[]{:S(2)}, u32[]{:S(2)}) collective-permute-start(bf16[16,32,128]{2,1,0:T(8,128)(2,1)} %bitcast.6), channel_id=1, source_target_pairs={{0,1},{1,0},{2,3},{3,2},{4,5},{5,4},{6,7},{7,6},{8,9},{9,8},{10,11... | collective-permute-start | bytes 393224 | tf_op jit(solution)/shard_map/ppermute | solution.py:36
  2.1 2.3 %collective-permute-start.1 = (bf16[16,32,128]{2,1,0:T(8,128)(2,1)}, bf16[16,32,128]{2,1,0:T(8,128)(2,1)S(1)}, u32[]{:S(2)}, u32[]{:S(2)}) collective-permute-start(bf16[16,32,128]{2,1,0:T(8,128)(2,1)} %bitcast.7), channel_id=1, source_target_pairs={{0,2},{1,3},{2,0},{3,1},{4,6},{5,7},{6,4},{7,5},{8,10},{9,11},{10,... | collective-permute-start | bytes 393224 | tf_op jit(solution)/shard_map/ppermute | solution.py:36
  4.4 0.0 collective-permute-start.2
  4.4 0.8 %dynamic-slice_bitcast_fusion = bf16[1,32,128]{2,1,0:T(8,128)(2,1)S(1)} fusion(bf16[1,16,32,128]{3,2,1,0:T(8,128)(2,1)} %param.5, s32[]{:T(128)S(6)} %select_n.5), kind=kLoop, calls=%fused_computation | loop fusion | bytes 16388 | tf_op jit(solution)/shard_map/dynamic_slice | solution.py:149
  5.2 1.2 %collective-permute-start.3 = (bf16[1,32,128]{2,1,0:T(8,128)(2,1)S(1)}, bf16[1,32,128]{2,1,0:T(8,128)(2,1)S(1)}, u32[]{:S(2)}, u32[]{:S(2)}) collective-permute-start(bf16[1,32,128]{2,1,0:T(8,128)(2,1)S(1)} %dynamic-slice_bitcast_fusion), channel_id=1, source_target_pairs={{0,4},{1,5},{2,6},{3,7},{4,0},{5,1},{6,2},{7,3},{8,12},{9,13},{10,... | collective-permute-start | bytes 24584 | tf_op jit(solution)/shard_map/ppermute | solution.py:48
  6.4 0.3 collective-permute-start.4
  6.7 1.3 %collective-permute-done.3.refs_4_ = bf16[1,32,128]{2,1,0:T(8,128)(2,1)S(1)} collective-permute-done((bf16[1,32,128]{2,1,0:T(8,128)(2,1)S(1)}, bf16[1,32,128]{2,1,0:T(8,128)(2,1)S(1)}, u32[]{:S(2)}, u32[]{:S(2)}) %collective-permute-start.3) | collective-permute-done | bytes 8224 | tf_op jit(solution)/shard_map/ppermute | solution.py:48
  8.0 2.8 %collective-permute-start.5 = (bf16[1,32,128]{2,1,0:T(8,128)(2,1)S(1)}, bf16[1,32,128]{2,1,0:T(8,128)(2,1)S(1)}, u32[]{:S(2)}, u32[]{:S(2)}) collective-permute-start(bf16[1,32,128]{2,1,0:T(8,128)(2,1)S(1)} %dynamic-slice_bitcast_fusion), channel_id=1, source_target_pairs={{0,6},{1,7},{2,4},{3,5},{4,2},{5,3},{6,0},{7,1},{8,14},{9,15},{10,... | collective-permute-start | bytes 24584 | tf_op jit(solution)/shard_map/ppermute | solution.py:48
  10.8 0.0 collective-permute-done.4.refs_5_
  10.8 2.6 %collective-permute-start.6 = (bf16[1,32,128]{2,1,0:T(8,128)(2,1)S(1)}, bf16[1,32,128]{2,1,0:T(8,128)(2,1)S(1)}, u32[]{:S(2)}, u32[]{:S(2)}) collective-permute-start(bf16[1,32,128]{2,1,0:T(8,128)(2,1)S(1)} %dynamic-slice_bitcast_fusion), channel_id=1, source_target_pairs={{0,7},{1,6},{2,5},{3,4},{4,3},{5,2},{6,1},{7,0},{8,15},{9,14},{10,... | collective-permute-start | bytes 24584 | tf_op jit(solution)/shard_map/ppermute | solution.py:48
  13.5 3.4 %collective-permute-done.5.refs_6_ = bf16[1,32,128]{2,1,0:T(8,128)(2,1)S(1)} collective-permute-done((bf16[1,32,128]{2,1,0:T(8,128)(2,1)S(1)}, bf16[1,32,128]{2,1,0:T(8,128)(2,1)S(1)}, u32[]{:S(2)}, u32[]{:S(2)}) %collective-permute-start.5) | collective-permute-done | bytes 8224 | tf_op jit(solution)/shard_map/ppermute | solution.py:48
  16.9 0.0 collective-permute-done.6.refs_7_
  16.9 0.0 collective-permute-done.refs_1_
  16.9 0.0 collective-permute-done.1.refs_2_
  16.9 0.0 collective-permute-done.2.refs_3_
  16.9 0.0 copy-start
  16.9 0.9 %copy-done = bf16[3,3,3,32,128]{4,3,2,1,0:T(8,128)(2,1)S(1)} copy-done((bf16[3,3,3,32,128]{4,3,2,1,0:T(8,128)(2,1)S(1)}, bf16[3,3,3,32,128]{4,3,2,1,0:T(8,128)(2,1)}, u32[]{:S(2)}) %copy-start) | copy-done | bytes 221208
  17.9 0.9 %copy-done.2 = bf16[1,16,32,128]{3,2,1,0:T(8,128)(2,1)S(1)} copy-done((bf16[1,16,32,128]{3,2,1,0:T(8,128)(2,1)S(1)}, bf16[1,16,32,128]{3,2,1,0:T(8,128)(2,1)}, u32[]{:S(2)}) %copy-start.2) | copy-done | bytes 131096
  18.8 0.9 %taps.2 = (bf16[16,32,128]{2,1,0:T(8,128)(2,1)S(1)}, f32[16,32,128]{2,1,0:T(8,128)S(1)}, bf16[16,32,128]{2,1,0:T(8,128)(2,1)S(1)}) custom-call(bf16[3,3,3,32,128]{4,3,2,1,0:T(8,128)(2,1)S(1)} %copy-done, bf16[16,32,128]{2,1,0:T(8,128)(2,1)S(1)} %bitcast.9, bf16[16,32,128]{2,1,0:T(8,128)(2,1)S(1)} %collective-permute-done.refs_1_, ...), custom_call_target="tpu_custom_call" | custom-call | tf_op jit(solution)/shard_map/taps/pallas_call | solution.py:19
  19.7 2.7 %collective-permute-start.7 = (bf16[16,32,128]{2,1,0:T(8,128)(2,1)S(1)}, bf16[16,32,128]{2,1,0:T(8,128)(2,1)S(1)}, u32[]{:S(2)}, u32[]{:S(2)}) collective-permute-start(bf16[16,32,128]{2,1,0:T(8,128)(2,1)S(1)} %get-tuple-element.13), channel_id=1, source_target_pairs={{0,8},{8,0},{16,24},{24,16},{1,9},{9,1},{17,25},{25,17},{2,10},{10... | collective-permute-start | bytes 393224 | tf_op jit(solution)/shard_map/ppermute | solution.py:131
  22.4 3.1 %collective-permute-start.8 = (bf16[16,32,128]{2,1,0:T(8,128)(2,1)S(1)}, bf16[16,32,128]{2,1,0:T(8,128)(2,1)S(1)}, u32[]{:S(2)}, u32[]{:S(2)}) collective-permute-start(bf16[16,32,128]{2,1,0:T(8,128)(2,1)S(1)} %get-tuple-element.15), channel_id=1, source_target_pairs={{0,0},{24,24},{8,16},{16,8},{1,1},{25,25},{9,17},{17,9},{2,2},{26,... | collective-permute-start | bytes 393224 | tf_op jit(solution)/shard_map/ppermute | solution.py:134
  25.5 0.0 copy-done.3
  25.5 0.1 copy.6.bias_ref
  25.6 0.0 collective-permute-done.7.near_ref
  25.6 3.5 %collective-permute-done.8.far_ref = bf16[16,32,128]{2,1,0:T(8,128)(2,1)S(1)} collective-permute-done((bf16[16,32,128]{2,1,0:T(8,128)(2,1)S(1)}, bf16[16,32,128]{2,1,0:T(8,128)(2,1)S(1)}, u32[]{:S(2)}, u32[]{:S(2)}) %collective-permute-start.8) | collective-permute-done | bytes 131104 | tf_op jit(solution)/shard_map/ppermute | solution.py:134
  29.1 0.1 finish.2
  29.2 1.2 %collective-permute-start.10 = (bf16[16,32,128]{2,1,0:T(8,128)(2,1)S(1)}, bf16[16,32,128]{2,1,0:T(8,128)(2,1)S(1)}, u32[]{:S(2)}, u32[]{:S(2)}) collective-permute-start(bf16[16,32,128]{2,1,0:T(8,128)(2,1)S(1)} %get-tuple-element.16.refs_0_), channel_id=1, source_target_pairs={{0,2},{1,3},{2,0},{3,1},{4,6},{5,7},{6,4},{7,5},{8,10},{9,11},{10,... | collective-permute-start | bytes 393224 | tf_op jit(solution)/shard_map/ppermute | solution.py:36
  30.4 1.8 %collective-permute-start.11 = (bf16[16,32,128]{2,1,0:T(8,128)(2,1)S(1)}, bf16[16,32,128]{2,1,0:T(8,128)(2,1)S(1)}, u32[]{:S(2)}, u32[]{:S(2)}) collective-permute-start(bf16[16,32,128]{2,1,0:T(8,128)(2,1)S(1)} %get-tuple-element.16.refs_0_), channel_id=1, source_target_pairs={{0,3},{1,2},{2,1},{3,0},{4,7},{5,6},{6,5},{7,4},{8,11},{9,10},{10,... | collective-permute-start | bytes 393224 | tf_op jit(solution)/shard_map/ppermute | solution.py:36
  32.2 0.2 collective-permute-start.9
  32.4 1.0 %collective-permute-start.12 = (bf16[1,32,128]{2,1,0:T(8,128)(2,1)S(1)}, bf16[1,32,128]{2,1,0:T(8,128)(2,1)S(1)}, u32[]{:S(2)}, u32[]{:S(2)}) collective-permute-start(bf16[1,32,128]{2,1,0:T(8,128)(2,1)S(1)} %get-tuple-element.17), channel_id=1, source_target_pairs={{0,4},{1,5},{2,6},{3,7},{4,0},{5,1},{6,2},{7,3},{8,12},{9,13},{10,... | collective-permute-start | bytes 24584 | tf_op jit(solution)/shard_map/ppermute | solution.py:48
  33.4 1.5 %collective-permute-start.13 = (bf16[1,32,128]{2,1,0:T(8,128)(2,1)S(1)}, bf16[1,32,128]{2,1,0:T(8,128)(2,1)S(1)}, u32[]{:S(2)}, u32[]{:S(2)}) collective-permute-start(bf16[1,32,128]{2,1,0:T(8,128)(2,1)S(1)} %get-tuple-element.17), channel_id=1, source_target_pairs={{0,5},{1,4},{2,7},{3,6},{4,1},{5,0},{6,3},{7,2},{8,13},{9,12},{10,... | collective-permute-start | bytes 24584 | tf_op jit(solution)/shard_map/ppermute | solution.py:48
  34.9 0.1 collective-permute-done.12.refs_4_
  34.9 2.0 %collective-permute-start.14 = (bf16[1,32,128]{2,1,0:T(8,128)(2,1)S(1)}, bf16[1,32,128]{2,1,0:T(8,128)(2,1)S(1)}, u32[]{:S(2)}, u32[]{:S(2)}) collective-permute-start(bf16[1,32,128]{2,1,0:T(8,128)(2,1)S(1)} %get-tuple-element.17), channel_id=1, source_target_pairs={{0,6},{1,7},{2,4},{3,5},{4,2},{5,3},{6,0},{7,1},{8,14},{9,15},{10,... | collective-permute-start | bytes 24584 | tf_op jit(solution)/shard_map/ppermute | solution.py:48
  36.9 2.1 %collective-permute-done.13.refs_5_ = bf16[1,32,128]{2,1,0:T(8,128)(2,1)S(1)} collective-permute-done((bf16[1,32,128]{2,1,0:T(8,128)(2,1)S(1)}, bf16[1,32,128]{2,1,0:T(8,128)(2,1)S(1)}, u32[]{:S(2)}, u32[]{:S(2)}) %collective-permute-start.13) | collective-permute-done | bytes 8224 | tf_op jit(solution)/shard_map/ppermute | solution.py:48
  39.0 2.3 %collective-permute-start.15 = (bf16[1,32,128]{2,1,0:T(8,128)(2,1)S(1)}, bf16[1,32,128]{2,1,0:T(8,128)(2,1)S(1)}, u32[]{:S(2)}, u32[]{:S(2)}) collective-permute-start(bf16[1,32,128]{2,1,0:T(8,128)(2,1)S(1)} %get-tuple-element.17), channel_id=1, source_target_pairs={{0,7},{1,6},{2,5},{3,4},{4,3},{5,2},{6,1},{7,0},{8,15},{9,14},{10,... | collective-permute-start | bytes 24584 | tf_op jit(solution)/shard_map/ppermute | solution.py:48
  41.4 0.0 collective-permute-done.14.refs_6_
  41.4 2.9 %collective-permute-done.15.refs_7_ = bf16[1,32,128]{2,1,0:T(8,128)(2,1)S(1)} collective-permute-done((bf16[1,32,128]{2,1,0:T(8,128)(2,1)S(1)}, bf16[1,32,128]{2,1,0:T(8,128)(2,1)S(1)}, u32[]{:S(2)}, u32[]{:S(2)}) %collective-permute-start.15) | collective-permute-done | bytes 8224 | tf_op jit(solution)/shard_map/ppermute | solution.py:48
  44.2 0.0 collective-permute-done.10.refs_2_
  44.2 0.0 collective-permute-done.11.refs_3_
  44.2 0.0 collective-permute-done.9.refs_1_
  44.3 0.9 %taps.3 = (bf16[16,32,128]{2,1,0:T(8,128)(2,1)S(1)}, f32[16,32,128]{2,1,0:T(8,128)S(1)}, bf16[16,32,128]{2,1,0:T(8,128)(2,1)S(1)}) custom-call(bf16[3,3,3,32,128]{4,3,2,1,0:T(8,128)(2,1)S(1)} %copy-done.1, bf16[16,32,128]{2,1,0:T(8,128)(2,1)S(1)} %get-tuple-element.16.refs_0_, bf16[16,32,128]{2,1,0:T(8,128)(2,1)S(1)} %collective-permute-done.9.refs_1_, ...), custom_call_target="tpu_custom_call" | custom-call | tf_op jit(solution)/shard_map/taps/pallas_call | solution.py:19
  45.2 0.1 collective-permute-start.16
  45.3 0.0 copy-start.4
  45.3 4.4 %collective-permute-start.17 = (bf16[16,32,128]{2,1,0:T(8,128)(2,1)S(1)}, bf16[16,32,128]{2,1,0:T(8,128)(2,1)S(1)}, u32[]{:S(2)}, u32[]{:S(2)}) collective-permute-start(bf16[16,32,128]{2,1,0:T(8,128)(2,1)S(1)} %get-tuple-element.20), channel_id=1, source_target_pairs={{0,0},{24,24},{8,16},{16,8},{1,1},{25,25},{9,17},{17,9},{2,2},{26,... | collective-permute-start | bytes 393224 | tf_op jit(solution)/shard_map/ppermute | solution.py:134
  49.7 0.1 copy.7.bias_ref
  49.8 0.0 collective-permute-done.16.near_ref
  49.8 2.5 %collective-permute-done.17.far_ref = bf16[16,32,128]{2,1,0:T(8,128)(2,1)S(1)} collective-permute-done((bf16[16,32,128]{2,1,0:T(8,128)(2,1)S(1)}, bf16[16,32,128]{2,1,0:T(8,128)(2,1)S(1)}, u32[]{:S(2)}, u32[]{:S(2)}) %collective-permute-start.17) | collective-permute-done | bytes 131104 | tf_op jit(solution)/shard_map/ppermute | solution.py:134
  52.4 0.7 %finish.3 = bf16[16,32,128]{2,1,0:T(8,128)(2,1)} custom-call(bf16[16,32,128]{2,1,0:T(8,128)(2,1)S(1)} %collective-permute-done.16.near_ref, f32[16,32,128]{2,1,0:T(8,128)S(1)} %get-tuple-element.19.center_ref, bf16[16,32,128]{2,1,0:T(8,128)(2,1)S(1)} %collective-permute-done.17.far_ref, f32[32,1]{1,0:T(8,128)S(1)} %copy.7.bias_ref), custom_call_target="tpu_custom_call" | custom-call | tf_op jit(solution)/shard_map/finish/pallas_call | solution.py:19
  (5 shorter events, 0.0 us)
Async XLA Ops:
  0.0 16.9 %collective-permute-start = (bf16[16,32,128]{2,1,0:T(8,128)(2,1)}, bf16[16,32,128]{2,1,0:T(8,128)(2,1)S(1)}, u32[]{:S(2)}, u32[]{:S(2)}) collective-permute-start(bf16[16,32,128]{2,1,0:T(8,128)(2,1)} %bitcast.6), channel_id=1, source_target_pairs={{0,1},{1,0},{2,3},{3,2},{4,5},{5,4},{6,7},{7,6},{8,9},{9,8},{10,11... | collective-permute-start | bytes 393224 | tf_op jit(solution)/shard_map/ppermute | solution.py:36
  2.1 14.8 %collective-permute-start.1 = (bf16[16,32,128]{2,1,0:T(8,128)(2,1)}, bf16[16,32,128]{2,1,0:T(8,128)(2,1)S(1)}, u32[]{:S(2)}, u32[]{:S(2)}) collective-permute-start(bf16[16,32,128]{2,1,0:T(8,128)(2,1)} %bitcast.7), channel_id=1, source_target_pairs={{0,2},{1,3},{2,0},{3,1},{4,6},{5,7},{6,4},{7,5},{8,10},{9,11},{10,... | collective-permute-start | bytes 393224 | tf_op jit(solution)/shard_map/ppermute | solution.py:36
  4.4 12.5 %collective-permute-start.2 = (bf16[16,32,128]{2,1,0:T(8,128)(2,1)}, bf16[16,32,128]{2,1,0:T(8,128)(2,1)S(1)}, u32[]{:S(2)}, u32[]{:S(2)}) collective-permute-start(bf16[16,32,128]{2,1,0:T(8,128)(2,1)} %bitcast.8), channel_id=1, source_target_pairs={{0,3},{1,2},{2,1},{3,0},{4,7},{5,6},{6,5},{7,4},{8,11},{9,10},{10,... | collective-permute-start | bytes 393224 | tf_op jit(solution)/shard_map/ppermute | solution.py:36
  5.2 2.8 %collective-permute-start.3 = (bf16[1,32,128]{2,1,0:T(8,128)(2,1)S(1)}, bf16[1,32,128]{2,1,0:T(8,128)(2,1)S(1)}, u32[]{:S(2)}, u32[]{:S(2)}) collective-permute-start(bf16[1,32,128]{2,1,0:T(8,128)(2,1)S(1)} %dynamic-slice_bitcast_fusion), channel_id=1, source_target_pairs={{0,4},{1,5},{2,6},{3,7},{4,0},{5,1},{6,2},{7,3},{8,12},{9,13},{10,... | collective-permute-start | bytes 24584 | tf_op jit(solution)/shard_map/ppermute | solution.py:48
  6.4 4.4 %collective-permute-start.4 = (bf16[1,32,128]{2,1,0:T(8,128)(2,1)S(1)}, bf16[1,32,128]{2,1,0:T(8,128)(2,1)S(1)}, u32[]{:S(2)}, u32[]{:S(2)}) collective-permute-start(bf16[1,32,128]{2,1,0:T(8,128)(2,1)S(1)} %dynamic-slice_bitcast_fusion), channel_id=1, source_target_pairs={{0,5},{1,4},{2,7},{3,6},{4,1},{5,0},{6,3},{7,2},{8,13},{9,12},{10,... | collective-permute-start | bytes 24584 | tf_op jit(solution)/shard_map/ppermute | solution.py:48
  8.0 8.9 %collective-permute-start.5 = (bf16[1,32,128]{2,1,0:T(8,128)(2,1)S(1)}, bf16[1,32,128]{2,1,0:T(8,128)(2,1)S(1)}, u32[]{:S(2)}, u32[]{:S(2)}) collective-permute-start(bf16[1,32,128]{2,1,0:T(8,128)(2,1)S(1)} %dynamic-slice_bitcast_fusion), channel_id=1, source_target_pairs={{0,6},{1,7},{2,4},{3,5},{4,2},{5,3},{6,0},{7,1},{8,14},{9,15},{10,... | collective-permute-start | bytes 24584 | tf_op jit(solution)/shard_map/ppermute | solution.py:48
  10.8 6.1 %collective-permute-start.6 = (bf16[1,32,128]{2,1,0:T(8,128)(2,1)S(1)}, bf16[1,32,128]{2,1,0:T(8,128)(2,1)S(1)}, u32[]{:S(2)}, u32[]{:S(2)}) collective-permute-start(bf16[1,32,128]{2,1,0:T(8,128)(2,1)S(1)} %dynamic-slice_bitcast_fusion), channel_id=1, source_target_pairs={{0,7},{1,6},{2,5},{3,4},{4,3},{5,2},{6,1},{7,0},{8,15},{9,14},{10,... | collective-permute-start | bytes 24584 | tf_op jit(solution)/shard_map/ppermute | solution.py:48
  16.9 0.9 %copy-start = (bf16[3,3,3,32,128]{4,3,2,1,0:T(8,128)(2,1)S(1)}, bf16[3,3,3,32,128]{4,3,2,1,0:T(8,128)(2,1)}, u32[]{:S(2)}) copy-start(bf16[3,3,3,32,128]{4,3,2,1,0:T(8,128)(2,1)} %kernel_ref.2) | copy-start | bytes 663556
  17.9 0.9 %copy-start.2 = (bf16[1,16,32,128]{3,2,1,0:T(8,128)(2,1)S(1)}, bf16[1,16,32,128]{3,2,1,0:T(8,128)(2,1)}, u32[]{:S(2)}) copy-start(bf16[1,16,32,128]{3,2,1,0:T(8,128)(2,1)} %param.5) | copy-start | bytes 393220
  19.7 5.9 %collective-permute-start.7 = (bf16[16,32,128]{2,1,0:T(8,128)(2,1)S(1)}, bf16[16,32,128]{2,1,0:T(8,128)(2,1)S(1)}, u32[]{:S(2)}, u32[]{:S(2)}) collective-permute-start(bf16[16,32,128]{2,1,0:T(8,128)(2,1)S(1)} %get-tuple-element.13), channel_id=1, source_target_pairs={{0,8},{8,0},{16,24},{24,16},{1,9},{9,1},{17,25},{25,17},{2,10},{10... | collective-permute-start | bytes 393224 | tf_op jit(solution)/shard_map/ppermute | solution.py:131
  22.4 3.1 %copy-start.3 = (f32[32]{0:T(128)S(1)}, f32[32]{0:T(128)}, u32[]{:S(2)}) copy-start(f32[32]{0:T(128)} %param.7) | copy-start | bytes 388
  22.4 6.7 %collective-permute-start.8 = (bf16[16,32,128]{2,1,0:T(8,128)(2,1)S(1)}, bf16[16,32,128]{2,1,0:T(8,128)(2,1)S(1)}, u32[]{:S(2)}, u32[]{:S(2)}) collective-permute-start(bf16[16,32,128]{2,1,0:T(8,128)(2,1)S(1)} %get-tuple-element.15), channel_id=1, source_target_pairs={{0,0},{24,24},{8,16},{16,8},{1,1},{25,25},{9,17},{17,9},{2,2},{26,... | collective-permute-start | bytes 393224 | tf_op jit(solution)/shard_map/ppermute | solution.py:134
  29.1 15.2 %copy-start.1 = (bf16[3,3,3,32,128]{4,3,2,1,0:T(8,128)(2,1)S(1)}, bf16[3,3,3,32,128]{4,3,2,1,0:T(8,128)(2,1)}, u32[]{:S(2)}) copy-start(bf16[3,3,3,32,128]{4,3,2,1,0:T(8,128)(2,1)} %kernel_ref.3) | copy-start | bytes 663556
  29.2 15.0 %collective-permute-start.10 = (bf16[16,32,128]{2,1,0:T(8,128)(2,1)S(1)}, bf16[16,32,128]{2,1,0:T(8,128)(2,1)S(1)}, u32[]{:S(2)}, u32[]{:S(2)}) collective-permute-start(bf16[16,32,128]{2,1,0:T(8,128)(2,1)S(1)} %get-tuple-element.16.refs_0_), channel_id=1, source_target_pairs={{0,2},{1,3},{2,0},{3,1},{4,6},{5,7},{6,4},{7,5},{8,10},{9,11},{10,... | collective-permute-start | bytes 393224 | tf_op jit(solution)/shard_map/ppermute | solution.py:36
  30.4 13.9 %collective-permute-start.11 = (bf16[16,32,128]{2,1,0:T(8,128)(2,1)S(1)}, bf16[16,32,128]{2,1,0:T(8,128)(2,1)S(1)}, u32[]{:S(2)}, u32[]{:S(2)}) collective-permute-start(bf16[16,32,128]{2,1,0:T(8,128)(2,1)S(1)} %get-tuple-element.16.refs_0_), channel_id=1, source_target_pairs={{0,3},{1,2},{2,1},{3,0},{4,7},{5,6},{6,5},{7,4},{8,11},{9,10},{10,... | collective-permute-start | bytes 393224 | tf_op jit(solution)/shard_map/ppermute | solution.py:36
  32.2 12.0 %collective-permute-start.9 = (bf16[16,32,128]{2,1,0:T(8,128)(2,1)S(1)}, bf16[16,32,128]{2,1,0:T(8,128)(2,1)S(1)}, u32[]{:S(2)}, u32[]{:S(2)}) collective-permute-start(bf16[16,32,128]{2,1,0:T(8,128)(2,1)S(1)} %get-tuple-element.16.refs_0_), channel_id=1, source_target_pairs={{0,1},{1,0},{2,3},{3,2},{4,5},{5,4},{6,7},{7,6},{8,9},{9,8},{10,11... | collective-permute-start | bytes 393224 | tf_op jit(solution)/shard_map/ppermute | solution.py:36
  32.4 2.5 %collective-permute-start.12 = (bf16[1,32,128]{2,1,0:T(8,128)(2,1)S(1)}, bf16[1,32,128]{2,1,0:T(8,128)(2,1)S(1)}, u32[]{:S(2)}, u32[]{:S(2)}) collective-permute-start(bf16[1,32,128]{2,1,0:T(8,128)(2,1)S(1)} %get-tuple-element.17), channel_id=1, source_target_pairs={{0,4},{1,5},{2,6},{3,7},{4,0},{5,1},{6,2},{7,3},{8,12},{9,13},{10,... | collective-permute-start | bytes 24584 | tf_op jit(solution)/shard_map/ppermute | solution.py:48
  33.4 5.6 %collective-permute-start.13 = (bf16[1,32,128]{2,1,0:T(8,128)(2,1)S(1)}, bf16[1,32,128]{2,1,0:T(8,128)(2,1)S(1)}, u32[]{:S(2)}, u32[]{:S(2)}) collective-permute-start(bf16[1,32,128]{2,1,0:T(8,128)(2,1)S(1)} %get-tuple-element.17), channel_id=1, source_target_pairs={{0,5},{1,4},{2,7},{3,6},{4,1},{5,0},{6,3},{7,2},{8,13},{9,12},{10,... | collective-permute-start | bytes 24584 | tf_op jit(solution)/shard_map/ppermute | solution.py:48
  34.9 6.4 %collective-permute-start.14 = (bf16[1,32,128]{2,1,0:T(8,128)(2,1)S(1)}, bf16[1,32,128]{2,1,0:T(8,128)(2,1)S(1)}, u32[]{:S(2)}, u32[]{:S(2)}) collective-permute-start(bf16[1,32,128]{2,1,0:T(8,128)(2,1)S(1)} %get-tuple-element.17), channel_id=1, source_target_pairs={{0,6},{1,7},{2,4},{3,5},{4,2},{5,3},{6,0},{7,1},{8,14},{9,15},{10,... | collective-permute-start | bytes 24584 | tf_op jit(solution)/shard_map/ppermute | solution.py:48
  39.0 5.2 %collective-permute-start.15 = (bf16[1,32,128]{2,1,0:T(8,128)(2,1)S(1)}, bf16[1,32,128]{2,1,0:T(8,128)(2,1)S(1)}, u32[]{:S(2)}, u32[]{:S(2)}) collective-permute-start(bf16[1,32,128]{2,1,0:T(8,128)(2,1)S(1)} %get-tuple-element.17), channel_id=1, source_target_pairs={{0,7},{1,6},{2,5},{3,4},{4,3},{5,2},{6,1},{7,0},{8,15},{9,14},{10,... | collective-permute-start | bytes 24584 | tf_op jit(solution)/shard_map/ppermute | solution.py:48
  45.2 4.6 %collective-permute-start.16 = (bf16[16,32,128]{2,1,0:T(8,128)(2,1)S(1)}, bf16[16,32,128]{2,1,0:T(8,128)(2,1)S(1)}, u32[]{:S(2)}, u32[]{:S(2)}) collective-permute-start(bf16[16,32,128]{2,1,0:T(8,128)(2,1)S(1)} %get-tuple-element.18), channel_id=1, source_target_pairs={{0,8},{8,0},{16,24},{24,16},{1,9},{9,1},{17,25},{25,17},{2,10},{10... | collective-permute-start | bytes 393224 | tf_op jit(solution)/shard_map/ppermute | solution.py:131
  45.3 4.4 %copy-start.4 = (f32[32]{0:T(128)S(1)}, f32[32]{0:T(128)}, u32[]{:S(2)}) copy-start(f32[32]{0:T(128)} %param.9) | copy-start | bytes 388
  45.3 7.1 %collective-permute-start.17 = (bf16[16,32,128]{2,1,0:T(8,128)(2,1)S(1)}, bf16[16,32,128]{2,1,0:T(8,128)(2,1)S(1)}, u32[]{:S(2)}, u32[]{:S(2)}) collective-permute-start(bf16[16,32,128]{2,1,0:T(8,128)(2,1)S(1)} %get-tuple-element.20), channel_id=1, source_target_pairs={{0,0},{24,24},{8,16},{16,8},{1,1},{25,25},{9,17},{17,9},{2,2},{26,... | collective-permute-start | bytes 393224 | tf_op jit(solution)/shard_map/ppermute | solution.py:134

commit v3 on v0

v3 whole, which is shorter than its diff:
```python
import functools

import jax
import jax.numpy as jnp
from jax import lax
from jax.experimental import pallas as pl
from jax.experimental.pallas import tpu as pltpu
from jax.sharding import PartitionSpec as P

VMEM_BYTES = 12 << 20
VMEM = pltpu.VMEM


def call(kernel, name, out_shape, *operands, stored=(), scratch=(), flops=0):
    spec = pl.BlockSpec(memory_space=VMEM)
    return pl.pallas_call(
        kernel,
        out_shape=out_shape,
        in_specs=[pl.BlockSpec(memory_space=pltpu.HBM)] * len(stored) + [spec] * len(operands),
        out_specs=[spec] * len(out_shape),
        scratch_shapes=scratch,
        compiler_params=pltpu.CompilerParams(vmem_limit_bytes=VMEM_BYTES),
        cost_estimate=pl.CostEstimate(flops=flops, bytes_accessed=0, transcendentals=0),
        name=name,
    )(
        *[pltpu.with_memory_space_constraint(operand, pltpu.HBM) for operand in stored],
        *[pltpu.with_memory_space_constraint(operand, VMEM) for operand in operands],
    )


def sides():
    return 1 if lax.axis_size("gy") == 2 else 2


def partners():
    count = lax.axis_size("ch")
    return [[(i, i ^ step) for i in range(count)] for step in range(count)]


def channel_swaps(block):
    return [lax.ppermute(block, "ch", pairs) for pairs in partners()[1:]]


def edge_moves(edge, step, pairings):
    rows, channels = lax.axis_size("gy"), lax.axis_size("ch")
    if rows == 2:
        along = [(0, 1), (1, 0)]
    else:
        along = [(i, i + step) for i in range(rows) if 0 <= i + step < rows]
    return [
        lax.ppermute(edge, ("gy", "ch"), [(i * channels + c, j * channels + d) for i, j in along for c, d in pairs])
        for pairs in pairings
    ]


def prepare_kernel(*refs):
    stored, (_, first_taps, second_taps, first_bias, second_bias, own), refs = refs[:5], refs[5:11], refs[11:]
    copies, first_ref, second_ref, *bias_refs = refs
    moves = [
        pltpu.make_async_copy(source, target, copies.at[i])
        for i, (source, target) in enumerate(zip(stored, (first_ref, second_ref, *bias_refs, own)))
    ]
    for move in moves:
        move.start()
    for move in moves:
        move.wait()
    gx = lax.axis_index("gx")
    outputs, inputs = first_ref.shape[3:]
    far = jnp.where(gx % 2 == 0, 2, 0)
    outer = jnp.full((outputs, inputs), (gx == 0) | (gx == lax.axis_size("gx") - 1))
    for kernel_ref, out in ((first_ref, first_taps), (second_ref, second_taps)):
        for slot, a in enumerate((far, 2 - far, 1)):
            for b in range(3):
                for c in range(3):
                    tap = kernel_ref[a, b, c]
                    if slot == 0:
                        tap = jnp.where(outer, 0.0, tap)
                    first = (slot * 3 + c) * outputs
                    out[first : first + outputs, b * inputs : (b + 1) * inputs] = tap
    at = [lax.broadcasted_iota(jnp.int32, (outputs, outputs), axis) for axis in range(2)]
    for bias_ref, out in zip(bias_refs, (first_bias, second_bias)):
        column = jnp.sum(jnp.where(at[0] == at[1], bias_ref[...], 0.0), axis=1, keepdims=True)
        out[...] = jnp.broadcast_to(column, out.shape)


def terms(taps, volume, slots, outs):
    rows, outputs, depth = outs[0].shape
    inputs = volume.shape[1]
    lane = lax.broadcasted_iota(jnp.int32, (outputs, depth), 1)
    for y in [*range(0, rows - 1, 2)] + [rows - 2] * (rows % 2):
        window = jnp.concatenate(
            [volume[y + i : y + i + 3].reshape(3 * inputs, depth) for i in range(2)], axis=1
        )
        product = jnp.dot(taps, window, preferred_element_type=jnp.float32)
        for i in range(2):
            for slot, out in zip(slots, outs):
                first, middle, last = (
                    product[(slot * 3 + c) * outputs : (slot * 3 + c + 1) * outputs, i * depth : (i + 1) * depth]
                    for c in range(3)
                )
                total = (
                    middle
                    + jnp.where(lane == 0, 0.0, pltpu.roll(first, 1, 1))
                    + jnp.where(lane == depth - 1, 0.0, pltpu.roll(last, depth - 1, 1))
                )
                out[y + i] = total.astype(out.dtype)


def beside_kernel(count, halo, taps_ref, *refs):
    (far_ref, near_ref, volume), refs = refs[-3:], refs[:-3]
    blocks, halos = refs[:count], refs[count:]
    rows, part, depth = blocks[0].shape
    place, low = lax.axis_index("ch"), lax.axis_index("gy") == 0
    if sides() == 1:
        own, beside = jnp.where(low, 1, halo), jnp.where(low, 1 + rows, 0)
        outside = jnp.where(low, 0, volume.shape[0] - 1)
        volume[outside] = jnp.zeros((part * count, depth), volume.dtype)
    else:
        own = halo
    def channels(step):
        source = jnp.bitwise_xor(place, step % count)
        return pl.ds(pl.multiple_of(source * part, part), part)

    for step in range(count):
        volume[pl.ds(own, rows), channels(step), :] = blocks[step][...]
    step = 0
    for ref in halos:
        for first in range(0, ref.shape[0], halo):
            if sides() == 1:
                at = beside
            else:
                at = 0 if step < count else halo + rows
            volume[pl.ds(at, halo), channels(step), :] = ref[first : first + halo]
            step += 1
    span = 3 * far_ref.shape[1]
    terms(taps_ref[: 2 * span], volume, (0, 1), (far_ref, near_ref))


def center_kernel(taps_ref, volume, center_ref):
    terms(taps_ref[6 * center_ref.shape[1] :], volume, (0,), (center_ref,))


def finish_kernel(near_ref, center_ref, far_ref, bias_ref, out_ref):
    total = center_ref[...] + near_ref[...].astype(jnp.float32) + far_ref[...].astype(jnp.float32)
    out_ref[...] = jnp.maximum(total + bias_ref[...][None], 0.0).astype(out_ref.dtype)


def hidden_kernel(near_ref, center_ref, far_ref, bias_ref, out_ref):
    finish_kernel(near_ref, center_ref, far_ref, bias_ref, out_ref)
    if lax.axis_size("gy") > 2:
        gy, rows = lax.axis_index("gy"), out_ref.shape[0]
        for row, outside in ((0, gy == 0), (rows - 1, gy == lax.axis_size("gy") - 1)):
            kept = out_ref[row]
            out_ref[row] = jnp.where(jnp.full(kept.shape, outside), 0.0, kept)


def layer(blocks, halos, halo, rows, taps, bias, kernel, out_type):
    count = len(blocks)
    _, part, depth = blocks[0].shape
    outputs = taps.shape[0] // 9
    flops = 2 * rows * depth * taps.shape[0] * taps.shape[1]
    side = VMEM((rows, outputs, depth), jnp.bfloat16)
    far, near, volume = call(
        functools.partial(beside_kernel, count, halo),
        "beside",
        [side, side, VMEM((rows + 2, part * count, depth), jnp.bfloat16)],
        taps,
        *blocks,
        *halos,
        flops=2 * flops // 3,
    )
    planes = lax.axis_size("gx")
    inner = [(i, i + 1) for i in range(1, planes - 1, 2)]
    outer = [(0, 0), (planes - 1, planes - 1)]
    far = lax.ppermute(far, "gx", outer + inner + [(j, i) for i, j in inner])
    near = lax.ppermute(near, "gx", [(i, i ^ 1) for i in range(planes)])
    (center,) = call(
        center_kernel, "center", [VMEM((rows, outputs, depth), jnp.float32)], taps, volume, flops=flops // 3
    )
    (out,) = call(
        kernel,
        "finish",
        [out_type((rows, outputs, depth), jnp.bfloat16)],
        near,
        center,
        far,
        bias,
    )
    return out


def per_device(density, first_kernel, first_bias, second_kernel, second_bias):
    density = density[0]
    rows, part, depth = density.shape
    outputs = first_kernel.shape[3]
    count = lax.axis_size("ch")
    pairings = partners()
    if sides() == 1:
        start = jnp.where(lax.axis_index("gy") == 0, rows - 2, 0)
        halos = edge_moves(lax.dynamic_slice_in_dim(density, start, 2, 0), 1, pairings[:2])
        last = lax.ppermute(density, "ch", pairings[-1])
        nearest = lax.ppermute(density, "ch", pairings[1])
    else:
        halos = edge_moves(density[-2:], 1, pairings) + edge_moves(density[:2], -1, pairings)
        others = channel_swaps(density)
    taps_shape = VMEM((9 * outputs, 3 * part * count), jnp.bfloat16)
    bias_shape = VMEM((outputs, depth), jnp.float32)
    first_taps, second_taps, first_bias, second_bias, own = call(
        prepare_kernel,
        "prepare",
        [taps_shape, taps_shape, bias_shape, bias_shape, VMEM(density.shape, density.dtype)],
        halos[0],
        stored=(first_kernel, second_kernel, first_bias.reshape(1, -1), second_bias.reshape(1, -1), density),
        scratch=[
            pltpu.SemaphoreType.DMA((5,)),
            *[VMEM(kernel.shape, kernel.dtype) for kernel in (first_kernel, second_kernel)],
            *[VMEM((1, outputs), jnp.float32)] * 2,
        ],
    )
    if sides() == 1:
        place = lax.axis_index("ch")
        inner = (place == 1) | (place == 2)
        handed = lax.ppermute(jnp.where(inner, last, own), "ch", [(0, 2), (3, 1), (1, 0), (2, 3)])
        others = [nearest, handed, last]
        pair, _ = lax.optimization_barrier((jnp.concatenate(halos, axis=0), last))
        halos = [pair, lax.ppermute(pair, "ch", pairings[2])]
    hidden = layer(
        [own, *others], halos, 2, rows + sides(), first_taps, first_bias, hidden_kernel, VMEM
    )
    blocks = [hidden, *channel_swaps(hidden)]
    out = layer(blocks, [], 0, rows, second_taps, second_bias, finish_kernel, jax.ShapeDtypeStruct)
    return out[None]


def solution(mesh):
    placed = (
        P("gx", "gy", "ch", None),
        P(None, None, None, "ch", None),
        P("ch"),
        P(None, None, None, "ch", None),
        P("ch"),
    )
    return jax.shard_map(
        per_device, mesh=mesh, in_specs=placed, out_specs=P("gx", "gy", "ch", None), check_vma=False
    )
```

time: 127 us -> 43.2 us (0.34); the launches traced: 125 us -> 43 us
  local copies, waits for them, and re-layouts: 39.1 us -> 0.75 us
  blocking collectives: 28 us -> 0 us
  other arithmetic: 9.15 us -> 0.02 us
  matrix products: 8.49 us -> 0 us
  starting transfers between devices: 27 us -> 19.2 us
  waiting for transfers between devices: 13 us -> 18.2 us
  Pallas kernels: 0 us -> 4.62 us
    all_gather x2 -> x0, blocking collectives: 28 us -> none  [layer_channels(): whole = lax.all_gather(field, 'ch', axis=2, tiled=True)]
    ppermute x6 -> x0, local copies, waits for them, and re-layouts: 9.81 us -> none  [the longest x3 4.91 us: with_halo(): lax.ppermute(lax.slice_in_dim(block, block.shape[dim] - width, None, axis...]
    conv_general_dilated x2 -> x0, matrix products: 8.49 us -> none  [conv_taps(): lax.conv_general_dilated(padded[None], kernel, (1, 1, 1), 'VALID', dimens...]
    conv_general_dilated x10 -> x0, local copies, waits for them, and re-layouts: 7.88 us -> none  [conv_taps(): lax.conv_general_dilated(padded[None], kernel, (1, 1, 1), 'VALID', dimens...]
    ppermute x8 -> x13, starting transfers between devices: 27 us -> 19.2 us  [the longest x2 6.14 us: layer(): far = lax.ppermute(far, 'gx', outer + inner + [(j, i) for i, j in inner])]
    concatenate x2 -> x0, local copies, waits for them, and re-layouts: 6.33 us -> none  [with_halo(): block = jnp.concatenate([low, block, high], axis=dim)]
    slice x4 -> x0, local copies, waits for them, and re-layouts: 5.99 us -> none  [the longest x3 4.21 us: with_halo(): lax.slice_in_dim(block, block.shape[dim] - width, None, axis=dim)]
    ppermute x8 -> x13, waiting for transfers between devices: 13 us -> 18.2 us  [the longest x3 6.28 us: channel_swaps(): return [lax.ppermute(block, 'ch', pairs) for pairs in partners()[1:]]]
  transfers between devices with their start and end apart: 8 -> 13, of which waited for: 3 -> 7; matrix products, arithmetic and copies ran while one was open for 9% -> 2% of each run, Pallas kernels for 0% -> 5%
where the time goes in v3:
time: 43.2 us; the launch traced here: 43 us
  starting transfers between devices  19.2 us (44%)
  waiting for transfers between devices  18.2 us (42%)
  Pallas kernels  4.62 us (11%)
  local copies, waits for them, and re-layouts  0.75 us (2%)
    ppermute x3, waiting for transfers between devices, channel_swaps(): return [lax.ppermute(block, 'ch', pairs) for pairs in partners()[1:]]  6.28 us
    ppermute x2, starting transfers between devices, layer(): far = lax.ppermute(far, 'gx', outer + inner + [(j, i) for i, j in inner])  6.14 us
    ppermute x2, waiting for transfers between devices, layer(): far = lax.ppermute(far, 'gx', outer + inner + [(j, i) for i, j in inner])  5.75 us
    ppermute x1, waiting for transfers between devices, per_device(): halos = [pair, lax.ppermute(pair, 'ch', pairings[2])]  5.59 us
    pallas_call x7, Pallas kernels, call(): pl.pallas_call(kernel, out_shape=out_shape, in_specs=[pl.BlockSpec(memory...  4.62 us
    ppermute x1, starting transfers between devices, per_device(): last = lax.ppermute(density, 'ch', pairings[-1])  4.15 us
    ppermute x3, starting transfers between devices, channel_swaps(): return [lax.ppermute(block, 'ch', pairs) for pairs in partners()[1:]]  3.61 us
    ppermute x1, starting transfers between devices, per_device(): halos = [pair, lax.ppermute(pair, 'ch', pairings[2])]  1.44 us
  transfers between devices with their start and end apart: 13, of which 7 were waited for; matrix products, arithmetic and copies ran while one was open for 2% of the time, Pallas kernels for 5%

profile of v3, /device:TPU:1, one launch (start us, length us, event | category | flops | bytes accessed | tf_op | source)
XLA Modules:
  0.0 43.0 jit_solution(4473817937262398244)
XLA Ops:
  0.0 4.2 %collective-permute-start.2 = (bf16[16,32,128]{2,1,0:T(8,128)(2,1)}, bf16[16,32,128]{2,1,0:T(8,128)(2,1)S(1)}, u32[]{:S(2)}, u32[]{:S(2)}) collective-permute-start(bf16[16,32,128]{2,1,0:T(8,128)(2,1)} %bitcast.6), channel_id=1, source_target_pairs={{0,3},{1,2},{2,1},{3,0},{4,7},{5,6},{6,5},{7,4},{8,11},{9,10},{10,... | collective-permute-start | bytes 393224 | tf_op jit(solution)/shard_map/ppermute | solution.py:201
  4.2 0.8 %dynamic-slice_bitcast_fusion = bf16[2,32,128]{2,1,0:T(8,128)(2,1)S(1)} fusion(bf16[1,16,32,128]{3,2,1,0:T(8,128)(2,1)} %param.5, s32[]{:T(128)S(6)} %select_n.13), kind=kLoop, calls=%fused_computation.2 | loop fusion | bytes 32772 | tf_op jit(solution)/shard_map/dynamic_slice | solution.py:200
  4.9 1.2 %collective-permute-start = (bf16[2,32,128]{2,1,0:T(8,128)(2,1)S(1)}, bf16[2,32,128]{2,1,0:T(8,128)(2,1)S(1)}, u32[]{:S(2)}, u32[]{:S(2)}) collective-permute-start(bf16[2,32,128]{2,1,0:T(8,128)(2,1)S(1)} %dynamic-slice_bitcast_fusion), channel_id=1, source_target_pairs={{0,4},{1,5},{2,6},{3,7},{4,0},{5,1},{6,2},{7,3},{8,12},{9,13},{10,... | collective-permute-start | bytes 49160 | tf_op jit(solution)/shard_map/ppermute | solution.py:51
  6.1 0.0 collective-permute-start.4
  6.1 1.4 %collective-permute-start.1 = (bf16[16,32,128]{2,1,0:T(8,128)(2,1)}, bf16[16,32,128]{2,1,0:T(8,128)(2,1)S(1)}, u32[]{:S(2)}, u32[]{:S(2)}) collective-permute-start(bf16[16,32,128]{2,1,0:T(8,128)(2,1)} %bitcast.7), channel_id=1, source_target_pairs={{0,1},{1,0},{2,3},{3,2},{4,5},{5,4},{6,7},{7,6},{8,9},{9,8},{10,11... | collective-permute-start | bytes 393224 | tf_op jit(solution)/shard_map/ppermute | solution.py:202
  7.6 0.2 collective-permute-done.refs_5_
  7.8 1.4 %prepare.1 = (bf16[288,384]{1,0:T(8,128)(2,1)S(1)}, bf16[288,384]{1,0:T(8,128)(2,1)S(1)}, f32[32,128]{1,0:T(8,128)S(1)}, f32[32,128]{1,0:T(8,128)S(1)}, bf16[16,32,128]{2,1,0:T(8,128)(2,1)S(1)}) custom-call(bf16[3,3,3,32,128]{4,3,2,1,0:T(8,128)(2,1)} %refs_0_.1, bf16[3,3,3,32,128]{4,3,2,1,0:T(8,128)(2,1)} %refs_1_.1, f32[1,32]{1,0:T(1,128)} %bitcast.9, ...), custom_call_target="tpu_custom_call" | custom-call | tf_op jit(solution)/shard_map/prepare/pallas_call | solution.py:16
  9.2 0.0 collective-permute-done.2.refs_3_
  9.2 0.1 collective-permute-start.3
  9.3 0.3 collective-permute-done.4
  9.6 1.4 %collective-permute-start.5 = (bf16[4,32,128]{2,1,0:T(8,128)(2,1)S(1)}, bf16[4,32,128]{2,1,0:T(8,128)(2,1)S(1)}, u32[]{:S(2)}, u32[]{:S(2)}) collective-permute-start(bf16[4,32,128]{2,1,0:T(8,128)(2,1)S(1)} %pad_maximum_fusion.refs_4_), channel_id=1, source_target_pairs={{0,2},{1,3},{2,0},{3,1},{4,6},{5,7},{6,4},{7,5},{8,10},{9,11},{10,... | collective-permute-start | bytes 98312 | tf_op jit(solution)/shard_map/ppermute | solution.py:226
  11.0 0.0 collective-permute-done.1.refs_1_
  11.1 5.6 %collective-permute-done.5.refs_5_ = bf16[4,32,128]{2,1,0:T(8,128)(2,1)S(1)} collective-permute-done((bf16[4,32,128]{2,1,0:T(8,128)(2,1)S(1)}, bf16[4,32,128]{2,1,0:T(8,128)(2,1)S(1)}, u32[]{:S(2)}, u32[]{:S(2)}) %collective-permute-start.5) | collective-permute-done | bytes 32800 | tf_op jit(solution)/shard_map/ppermute | solution.py:226
  16.6 0.0 collective-permute-done.3.refs_2_
  16.6 0.8 %beside.2 = (bf16[17,32,128]{2,1,0:T(8,128)(2,1)S(1)}, bf16[17,32,128]{2,1,0:T(8,128)(2,1)S(1)}, bf16[19,128,128]{2,1,0:T(8,128)(2,1)S(1)}) custom-call(bf16[288,384]{1,0:T(8,128)(2,1)S(1)} %get-tuple-element.18.taps_ref, bf16[16,32,128]{2,1,0:T(8,128)(2,1)S(1)} %get-tuple-element.19.refs_0_, bf16[16,32,128]{2,1,0:T(8,128)(2,1)S(1)} %collective-permute-done.1.refs_1_, ...), custom_call_target="tpu_custom_call" | custom-call | flops 320864256 | tf_op jit(solution)/shard_map/beside/pallas_call | solution.py:16
  17.4 1.1 %collective-permute-start.6 = (bf16[17,32,128]{2,1,0:T(8,128)(2,1)S(1)}, bf16[17,32,128]{2,1,0:T(8,128)(2,1)S(1)}, u32[]{:S(2)}, u32[]{:S(2)}) collective-permute-start(bf16[17,32,128]{2,1,0:T(8,128)(2,1)S(1)} %get-tuple-element.21), channel_id=1, source_target_pairs={{0,8},{8,0},{16,24},{24,16},{1,9},{9,1},{17,25},{25,17},{2,10},{10... | collective-permute-start | bytes 417800 | tf_op jit(solution)/shard_map/ppermute | solution.py:176
  18.5 3.0 %collective-permute-start.7 = (bf16[17,32,128]{2,1,0:T(8,128)(2,1)S(1)}, bf16[17,32,128]{2,1,0:T(8,128)(2,1)S(1)}, u32[]{:S(2)}, u32[]{:S(2)}) collective-permute-start(bf16[17,32,128]{2,1,0:T(8,128)(2,1)S(1)} %get-tuple-element.23), channel_id=1, source_target_pairs={{0,0},{24,24},{8,16},{16,8},{1,1},{25,25},{9,17},{17,9},{2,2},{26,... | collective-permute-start | bytes 417800 | tf_op jit(solution)/shard_map/ppermute | solution.py:175
  21.6 0.5 %center.2.center_ref = f32[17,32,128]{2,1,0:T(8,128)S(1)} custom-call(bf16[288,384]{1,0:T(8,128)(2,1)S(1)} %get-tuple-element.18.taps_ref, bf16[19,128,128]{2,1,0:T(8,128)(2,1)S(1)} %get-tuple-element.22.volume), custom_call_target="tpu_custom_call" | custom-call | flops 160432128 | tf_op jit(solution)/shard_map/center/pallas_call | solution.py:16
  22.1 0.0 collective-permute-done.6.near_ref
  22.1 3.1 %collective-permute-done.7.far_ref = bf16[17,32,128]{2,1,0:T(8,128)(2,1)S(1)} collective-permute-done((bf16[17,32,128]{2,1,0:T(8,128)(2,1)S(1)}, bf16[17,32,128]{2,1,0:T(8,128)(2,1)S(1)}, u32[]{:S(2)}, u32[]{:S(2)}) %collective-permute-start.7) | collective-permute-done | bytes 139296 | tf_op jit(solution)/shard_map/ppermute | solution.py:175
  25.2 0.1 finish.2.refs_0_
  25.3 2.0 %collective-permute-start.10 = (bf16[17,32,128]{2,1,0:T(8,128)(2,1)S(1)}, bf16[17,32,128]{2,1,0:T(8,128)(2,1)S(1)}, u32[]{:S(2)}, u32[]{:S(2)}) collective-permute-start(bf16[17,32,128]{2,1,0:T(8,128)(2,1)S(1)} %finish.2.refs_0_), channel_id=1, source_target_pairs={{0,3},{1,2},{2,1},{3,0},{4,7},{5,6},{6,5},{7,4},{8,11},{9,10},{10,... | collective-permute-start | bytes 417800 | tf_op jit(solution)/shard_map/ppermute | solution.py:41
  27.2 0.0 collective-permute-start.9
  27.2 1.6 %collective-permute-start.8 = (bf16[17,32,128]{2,1,0:T(8,128)(2,1)S(1)}, bf16[17,32,128]{2,1,0:T(8,128)(2,1)S(1)}, u32[]{:S(2)}, u32[]{:S(2)}) collective-permute-start(bf16[17,32,128]{2,1,0:T(8,128)(2,1)S(1)} %finish.2.refs_0_), channel_id=1, source_target_pairs={{0,1},{1,0},{2,3},{3,2},{4,5},{5,4},{6,7},{7,6},{8,9},{9,8},{10,11... | collective-permute-start | bytes 417800 | tf_op jit(solution)/shard_map/ppermute | solution.py:41
  28.9 2.4 %collective-permute-done.10.refs_3_ = bf16[17,32,128]{2,1,0:T(8,128)(2,1)S(1)} collective-permute-done((bf16[17,32,128]{2,1,0:T(8,128)(2,1)S(1)}, bf16[17,32,128]{2,1,0:T(8,128)(2,1)S(1)}, u32[]{:S(2)}, u32[]{:S(2)}) %collective-permute-start.10) | collective-permute-done | bytes 139296 | tf_op jit(solution)/shard_map/ppermute | solution.py:41
  31.2 3.9 %collective-permute-done.9.refs_2_ = bf16[17,32,128]{2,1,0:T(8,128)(2,1)S(1)} collective-permute-done((bf16[17,32,128]{2,1,0:T(8,128)(2,1)S(1)}, bf16[17,32,128]{2,1,0:T(8,128)(2,1)S(1)}, u32[]{:S(2)}, u32[]{:S(2)}) %collective-permute-start.9) | collective-permute-done | bytes 139296 | tf_op jit(solution)/shard_map/ppermute | solution.py:41
  35.2 0.0 collective-permute-done.8.refs_1_
  35.2 0.7 %beside.3 = (bf16[16,32,128]{2,1,0:T(8,128)(2,1)S(1)}, bf16[16,32,128]{2,1,0:T(8,128)(2,1)S(1)}, bf16[18,128,128]{2,1,0:T(8,128)(2,1)S(1)}) custom-call(bf16[288,384]{1,0:T(8,128)(2,1)S(1)} %get-tuple-element.17.taps_ref, bf16[17,32,128]{2,1,0:T(8,128)(2,1)S(1)} %finish.2.refs_0_, bf16[17,32,128]{2,1,0:T(8,128)(2,1)S(1)} %collective-permute-done.8.refs_1_, ...), custom_call_target="tpu_custom_call" | custom-call | flops 301989888 | tf_op jit(solution)/shard_map/beside/pallas_call | solution.py:16
  35.9 0.1 collective-permute-start.11
  36.0 3.1 %collective-permute-start.12 = (bf16[16,32,128]{2,1,0:T(8,128)(2,1)S(1)}, bf16[16,32,128]{2,1,0:T(8,128)(2,1)S(1)}, u32[]{:S(2)}, u32[]{:S(2)}) collective-permute-start(bf16[16,32,128]{2,1,0:T(8,128)(2,1)S(1)} %get-tuple-element.27), channel_id=1, source_target_pairs={{0,0},{24,24},{8,16},{16,8},{1,1},{25,25},{9,17},{17,9},{2,2},{26,... | collective-permute-start | bytes 393224 | tf_op jit(solution)/shard_map/ppermute | solution.py:175
  39.1 0.5 %center.3.center_ref = f32[16,32,128]{2,1,0:T(8,128)S(1)} custom-call(bf16[288,384]{1,0:T(8,128)(2,1)S(1)} %get-tuple-element.17.taps_ref, bf16[18,128,128]{2,1,0:T(8,128)(2,1)S(1)} %get-tuple-element.26.volume), custom_call_target="tpu_custom_call" | custom-call | flops 150994944 | tf_op jit(solution)/shard_map/center/pallas_call | solution.py:16
  39.6 0.0 collective-permute-done.11.near_ref
  39.6 2.7 %collective-permute-done.12.far_ref = bf16[16,32,128]{2,1,0:T(8,128)(2,1)S(1)} collective-permute-done((bf16[16,32,128]{2,1,0:T(8,128)(2,1)S(1)}, bf16[16,32,128]{2,1,0:T(8,128)(2,1)S(1)}, u32[]{:S(2)}, u32[]{:S(2)}) %collective-permute-start.12) | collective-permute-done | bytes 131104 | tf_op jit(solution)/shard_map/ppermute | solution.py:175
  42.2 0.7 %finish.3 = bf16[16,32,128]{2,1,0:T(8,128)(2,1)} custom-call(bf16[16,32,128]{2,1,0:T(8,128)(2,1)S(1)} %collective-permute-done.11.near_ref, f32[16,32,128]{2,1,0:T(8,128)S(1)} %center.3.center_ref, bf16[16,32,128]{2,1,0:T(8,128)(2,1)S(1)} %collective-permute-done.12.far_ref, f32[32,128]{1,0:T(8,128)S(1)} %get-tuple-element.28.bias_ref), custom_call_target="tpu_custom_call" | custom-call | tf_op jit(solution)/shard_map/finish/pallas_call | solution.py:16
  (2 shorter events, 0.0 us)
Async XLA Ops:
  0.0 9.2 %collective-permute-start.2 = (bf16[16,32,128]{2,1,0:T(8,128)(2,1)}, bf16[16,32,128]{2,1,0:T(8,128)(2,1)S(1)}, u32[]{:S(2)}, u32[]{:S(2)}) collective-permute-start(bf16[16,32,128]{2,1,0:T(8,128)(2,1)} %bitcast.6), channel_id=1, source_target_pairs={{0,3},{1,2},{2,1},{3,0},{4,7},{5,6},{6,5},{7,4},{8,11},{9,10},{10,... | collective-permute-start | bytes 393224 | tf_op jit(solution)/shard_map/ppermute | solution.py:201
  4.9 2.9 %collective-permute-start = (bf16[2,32,128]{2,1,0:T(8,128)(2,1)S(1)}, bf16[2,32,128]{2,1,0:T(8,128)(2,1)S(1)}, u32[]{:S(2)}, u32[]{:S(2)}) collective-permute-start(bf16[2,32,128]{2,1,0:T(8,128)(2,1)S(1)} %dynamic-slice_bitcast_fusion), channel_id=1, source_target_pairs={{0,4},{1,5},{2,6},{3,7},{4,0},{5,1},{6,2},{7,3},{8,12},{9,13},{10,... | collective-permute-start | bytes 49160 | tf_op jit(solution)/shard_map/ppermute | solution.py:51
  6.1 3.5 %collective-permute-start.4 = (bf16[2,32,128]{2,1,0:T(8,128)(2,1)S(1)}, bf16[2,32,128]{2,1,0:T(8,128)(2,1)S(1)}, u32[]{:S(2)}, u32[]{:S(2)}) collective-permute-start(bf16[2,32,128]{2,1,0:T(8,128)(2,1)S(1)} %dynamic-slice_bitcast_fusion), channel_id=1, source_target_pairs={{0,5},{1,4},{2,7},{3,6},{4,1},{5,0},{6,3},{7,2},{8,13},{9,12},{10,... | collective-permute-start | bytes 49160 | tf_op jit(solution)/shard_map/ppermute | solution.py:51
  6.1 4.9 %collective-permute-start.1 = (bf16[16,32,128]{2,1,0:T(8,128)(2,1)}, bf16[16,32,128]{2,1,0:T(8,128)(2,1)S(1)}, u32[]{:S(2)}, u32[]{:S(2)}) collective-permute-start(bf16[16,32,128]{2,1,0:T(8,128)(2,1)} %bitcast.7), channel_id=1, source_target_pairs={{0,1},{1,0},{2,3},{3,2},{4,5},{5,4},{6,7},{7,6},{8,9},{9,8},{10,11... | collective-permute-start | bytes 393224 | tf_op jit(solution)/shard_map/ppermute | solution.py:202
  9.2 7.4 %collective-permute-start.3 = (bf16[16,32,128]{2,1,0:T(8,128)(2,1)S(1)}, bf16[16,32,128]{2,1,0:T(8,128)(2,1)S(1)}, u32[]{:S(2)}, u32[]{:S(2)}) collective-permute-start(bf16[16,32,128]{2,1,0:T(8,128)(2,1)S(1)} %broadcast_select_fusion), channel_id=1, source_target_pairs={{0,2},{3,1},{1,0},{2,3},{4,6},{7,5},{5,4},{6,7},{8,10},{11,9},{9,8... | collective-permute-start | bytes 393224 | tf_op jit(solution)/shard_map/ppermute | solution.py:223
  9.6 7.0 %collective-permute-start.5 = (bf16[4,32,128]{2,1,0:T(8,128)(2,1)S(1)}, bf16[4,32,128]{2,1,0:T(8,128)(2,1)S(1)}, u32[]{:S(2)}, u32[]{:S(2)}) collective-permute-start(bf16[4,32,128]{2,1,0:T(8,128)(2,1)S(1)} %pad_maximum_fusion.refs_4_), channel_id=1, source_target_pairs={{0,2},{1,3},{2,0},{3,1},{4,6},{5,7},{6,4},{7,5},{8,10},{9,11},{10,... | collective-permute-start | bytes 98312 | tf_op jit(solution)/shard_map/ppermute | solution.py:226
  17.4 4.7 %collective-permute-start.6 = (bf16[17,32,128]{2,1,0:T(8,128)(2,1)S(1)}, bf16[17,32,128]{2,1,0:T(8,128)(2,1)S(1)}, u32[]{:S(2)}, u32[]{:S(2)}) collective-permute-start(bf16[17,32,128]{2,1,0:T(8,128)(2,1)S(1)} %get-tuple-element.21), channel_id=1, source_target_pairs={{0,8},{8,0},{16,24},{24,16},{1,9},{9,1},{17,25},{25,17},{2,10},{10... | collective-permute-start | bytes 417800 | tf_op jit(solution)/shard_map/ppermute | solution.py:176
  18.5 6.7 %collective-permute-start.7 = (bf16[17,32,128]{2,1,0:T(8,128)(2,1)S(1)}, bf16[17,32,128]{2,1,0:T(8,128)(2,1)S(1)}, u32[]{:S(2)}, u32[]{:S(2)}) collective-permute-start(bf16[17,32,128]{2,1,0:T(8,128)(2,1)S(1)} %get-tuple-element.23), channel_id=1, source_target_pairs={{0,0},{24,24},{8,16},{16,8},{1,1},{25,25},{9,17},{17,9},{2,2},{26,... | collective-permute-start | bytes 417800 | tf_op jit(solution)/shard_map/ppermute | solution.py:175
  25.3 6.0 %collective-permute-start.10 = (bf16[17,32,128]{2,1,0:T(8,128)(2,1)S(1)}, bf16[17,32,128]{2,1,0:T(8,128)(2,1)S(1)}, u32[]{:S(2)}, u32[]{:S(2)}) collective-permute-start(bf16[17,32,128]{2,1,0:T(8,128)(2,1)S(1)} %finish.2.refs_0_), channel_id=1, source_target_pairs={{0,3},{1,2},{2,1},{3,0},{4,7},{5,6},{6,5},{7,4},{8,11},{9,10},{10,... | collective-permute-start | bytes 417800 | tf_op jit(solution)/shard_map/ppermute | solution.py:41
  27.2 7.9 %collective-permute-start.9 = (bf16[17,32,128]{2,1,0:T(8,128)(2,1)S(1)}, bf16[17,32,128]{2,1,0:T(8,128)(2,1)S(1)}, u32[]{:S(2)}, u32[]{:S(2)}) collective-permute-start(bf16[17,32,128]{2,1,0:T(8,128)(2,1)S(1)} %finish.2.refs_0_), channel_id=1, source_target_pairs={{0,2},{1,3},{2,0},{3,1},{4,6},{5,7},{6,4},{7,5},{8,10},{9,11},{10,... | collective-permute-start | bytes 417800 | tf_op jit(solution)/shard_map/ppermute | solution.py:41
  27.2 7.9 %collective-permute-start.8 = (bf16[17,32,128]{2,1,0:T(8,128)(2,1)S(1)}, bf16[17,32,128]{2,1,0:T(8,128)(2,1)S(1)}, u32[]{:S(2)}, u32[]{:S(2)}) collective-permute-start(bf16[17,32,128]{2,1,0:T(8,128)(2,1)S(1)} %finish.2.refs_0_), channel_id=1, source_target_pairs={{0,1},{1,0},{2,3},{3,2},{4,5},{5,4},{6,7},{7,6},{8,9},{9,8},{10,11... | collective-permute-start | bytes 417800 | tf_op jit(solution)/shard_map/ppermute | solution.py:41
  35.9 3.7 %collective-permute-start.11 = (bf16[16,32,128]{2,1,0:T(8,128)(2,1)S(1)}, bf16[16,32,128]{2,1,0:T(8,128)(2,1)S(1)}, u32[]{:S(2)}, u32[]{:S(2)}) collective-permute-start(bf16[16,32,128]{2,1,0:T(8,128)(2,1)S(1)} %get-tuple-element.25), channel_id=1, source_target_pairs={{0,8},{8,0},{16,24},{24,16},{1,9},{9,1},{17,25},{25,17},{2,10},{10... | collective-permute-start | bytes 393224 | tf_op jit(solution)/shard_map/ppermute | solution.py:176
  36.0 6.3 %collective-permute-start.12 = (bf16[16,32,128]{2,1,0:T(8,128)(2,1)S(1)}, bf16[16,32,128]{2,1,0:T(8,128)(2,1)S(1)}, u32[]{:S(2)}, u32[]{:S(2)}) collective-permute-start(bf16[16,32,128]{2,1,0:T(8,128)(2,1)S(1)} %get-tuple-element.27), channel_id=1, source_target_pairs={{0,0},{24,24},{8,16},{16,8},{1,1},{25,25},{9,17},{17,9},{2,2},{26,... | collective-permute-start | bytes 393224 | tf_op jit(solution)/shard_map/ppermute | solution.py:175

commit v4 on v3

--- a/solution.py
+++ b/solution.py
@@ -51,6 +51,18 @@
         lax.ppermute(edge, ("gy", "ch"), [(i * channels + c, j * channels + d) for i, j in along for c, d in pairs])
         for pairs in pairings
     ]
+
+
+def far_pairs(idle):
+    planes, rows = lax.axis_size("gx"), lax.axis_size("gy")
+    pairs = [(i, i + 1, g, g) for i in range(1, planes - 1, 2) for g in range(rows)]
+    if idle:
+        alone = [(i * rows + g, i * rows + g) for i in (0, planes - 1) for g in range(rows)]
+    else:
+        alone = []
+        pairs += [(i, i, g, g + 1) for i in (0, planes - 1) for g in range(0, rows, 2)]
+    there = [(i * rows + g, j * rows + h) for i, j, g, h in pairs]
+    return alone + there + [(j, i) for i, j in there]
 
 
 def prepare_kernel(*refs):
@@ -154,7 +166,7 @@
             out_ref[row] = jnp.where(jnp.full(kept.shape, outside), 0.0, kept)
 
 
-def layer(blocks, halos, halo, rows, taps, bias, kernel, out_type):
+def layer(blocks, halos, halo, rows, taps, bias, kernel, out_type, idle):
     count = len(blocks)
     _, part, depth = blocks[0].shape
     outputs = taps.shape[0] // 9
@@ -170,9 +182,7 @@
         flops=2 * flops // 3,
     )
     planes = lax.axis_size("gx")
-    inner = [(i, i + 1) for i in range(1, planes - 1, 2)]
-    outer = [(0, 0), (planes - 1, planes - 1)]
-    far = lax.ppermute(far, "gx", outer + inner + [(j, i) for i, j in inner])
+    far = lax.ppermute(far, ("gx", "gy"), far_pairs(idle))
     near = lax.ppermute(near, "gx", [(i, i ^ 1) for i in range(planes)])
     (center,) = call(
         center_kernel, "center", [VMEM((rows, outputs, depth), jnp.float32)], taps, volume, flops=flops // 3
@@ -225,10 +235,10 @@
         pair, _ = lax.optimization_barrier((jnp.concatenate(halos, axis=0), last))
         halos = [pair, lax.ppermute(pair, "ch", pairings[2])]
     hidden = layer(
-        [own, *others], halos, 2, rows + sides(), first_taps, first_bias, hidden_kernel, VMEM
+        [own, *others], halos, 2, rows + sides(), first_taps, first_bias, hidden_kernel, VMEM, True
     )
     blocks = [hidden, *channel_swaps(hidden)]
-    out = layer(blocks, [], 0, rows, second_taps, second_bias, finish_kernel, jax.ShapeDtypeStruct)
+    out = layer(blocks, [], 0, rows, second_taps, second_bias, finish_kernel, jax.ShapeDtypeStruct, False)
     return out[None]
 
 

time: 43.2 us -> 42.3 us (0.979)
  the two profiles are of different devices: /device:TPU:1 before, /device:TPU:0 now
where the time goes in v4:
time: 42.3 us; the launch traced here: 42.1 us
  starting transfers between devices  19 us (45%)
  waiting for transfers between devices  17.6 us (42%)
  Pallas kernels  4.62 us (11%)
  local copies, waits for them, and re-layouts  0.75 us (2%)
    ppermute x3, waiting for transfers between devices, channel_swaps(): return [lax.ppermute(block, 'ch', pairs) for pairs in partners()[1:]]  9.83 us
    ppermute x1, starting transfers between devices, per_device(): last = lax.ppermute(density, 'ch', pairings[-1])  5.05 us
    pallas_call x7, Pallas kernels, call(): pl.pallas_call(kernel, out_shape=out_shape, in_specs=[pl.BlockSpec(memory...  4.62 us
    ppermute x3, starting transfers between devices, channel_swaps(): return [lax.ppermute(block, 'ch', pairs) for pairs in partners()[1:]]  4.45 us
    ppermute x1, waiting for transfers between devices, per_device(): halos = [pair, lax.ppermute(pair, 'ch', pairings[2])]  4.28 us
    ppermute x2, waiting for transfers between devices, layer(): far = lax.ppermute(far, ('gx', 'gy'), far_pairs(idle))  2.99 us
    ppermute x2, starting transfers between devices, layer(): far = lax.ppermute(far, ('gx', 'gy'), far_pairs(idle))  2.13 us
    ppermute x1, starting transfers between devices, per_device(): nearest = lax.ppermute(density, 'ch', pairings[1])  1.99 us
  transfers between devices with their start and end apart: 13, of which 7 were waited for; matrix products, arithmetic and copies ran while one was open for 2% of the time, Pallas kernels for 6%

profile of v4, /device:TPU:0, one launch (start us, length us, event | category | flops | bytes accessed | tf_op | source)
XLA Modules:
  0.0 42.1 jit_solution(13357758908462568549)
XLA Ops:
  0.0 5.0 %collective-permute-start.2 = (bf16[16,32,128]{2,1,0:T(8,128)(2,1)}, bf16[16,32,128]{2,1,0:T(8,128)(2,1)S(1)}, u32[]{:S(2)}, u32[]{:S(2)}) collective-permute-start(bf16[16,32,128]{2,1,0:T(8,128)(2,1)} %bitcast.6), channel_id=1, source_target_pairs={{0,3},{1,2},{2,1},{3,0},{4,7},{5,6},{6,5},{7,4},{8,11},{9,10},{10,... | collective-permute-start | bytes 393224 | tf_op jit(solution)/shard_map/ppermute | solution.py:211
  5.0 0.8 %dynamic-slice_bitcast_fusion = bf16[2,32,128]{2,1,0:T(8,128)(2,1)S(1)} fusion(bf16[1,16,32,128]{3,2,1,0:T(8,128)(2,1)} %param.5, s32[]{:T(128)S(6)} %select_n.13), kind=kLoop, calls=%fused_computation.2 | loop fusion | bytes 32772 | tf_op jit(solution)/shard_map/dynamic_slice | solution.py:210
  5.8 1.5 %collective-permute-start = (bf16[2,32,128]{2,1,0:T(8,128)(2,1)S(1)}, bf16[2,32,128]{2,1,0:T(8,128)(2,1)S(1)}, u32[]{:S(2)}, u32[]{:S(2)}) collective-permute-start(bf16[2,32,128]{2,1,0:T(8,128)(2,1)S(1)} %dynamic-slice_bitcast_fusion), channel_id=1, source_target_pairs={{0,4},{1,5},{2,6},{3,7},{4,0},{5,1},{6,2},{7,3},{8,12},{9,13},{10,... | collective-permute-start | bytes 49160 | tf_op jit(solution)/shard_map/ppermute | solution.py:51
  7.3 0.0 collective-permute-start.4
  7.3 2.0 %collective-permute-start.1 = (bf16[16,32,128]{2,1,0:T(8,128)(2,1)}, bf16[16,32,128]{2,1,0:T(8,128)(2,1)S(1)}, u32[]{:S(2)}, u32[]{:S(2)}) collective-permute-start(bf16[16,32,128]{2,1,0:T(8,128)(2,1)} %bitcast.7), channel_id=1, source_target_pairs={{0,1},{1,0},{2,3},{3,2},{4,5},{5,4},{6,7},{7,6},{8,9},{9,8},{10,11... | collective-permute-start | bytes 393224 | tf_op jit(solution)/shard_map/ppermute | solution.py:212
  9.3 0.2 collective-permute-done.refs_5_
  9.5 1.4 %prepare.1 = (bf16[288,384]{1,0:T(8,128)(2,1)S(1)}, bf16[288,384]{1,0:T(8,128)(2,1)S(1)}, f32[32,128]{1,0:T(8,128)S(1)}, f32[32,128]{1,0:T(8,128)S(1)}, bf16[16,32,128]{2,1,0:T(8,128)(2,1)S(1)}) custom-call(bf16[3,3,3,32,128]{4,3,2,1,0:T(8,128)(2,1)} %refs_0_.1, bf16[3,3,3,32,128]{4,3,2,1,0:T(8,128)(2,1)} %refs_1_.1, f32[1,32]{1,0:T(1,128)} %bitcast.9, ...), custom_call_target="tpu_custom_call" | custom-call | tf_op jit(solution)/shard_map/prepare/pallas_call | solution.py:16
  10.9 0.0 collective-permute-done.2.refs_3_
  10.9 1.4 %collective-permute-start.3 = (bf16[16,32,128]{2,1,0:T(8,128)(2,1)S(1)}, bf16[16,32,128]{2,1,0:T(8,128)(2,1)S(1)}, u32[]{:S(2)}, u32[]{:S(2)}) collective-permute-start(bf16[16,32,128]{2,1,0:T(8,128)(2,1)S(1)} %broadcast_select_fusion), channel_id=1, source_target_pairs={{0,2},{3,1},{1,0},{2,3},{4,6},{7,5},{5,4},{6,7},{8,10},{11,9},{9,8... | collective-permute-start | bytes 393224 | tf_op jit(solution)/shard_map/ppermute | solution.py:233
  12.4 0.0 collective-permute-done.4
  12.4 0.9 %collective-permute-start.5 = (bf16[4,32,128]{2,1,0:T(8,128)(2,1)S(1)}, bf16[4,32,128]{2,1,0:T(8,128)(2,1)S(1)}, u32[]{:S(2)}, u32[]{:S(2)}) collective-permute-start(bf16[4,32,128]{2,1,0:T(8,128)(2,1)S(1)} %pad_maximum_fusion.refs_4_), channel_id=1, source_target_pairs={{0,2},{1,3},{2,0},{3,1},{4,6},{5,7},{6,4},{7,5},{8,10},{9,11},{10,... | collective-permute-start | bytes 98312 | tf_op jit(solution)/shard_map/ppermute | solution.py:236
  13.3 0.1 collective-permute-done.1.refs_1_
  13.4 4.3 %collective-permute-done.5.refs_5_ = bf16[4,32,128]{2,1,0:T(8,128)(2,1)S(1)} collective-permute-done((bf16[4,32,128]{2,1,0:T(8,128)(2,1)S(1)}, bf16[4,32,128]{2,1,0:T(8,128)(2,1)S(1)}, u32[]{:S(2)}, u32[]{:S(2)}) %collective-permute-start.5) | collective-permute-done | bytes 32800 | tf_op jit(solution)/shard_map/ppermute | solution.py:236
  17.6 0.0 collective-permute-done.3.refs_2_
  17.6 0.8 %beside.2 = (bf16[17,32,128]{2,1,0:T(8,128)(2,1)S(1)}, bf16[17,32,128]{2,1,0:T(8,128)(2,1)S(1)}, bf16[19,128,128]{2,1,0:T(8,128)(2,1)S(1)}) custom-call(bf16[288,384]{1,0:T(8,128)(2,1)S(1)} %get-tuple-element.18.taps_ref, bf16[16,32,128]{2,1,0:T(8,128)(2,1)S(1)} %get-tuple-element.19.refs_0_, bf16[16,32,128]{2,1,0:T(8,128)(2,1)S(1)} %collective-permute-done.1.refs_1_, ...), custom_call_target="tpu_custom_call" | custom-call | flops 320864256 | tf_op jit(solution)/shard_map/beside/pallas_call | solution.py:16
  18.4 0.1 collective-permute-start.6
  18.5 0.7 %collective-permute-start.7 = (bf16[17,32,128]{2,1,0:T(8,128)(2,1)S(1)}, bf16[17,32,128]{2,1,0:T(8,128)(2,1)S(1)}, u32[]{:S(2)}, u32[]{:S(2)}) collective-permute-start(bf16[17,32,128]{2,1,0:T(8,128)(2,1)S(1)} %get-tuple-element.23), channel_id=1, source_target_pairs={{0,0},{4,4},{24,24},{28,28},{8,16},{12,20},{16,8},{20,12},{1,1},{5... | collective-permute-start | bytes 417800 | tf_op jit(solution)/shard_map/ppermute | solution.py:185
  19.2 0.5 %center.2.center_ref = f32[17,32,128]{2,1,0:T(8,128)S(1)} custom-call(bf16[288,384]{1,0:T(8,128)(2,1)S(1)} %get-tuple-element.18.taps_ref, bf16[19,128,128]{2,1,0:T(8,128)(2,1)S(1)} %get-tuple-element.22.volume), custom_call_target="tpu_custom_call" | custom-call | flops 160432128 | tf_op jit(solution)/shard_map/center/pallas_call | solution.py:16
  19.7 0.2 collective-permute-done.6.near_ref
  19.8 0.0 collective-permute-done.7.far_ref
  19.8 0.1 finish.2.refs_0_
  19.9 2.3 %collective-permute-start.10 = (bf16[17,32,128]{2,1,0:T(8,128)(2,1)S(1)}, bf16[17,32,128]{2,1,0:T(8,128)(2,1)S(1)}, u32[]{:S(2)}, u32[]{:S(2)}) collective-permute-start(bf16[17,32,128]{2,1,0:T(8,128)(2,1)S(1)} %finish.2.refs_0_), channel_id=1, source_target_pairs={{0,3},{1,2},{2,1},{3,0},{4,7},{5,6},{6,5},{7,4},{8,11},{9,10},{10,... | collective-permute-start | bytes 417800 | tf_op jit(solution)/shard_map/ppermute | solution.py:41
  22.2 0.0 collective-permute-start.9
  22.2 2.2 %collective-permute-start.8 = (bf16[17,32,128]{2,1,0:T(8,128)(2,1)S(1)}, bf16[17,32,128]{2,1,0:T(8,128)(2,1)S(1)}, u32[]{:S(2)}, u32[]{:S(2)}) collective-permute-start(bf16[17,32,128]{2,1,0:T(8,128)(2,1)S(1)} %finish.2.refs_0_), channel_id=1, source_target_pairs={{0,1},{1,0},{2,3},{3,2},{4,5},{5,4},{6,7},{7,6},{8,9},{9,8},{10,11... | collective-permute-start | bytes 417800 | tf_op jit(solution)/shard_map/ppermute | solution.py:41
  24.4 2.6 %collective-permute-done.10.refs_3_ = bf16[17,32,128]{2,1,0:T(8,128)(2,1)S(1)} collective-permute-done((bf16[17,32,128]{2,1,0:T(8,128)(2,1)S(1)}, bf16[17,32,128]{2,1,0:T(8,128)(2,1)S(1)}, u32[]{:S(2)}, u32[]{:S(2)}) %collective-permute-start.10) | collective-permute-done | bytes 139296 | tf_op jit(solution)/shard_map/ppermute | solution.py:41
  26.9 7.2 %collective-permute-done.9.refs_2_ = bf16[17,32,128]{2,1,0:T(8,128)(2,1)S(1)} collective-permute-done((bf16[17,32,128]{2,1,0:T(8,128)(2,1)S(1)}, bf16[17,32,128]{2,1,0:T(8,128)(2,1)S(1)}, u32[]{:S(2)}, u32[]{:S(2)}) %collective-permute-start.9) | collective-permute-done | bytes 139296 | tf_op jit(solution)/shard_map/ppermute | solution.py:41
  34.2 0.0 collective-permute-done.8.refs_1_
  34.2 0.7 %beside.3 = (bf16[16,32,128]{2,1,0:T(8,128)(2,1)S(1)}, bf16[16,32,128]{2,1,0:T(8,128)(2,1)S(1)}, bf16[18,128,128]{2,1,0:T(8,128)(2,1)S(1)}) custom-call(bf16[288,384]{1,0:T(8,128)(2,1)S(1)} %get-tuple-element.17.taps_ref, bf16[17,32,128]{2,1,0:T(8,128)(2,1)S(1)} %finish.2.refs_0_, bf16[17,32,128]{2,1,0:T(8,128)(2,1)S(1)} %collective-permute-done.8.refs_1_, ...), custom_call_target="tpu_custom_call" | custom-call | flops 301989888 | tf_op jit(solution)/shard_map/beside/pallas_call | solution.py:16
  34.9 1.5 %collective-permute-start.11 = (bf16[16,32,128]{2,1,0:T(8,128)(2,1)S(1)}, bf16[16,32,128]{2,1,0:T(8,128)(2,1)S(1)}, u32[]{:S(2)}, u32[]{:S(2)}) collective-permute-start(bf16[16,32,128]{2,1,0:T(8,128)(2,1)S(1)} %get-tuple-element.25), channel_id=1, source_target_pairs={{0,8},{8,0},{16,24},{24,16},{1,9},{9,1},{17,25},{25,17},{2,10},{10... | collective-permute-start | bytes 393224 | tf_op jit(solution)/shard_map/ppermute | solution.py:186
  36.4 1.5 %collective-permute-start.12 = (bf16[16,32,128]{2,1,0:T(8,128)(2,1)S(1)}, bf16[16,32,128]{2,1,0:T(8,128)(2,1)S(1)}, u32[]{:S(2)}, u32[]{:S(2)}) collective-permute-start(bf16[16,32,128]{2,1,0:T(8,128)(2,1)S(1)} %get-tuple-element.27), channel_id=1, source_target_pairs={{8,16},{12,20},{0,4},{24,28},{16,8},{20,12},{4,0},{28,24},{9,17},{... | collective-permute-start | bytes 393224 | tf_op jit(solution)/shard_map/ppermute | solution.py:185
  37.9 0.5 %center.3.center_ref = f32[16,32,128]{2,1,0:T(8,128)S(1)} custom-call(bf16[288,384]{1,0:T(8,128)(2,1)S(1)} %get-tuple-element.17.taps_ref, bf16[18,128,128]{2,1,0:T(8,128)(2,1)S(1)} %get-tuple-element.26.volume), custom_call_target="tpu_custom_call" | custom-call | flops 150994944 | tf_op jit(solution)/shard_map/center/pallas_call | solution.py:16
  38.4 0.0 collective-permute-done.11.near_ref
  38.4 3.0 %collective-permute-done.12.far_ref = bf16[16,32,128]{2,1,0:T(8,128)(2,1)S(1)} collective-permute-done((bf16[16,32,128]{2,1,0:T(8,128)(2,1)S(1)}, bf16[16,32,128]{2,1,0:T(8,128)(2,1)S(1)}, u32[]{:S(2)}, u32[]{:S(2)}) %collective-permute-start.12) | collective-permute-done | bytes 131104 | tf_op jit(solution)/shard_map/ppermute | solution.py:185
  41.4 0.7 %finish.3 = bf16[16,32,128]{2,1,0:T(8,128)(2,1)} custom-call(bf16[16,32,128]{2,1,0:T(8,128)(2,1)S(1)} %collective-permute-done.11.near_ref, f32[16,32,128]{2,1,0:T(8,128)S(1)} %center.3.center_ref, bf16[16,32,128]{2,1,0:T(8,128)(2,1)S(1)} %collective-permute-done.12.far_ref, f32[32,128]{1,0:T(8,128)S(1)} %get-tuple-element.28.bias_ref), custom_call_target="tpu_custom_call" | custom-call | tf_op jit(solution)/shard_map/finish/pallas_call | solution.py:16
  (2 shorter events, 0.0 us)
Async XLA Ops:
  0.0 10.9 %collective-permute-start.2 = (bf16[16,32,128]{2,1,0:T(8,128)(2,1)}, bf16[16,32,128]{2,1,0:T(8,128)(2,1)S(1)}, u32[]{:S(2)}, u32[]{:S(2)}) collective-permute-start(bf16[16,32,128]{2,1,0:T(8,128)(2,1)} %bitcast.6), channel_id=1, source_target_pairs={{0,3},{1,2},{2,1},{3,0},{4,7},{5,6},{6,5},{7,4},{8,11},{9,10},{10,... | collective-permute-start | bytes 393224 | tf_op jit(solution)/shard_map/ppermute | solution.py:211
  5.8 3.7 %collective-permute-start = (bf16[2,32,128]{2,1,0:T(8,128)(2,1)S(1)}, bf16[2,32,128]{2,1,0:T(8,128)(2,1)S(1)}, u32[]{:S(2)}, u32[]{:S(2)}) collective-permute-start(bf16[2,32,128]{2,1,0:T(8,128)(2,1)S(1)} %dynamic-slice_bitcast_fusion), channel_id=1, source_target_pairs={{0,4},{1,5},{2,6},{3,7},{4,0},{5,1},{6,2},{7,3},{8,12},{9,13},{10,... | collective-permute-start | bytes 49160 | tf_op jit(solution)/shard_map/ppermute | solution.py:51
  7.3 5.1 %collective-permute-start.4 = (bf16[2,32,128]{2,1,0:T(8,128)(2,1)S(1)}, bf16[2,32,128]{2,1,0:T(8,128)(2,1)S(1)}, u32[]{:S(2)}, u32[]{:S(2)}) collective-permute-start(bf16[2,32,128]{2,1,0:T(8,128)(2,1)S(1)} %dynamic-slice_bitcast_fusion), channel_id=1, source_target_pairs={{0,5},{1,4},{2,7},{3,6},{4,1},{5,0},{6,3},{7,2},{8,13},{9,12},{10,... | collective-permute-start | bytes 49160 | tf_op jit(solution)/shard_map/ppermute | solution.py:51
  7.3 6.1 %collective-permute-start.1 = (bf16[16,32,128]{2,1,0:T(8,128)(2,1)}, bf16[16,32,128]{2,1,0:T(8,128)(2,1)S(1)}, u32[]{:S(2)}, u32[]{:S(2)}) collective-permute-start(bf16[16,32,128]{2,1,0:T(8,128)(2,1)} %bitcast.7), channel_id=1, source_target_pairs={{0,1},{1,0},{2,3},{3,2},{4,5},{5,4},{6,7},{7,6},{8,9},{9,8},{10,11... | collective-permute-start | bytes 393224 | tf_op jit(solution)/shard_map/ppermute | solution.py:212
  10.9 6.7 %collective-permute-start.3 = (bf16[16,32,128]{2,1,0:T(8,128)(2,1)S(1)}, bf16[16,32,128]{2,1,0:T(8,128)(2,1)S(1)}, u32[]{:S(2)}, u32[]{:S(2)}) collective-permute-start(bf16[16,32,128]{2,1,0:T(8,128)(2,1)S(1)} %broadcast_select_fusion), channel_id=1, source_target_pairs={{0,2},{3,1},{1,0},{2,3},{4,6},{7,5},{5,4},{6,7},{8,10},{11,9},{9,8... | collective-permute-start | bytes 393224 | tf_op jit(solution)/shard_map/ppermute | solution.py:233
  12.4 5.3 %collective-permute-start.5 = (bf16[4,32,128]{2,1,0:T(8,128)(2,1)S(1)}, bf16[4,32,128]{2,1,0:T(8,128)(2,1)S(1)}, u32[]{:S(2)}, u32[]{:S(2)}) collective-permute-start(bf16[4,32,128]{2,1,0:T(8,128)(2,1)S(1)} %pad_maximum_fusion.refs_4_), channel_id=1, source_target_pairs={{0,2},{1,3},{2,0},{3,1},{4,6},{5,7},{6,4},{7,5},{8,10},{9,11},{10,... | collective-permute-start | bytes 98312 | tf_op jit(solution)/shard_map/ppermute | solution.py:236
  18.4 1.4 %collective-permute-start.6 = (bf16[17,32,128]{2,1,0:T(8,128)(2,1)S(1)}, bf16[17,32,128]{2,1,0:T(8,128)(2,1)S(1)}, u32[]{:S(2)}, u32[]{:S(2)}) collective-permute-start(bf16[17,32,128]{2,1,0:T(8,128)(2,1)S(1)} %get-tuple-element.21), channel_id=1, source_target_pairs={{0,8},{8,0},{16,24},{24,16},{1,9},{9,1},{17,25},{25,17},{2,10},{10... | collective-permute-start | bytes 417800 | tf_op jit(solution)/shard_map/ppermute | solution.py:186
  18.5 1.3 %collective-permute-start.7 = (bf16[17,32,128]{2,1,0:T(8,128)(2,1)S(1)}, bf16[17,32,128]{2,1,0:T(8,128)(2,1)S(1)}, u32[]{:S(2)}, u32[]{:S(2)}) collective-permute-start(bf16[17,32,128]{2,1,0:T(8,128)(2,1)S(1)} %get-tuple-element.23), channel_id=1, source_target_pairs={{0,0},{4,4},{24,24},{28,28},{8,16},{12,20},{16,8},{20,12},{1,1},{5... | collective-permute-start | bytes 417800 | tf_op jit(solution)/shard_map/ppermute | solution.py:185
  19.9 7.0 %collective-permute-start.10 = (bf16[17,32,128]{2,1,0:T(8,128)(2,1)S(1)}, bf16[17,32,128]{2,1,0:T(8,128)(2,1)S(1)}, u32[]{:S(2)}, u32[]{:S(2)}) collective-permute-start(bf16[17,32,128]{2,1,0:T(8,128)(2,1)S(1)} %finish.2.refs_0_), channel_id=1, source_target_pairs={{0,3},{1,2},{2,1},{3,0},{4,7},{5,6},{6,5},{7,4},{8,11},{9,10},{10,... | collective-permute-start | bytes 417800 | tf_op jit(solution)/shard_map/ppermute | solution.py:41
  22.2 12.0 %collective-permute-start.9 = (bf16[17,32,128]{2,1,0:T(8,128)(2,1)S(1)}, bf16[17,32,128]{2,1,0:T(8,128)(2,1)S(1)}, u32[]{:S(2)}, u32[]{:S(2)}) collective-permute-start(bf16[17,32,128]{2,1,0:T(8,128)(2,1)S(1)} %finish.2.refs_0_), channel_id=1, source_target_pairs={{0,2},{1,3},{2,0},{3,1},{4,6},{5,7},{6,4},{7,5},{8,10},{9,11},{10,... | collective-permute-start | bytes 417800 | tf_op jit(solution)/shard_map/ppermute | solution.py:41
  22.2 12.0 %collective-permute-start.8 = (bf16[17,32,128]{2,1,0:T(8,128)(2,1)S(1)}, bf16[17,32,128]{2,1,0:T(8,128)(2,1)S(1)}, u32[]{:S(2)}, u32[]{:S(2)}) collective-permute-start(bf16[17,32,128]{2,1,0:T(8,128)(2,1)S(1)} %finish.2.refs_0_), channel_id=1, source_target_pairs={{0,1},{1,0},{2,3},{3,2},{4,5},{5,4},{6,7},{7,6},{8,9},{9,8},{10,11... | collective-permute-start | bytes 417800 | tf_op jit(solution)/shard_map/ppermute | solution.py:41
  34.9 3.5 %collective-permute-start.11 = (bf16[16,32,128]{2,1,0:T(8,128)(2,1)S(1)}, bf16[16,32,128]{2,1,0:T(8,128)(2,1)S(1)}, u32[]{:S(2)}, u32[]{:S(2)}) collective-permute-start(bf16[16,32,128]{2,1,0:T(8,128)(2,1)S(1)} %get-tuple-element.25), channel_id=1, source_target_pairs={{0,8},{8,0},{16,24},{24,16},{1,9},{9,1},{17,25},{25,17},{2,10},{10... | collective-permute-start | bytes 393224 | tf_op jit(solution)/shard_map/ppermute | solution.py:186
  36.4 5.0 %collective-permute-start.12 = (bf16[16,32,128]{2,1,0:T(8,128)(2,1)S(1)}, bf16[16,32,128]{2,1,0:T(8,128)(2,1)S(1)}, u32[]{:S(2)}, u32[]{:S(2)}) collective-permute-start(bf16[16,32,128]{2,1,0:T(8,128)(2,1)S(1)} %get-tuple-element.27), channel_id=1, source_target_pairs={{8,16},{12,20},{0,4},{24,28},{16,8},{20,12},{4,0},{28,24},{9,17},{... | collective-permute-start | bytes 393224 | tf_op jit(solution)/shard_map/ppermute | solution.py:185

commit v5 on v4

--- a/solution.py
+++ b/solution.py
@@ -9,6 +9,9 @@
 
 VMEM_BYTES = 12 << 20
 VMEM = pltpu.VMEM
+SENT = (2, 1)
+IDLE = (True, False)
+NEAR_FIRST = (True, False)
 
 
 def call(kernel, name, out_shape, *operands, stored=(), scratch=(), flops=0):
@@ -66,8 +69,8 @@
 
 
 def prepare_kernel(*refs):
-    stored, (_, first_taps, second_taps, first_bias, second_bias, own), refs = refs[:5], refs[5:11], refs[11:]
-    copies, first_ref, second_ref, *bias_refs = refs
+    stored = refs[:5]
+    first_taps, second_taps, first_bias, second_bias, own, copies, first_ref, second_ref, *bias_refs = refs[-10:]
     moves = [
         pltpu.make_async_copy(source, target, copies.at[i])
         for i, (source, target) in enumerate(zip(stored, (first_ref, second_ref, *bias_refs, own)))
@@ -118,9 +121,10 @@
                 out[y + i] = total.astype(out.dtype)
 
 
-def beside_kernel(count, halo, taps_ref, *refs):
-    (far_ref, near_ref, volume), refs = refs[-3:], refs[:-3]
-    blocks, halos = refs[:count], refs[count:]
+def beside_kernel(count, halo, steps, sent, taps_ref, *refs):
+    blocks, refs = refs[:count], refs[count:]
+    outs, volume = refs[-1 - sent : -1], refs[-1]
+    halos = refs[: -1 - sent]
     rows, part, depth = blocks[0].shape
     place, low = lax.axis_index("ch"), lax.axis_index("gy") == 0
     if sides() == 1:
@@ -133,8 +137,8 @@
         source = jnp.bitwise_xor(place, step % count)
         return pl.ds(pl.multiple_of(source * part, part), part)
 
-    for step in range(count):
-        volume[pl.ds(own, rows), channels(step), :] = blocks[step][...]
+    for step, block in zip(steps, blocks):
+        volume[pl.ds(own, rows), channels(step), :] = block[...]
     step = 0
     for ref in halos:
         for first in range(0, ref.shape[0], halo):
@@ -144,12 +148,11 @@
                 at = 0 if step < count else halo + rows
             volume[pl.ds(at, halo), channels(step), :] = ref[first : first + halo]
             step += 1
-    span = 3 * far_ref.shape[1]
-    terms(taps_ref[: 2 * span], volume, (0, 1), (far_ref, near_ref))
-
-
-def center_kernel(taps_ref, volume, center_ref):
-    terms(taps_ref[6 * center_ref.shape[1] :], volume, (0,), (center_ref,))
+    terms(taps_ref[: 3 * sent * outs[0].shape[1]], volume, range(sent), outs)
+
+
+def center_kernel(taps_ref, volume, *outs):
+    terms(taps_ref[3 * (3 - len(outs)) * outs[0].shape[1] :], volume, range(len(outs)), outs)
 
 
 def finish_kernel(near_ref, center_ref, far_ref, bias_ref, out_ref):
@@ -166,36 +169,37 @@
             out_ref[row] = jnp.where(jnp.full(kept.shape, outside), 0.0, kept)
 
 
-def layer(blocks, halos, halo, rows, taps, bias, kernel, out_type, idle):
+def layer(blocks, steps, halos, halo, rows, taps, bias, kernel, out_type, last):
     count = len(blocks)
     _, part, depth = blocks[0].shape
     outputs = taps.shape[0] // 9
     flops = 2 * rows * depth * taps.shape[0] * taps.shape[1]
     side = VMEM((rows, outputs, depth), jnp.bfloat16)
-    far, near, volume = call(
-        functools.partial(beside_kernel, count, halo),
+    side = VMEM((rows, outputs, depth), jnp.bfloat16)
+    sent = SENT[last]
+    *outs, volume = call(
+        functools.partial(beside_kernel, count, halo, steps, sent),
         "beside",
-        [side, side, VMEM((rows + 2, part * count, depth), jnp.bfloat16)],
+        [side] * sent + [VMEM((rows + 2, part * count, depth), jnp.bfloat16)],
         taps,
         *blocks,
         *halos,
-        flops=2 * flops // 3,
+        flops=sent * flops // 3,
     )
     planes = lax.axis_size("gx")
-    far = lax.ppermute(far, ("gx", "gy"), far_pairs(idle))
-    near = lax.ppermute(near, "gx", [(i, i ^ 1) for i in range(planes)])
-    (center,) = call(
-        center_kernel, "center", [VMEM((rows, outputs, depth), jnp.float32)], taps, volume, flops=flops // 3
-    )
-    (out,) = call(
-        kernel,
-        "finish",
-        [out_type((rows, outputs, depth), jnp.bfloat16)],
-        near,
-        center,
-        far,
-        bias,
-    )
+    far = lax.ppermute(outs[0], ("gx", "gy"), far_pairs(IDLE[last]))
+    outs += call(
+        center_kernel,
+        "center",
+        [side] * (2 - sent) + [VMEM((rows, outputs, depth), jnp.float32)],
+        taps,
+        volume,
+        flops=(3 - sent) * flops // 3,
+    )
+    center = outs[2]
+    near = lax.ppermute(outs[1], "gx", [(i, i ^ 1) for i in range(planes)])
+    both = (near, center, far) if NEAR_FIRST[last] else (far, center, near)
+    (out,) = call(kernel, "finish", [out_type((rows, outputs, depth), jnp.bfloat16)], *both, bias)
     return out
 
 
@@ -232,13 +236,15 @@
         inner = (place == 1) | (place == 2)
         handed = lax.ppermute(jnp.where(inner, last, own), "ch", [(0, 2), (3, 1), (1, 0), (2, 3)])
         others = [nearest, handed, last]
-        pair, _ = lax.optimization_barrier((jnp.concatenate(halos, axis=0), last))
+        pair = jnp.concatenate(halos, axis=0)
+        pair, _ = lax.optimization_barrier((pair, last))
         halos = [pair, lax.ppermute(pair, "ch", pairings[2])]
     hidden = layer(
-        [own, *others], halos, 2, rows + sides(), first_taps, first_bias, hidden_kernel, VMEM, True
-    )
-    blocks = [hidden, *channel_swaps(hidden)]
-    out = layer(blocks, [], 0, rows, second_taps, second_bias, finish_kernel, jax.ShapeDtypeStruct, False)
+        [own, *others], [*range(count)], halos, 2, rows + sides(), first_taps, first_bias, hidden_kernel, VMEM, 0
+    )
+    order = sorted(range(1, count), key=lambda step: (step != count - 1, step))
+    blocks = [hidden] + [lax.ppermute(hidden, "ch", pairings[step]) for step in order]
+    out = layer(blocks, [0, *order], [], 0, rows, second_taps, second_bias, finish_kernel, jax.ShapeDtypeStruct, 1)
     return out[None]
 
 

time: 42.3 us -> 40.1 us (0.948)
  the two profiles are of different devices: /device:TPU:0 before, /device:TPU:1 now
where the time goes in v5:
time: 40.1 us; the launch traced here: 39.9 us
  starting transfers between devices  18.1 us (45%)
  waiting for transfers between devices  16.3 us (41%)
  Pallas kernels  4.63 us (12%)
  local copies, waits for them, and re-layouts  0.75 us (2%)
    ppermute x1, waiting for transfers between devices, per_device(): halos = [pair, lax.ppermute(pair, 'ch', pairings[2])]  5.59 us
    ppermute x3, waiting for transfers between devices, per_device(): lax.ppermute(hidden, 'ch', pairings[step])  5.14 us
    ppermute x2, waiting for transfers between devices, layer(): far = lax.ppermute(outs[0], ('gx', 'gy'), far_pairs(IDLE[last]))  5 us
    ppermute x2, starting transfers between devices, layer(): far = lax.ppermute(outs[0], ('gx', 'gy'), far_pairs(IDLE[last]))  4.99 us
    pallas_call x7, Pallas kernels, call(): pl.pallas_call(kernel, out_shape=out_shape, in_specs=[pl.BlockSpec(memory...  4.63 us
    ppermute x1, starting transfers between devices, per_device(): last = lax.ppermute(density, 'ch', pairings[-1])  4.15 us
    ppermute x3, starting transfers between devices, per_device(): lax.ppermute(hidden, 'ch', pairings[step])  3.61 us
    ppermute x1, starting transfers between devices, per_device(): halos = [pair, lax.ppermute(pair, 'ch', pairings[2])]  1.44 us
  transfers between devices with their start and end apart: 13, of which 6 were waited for; matrix products, arithmetic and copies ran while one was open for 2% of the time, Pallas kernels for 6%

profile of v5, /device:TPU:1, one launch (start us, length us, event | category | flops | bytes accessed | tf_op | source)
XLA Modules:
  0.0 39.9 jit_solution(13361381382148497583)
XLA Ops:
  0.0 4.2 %collective-permute-start.2 = (bf16[16,32,128]{2,1,0:T(8,128)(2,1)}, bf16[16,32,128]{2,1,0:T(8,128)(2,1)S(1)}, u32[]{:S(2)}, u32[]{:S(2)}) collective-permute-start(bf16[16,32,128]{2,1,0:T(8,128)(2,1)} %bitcast.6), channel_id=1, source_target_pairs={{0,3},{1,2},{2,1},{3,0},{4,7},{5,6},{6,5},{7,4},{8,11},{9,10},{10,... | collective-permute-start | bytes 393224 | tf_op jit(solution)/shard_map/ppermute | solution.py:215
  4.2 0.8 %dynamic-slice_bitcast_fusion = bf16[2,32,128]{2,1,0:T(8,128)(2,1)S(1)} fusion(bf16[1,16,32,128]{3,2,1,0:T(8,128)(2,1)} %param.5, s32[]{:T(128)S(6)} %select_n.13), kind=kLoop, calls=%fused_computation.2 | loop fusion | bytes 32772 | tf_op jit(solution)/shard_map/dynamic_slice | solution.py:214
  4.9 1.2 %collective-permute-start = (bf16[2,32,128]{2,1,0:T(8,128)(2,1)S(1)}, bf16[2,32,128]{2,1,0:T(8,128)(2,1)S(1)}, u32[]{:S(2)}, u32[]{:S(2)}) collective-permute-start(bf16[2,32,128]{2,1,0:T(8,128)(2,1)S(1)} %dynamic-slice_bitcast_fusion), channel_id=1, source_target_pairs={{0,4},{1,5},{2,6},{3,7},{4,0},{5,1},{6,2},{7,3},{8,12},{9,13},{10,... | collective-permute-start | bytes 49160 | tf_op jit(solution)/shard_map/ppermute | solution.py:54
  6.1 0.0 collective-permute-start.4
  6.1 1.4 %collective-permute-start.1 = (bf16[16,32,128]{2,1,0:T(8,128)(2,1)}, bf16[16,32,128]{2,1,0:T(8,128)(2,1)S(1)}, u32[]{:S(2)}, u32[]{:S(2)}) collective-permute-start(bf16[16,32,128]{2,1,0:T(8,128)(2,1)} %bitcast.7), channel_id=1, source_target_pairs={{0,1},{1,0},{2,3},{3,2},{4,5},{5,4},{6,7},{7,6},{8,9},{9,8},{10,11... | collective-permute-start | bytes 393224 | tf_op jit(solution)/shard_map/ppermute | solution.py:216
  7.6 0.2 collective-permute-done.refs_5_
  7.8 1.4 %prepare.1 = (bf16[288,384]{1,0:T(8,128)(2,1)S(1)}, bf16[288,384]{1,0:T(8,128)(2,1)S(1)}, f32[32,128]{1,0:T(8,128)S(1)}, f32[32,128]{1,0:T(8,128)S(1)}, bf16[16,32,128]{2,1,0:T(8,128)(2,1)S(1)}) custom-call(bf16[3,3,3,32,128]{4,3,2,1,0:T(8,128)(2,1)} %refs_0_.1, bf16[3,3,3,32,128]{4,3,2,1,0:T(8,128)(2,1)} %refs_1_.1, f32[1,32]{1,0:T(1,128)} %bitcast.9, ...), custom_call_target="tpu_custom_call" | custom-call | tf_op jit(solution)/shard_map/prepare/pallas_call | solution.py:19
  9.2 0.0 collective-permute-done.2.refs_3_
  9.2 0.1 collective-permute-start.3
  9.3 0.3 collective-permute-done.4
  9.6 1.4 %collective-permute-start.5 = (bf16[4,32,128]{2,1,0:T(8,128)(2,1)S(1)}, bf16[4,32,128]{2,1,0:T(8,128)(2,1)S(1)}, u32[]{:S(2)}, u32[]{:S(2)}) collective-permute-start(bf16[4,32,128]{2,1,0:T(8,128)(2,1)S(1)} %pad_maximum_fusion.refs_4_), channel_id=1, source_target_pairs={{0,2},{1,3},{2,0},{3,1},{4,6},{5,7},{6,4},{7,5},{8,10},{9,11},{10,... | collective-permute-start | bytes 98312 | tf_op jit(solution)/shard_map/ppermute | solution.py:241
  11.0 0.0 collective-permute-done.1.refs_1_
  11.1 5.6 %collective-permute-done.5.refs_5_ = bf16[4,32,128]{2,1,0:T(8,128)(2,1)S(1)} collective-permute-done((bf16[4,32,128]{2,1,0:T(8,128)(2,1)S(1)}, bf16[4,32,128]{2,1,0:T(8,128)(2,1)S(1)}, u32[]{:S(2)}, u32[]{:S(2)}) %collective-permute-start.5) | collective-permute-done | bytes 32800 | tf_op jit(solution)/shard_map/ppermute | solution.py:241
  16.6 0.0 collective-permute-done.3.refs_2_
  16.6 0.8 %beside.2 = (bf16[17,32,128]{2,1,0:T(8,128)(2,1)S(1)}, bf16[17,32,128]{2,1,0:T(8,128)(2,1)S(1)}, bf16[19,128,128]{2,1,0:T(8,128)(2,1)S(1)}) custom-call(bf16[288,384]{1,0:T(8,128)(2,1)S(1)} %get-tuple-element.19.taps_ref, bf16[16,32,128]{2,1,0:T(8,128)(2,1)S(1)} %get-tuple-element.20.refs_0_, bf16[16,32,128]{2,1,0:T(8,128)(2,1)S(1)} %collective-permute-done.1.refs_1_, ...), custom_call_target="tpu_custom_call" | custom-call | flops 320864256 | tf_op jit(solution)/shard_map/beside/pallas_call | solution.py:19
  17.4 1.1 %collective-permute-start.6 = (bf16[17,32,128]{2,1,0:T(8,128)(2,1)S(1)}, bf16[17,32,128]{2,1,0:T(8,128)(2,1)S(1)}, u32[]{:S(2)}, u32[]{:S(2)}) collective-permute-start(bf16[17,32,128]{2,1,0:T(8,128)(2,1)S(1)} %get-tuple-element.22), channel_id=1, source_target_pairs={{0,8},{8,0},{16,24},{24,16},{1,9},{9,1},{17,25},{25,17},{2,10},{10... | collective-permute-start | bytes 417800 | tf_op jit(solution)/shard_map/ppermute | solution.py:200
  18.5 3.0 %collective-permute-start.7 = (bf16[17,32,128]{2,1,0:T(8,128)(2,1)S(1)}, bf16[17,32,128]{2,1,0:T(8,128)(2,1)S(1)}, u32[]{:S(2)}, u32[]{:S(2)}) collective-permute-start(bf16[17,32,128]{2,1,0:T(8,128)(2,1)S(1)} %get-tuple-element.24), channel_id=1, source_target_pairs={{0,0},{4,4},{24,24},{28,28},{8,16},{12,20},{16,8},{20,12},{1,1},{5... | collective-permute-start | bytes 417800 | tf_op jit(solution)/shard_map/ppermute | solution.py:190
  21.6 0.5 %center.2.center_ref = f32[17,32,128]{2,1,0:T(8,128)S(1)} custom-call(bf16[288,384]{1,0:T(8,128)(2,1)S(1)} %get-tuple-element.19.taps_ref, bf16[19,128,128]{2,1,0:T(8,128)(2,1)S(1)} %get-tuple-element.23.volume), custom_call_target="tpu_custom_call" | custom-call | flops 160432128 | tf_op jit(solution)/shard_map/center/pallas_call | solution.py:19
  22.1 0.0 collective-permute-done.6.near_ref
  22.1 3.1 %collective-permute-done.7.far_ref = bf16[17,32,128]{2,1,0:T(8,128)(2,1)S(1)} collective-permute-done((bf16[17,32,128]{2,1,0:T(8,128)(2,1)S(1)}, bf16[17,32,128]{2,1,0:T(8,128)(2,1)S(1)}, u32[]{:S(2)}, u32[]{:S(2)}) %collective-permute-start.7) | collective-permute-done | bytes 139296 | tf_op jit(solution)/shard_map/ppermute | solution.py:190
  25.2 0.1 finish.2.refs_0_
  25.3 0.8 %collective-permute-start.10 = (bf16[17,32,128]{2,1,0:T(8,128)(2,1)S(1)}, bf16[17,32,128]{2,1,0:T(8,128)(2,1)S(1)}, u32[]{:S(2)}, u32[]{:S(2)}) collective-permute-start(bf16[17,32,128]{2,1,0:T(8,128)(2,1)S(1)} %finish.2.refs_0_), channel_id=1, source_target_pairs={{0,2},{1,3},{2,0},{3,1},{4,6},{5,7},{6,4},{7,5},{8,10},{9,11},{10,... | collective-permute-start | bytes 417800 | tf_op jit(solution)/shard_map/ppermute | solution.py:246
  26.1 1.4 %collective-permute-start.9 = (bf16[17,32,128]{2,1,0:T(8,128)(2,1)S(1)}, bf16[17,32,128]{2,1,0:T(8,128)(2,1)S(1)}, u32[]{:S(2)}, u32[]{:S(2)}) collective-permute-start(bf16[17,32,128]{2,1,0:T(8,128)(2,1)S(1)} %finish.2.refs_0_), channel_id=1, source_target_pairs={{0,1},{1,0},{2,3},{3,2},{4,5},{5,4},{6,7},{7,6},{8,9},{9,8},{10,11... | collective-permute-start | bytes 417800 | tf_op jit(solution)/shard_map/ppermute | solution.py:246
  27.5 1.4 %collective-permute-start.8 = (bf16[17,32,128]{2,1,0:T(8,128)(2,1)S(1)}, bf16[17,32,128]{2,1,0:T(8,128)(2,1)S(1)}, u32[]{:S(2)}, u32[]{:S(2)}) collective-permute-start(bf16[17,32,128]{2,1,0:T(8,128)(2,1)S(1)} %finish.2.refs_0_), channel_id=1, source_target_pairs={{0,3},{1,2},{2,1},{3,0},{4,7},{5,6},{6,5},{7,4},{8,11},{9,10},{10,... | collective-permute-start | bytes 417800 | tf_op jit(solution)/shard_map/ppermute | solution.py:246
  28.9 5.1 %collective-permute-done.10.refs_3_ = bf16[17,32,128]{2,1,0:T(8,128)(2,1)S(1)} collective-permute-done((bf16[17,32,128]{2,1,0:T(8,128)(2,1)S(1)}, bf16[17,32,128]{2,1,0:T(8,128)(2,1)S(1)}, u32[]{:S(2)}, u32[]{:S(2)}) %collective-permute-start.10) | collective-permute-done | bytes 139296 | tf_op jit(solution)/shard_map/ppermute | solution.py:246
  34.0 0.0 collective-permute-done.9.refs_2_
  34.0 0.0 collective-permute-done.8.refs_1_
  34.0 0.6 %beside.3 = (bf16[16,32,128]{2,1,0:T(8,128)(2,1)S(1)}, bf16[18,128,128]{2,1,0:T(8,128)(2,1)S(1)}) custom-call(bf16[288,384]{1,0:T(8,128)(2,1)S(1)} %get-tuple-element.18.taps_ref, bf16[17,32,128]{2,1,0:T(8,128)(2,1)S(1)} %finish.2.refs_0_, bf16[17,32,128]{2,1,0:T(8,128)(2,1)S(1)} %collective-permute-done.8.refs_1_, ...), custom_call_target="tpu_custom_call" | custom-call | flops 150994944 | tf_op jit(solution)/shard_map/beside/pallas_call | solution.py:19
  34.6 1.9 %collective-permute-start.11 = (bf16[16,32,128]{2,1,0:T(8,128)(2,1)S(1)}, bf16[16,32,128]{2,1,0:T(8,128)(2,1)S(1)}, u32[]{:S(2)}, u32[]{:S(2)}) collective-permute-start(bf16[16,32,128]{2,1,0:T(8,128)(2,1)S(1)} %get-tuple-element.26), channel_id=1, source_target_pairs={{8,16},{12,20},{0,4},{24,28},{16,8},{20,12},{4,0},{28,24},{9,17},{... | collective-permute-start | bytes 393224 | tf_op jit(solution)/shard_map/ppermute | solution.py:190
  36.5 0.7 %center.3 = (bf16[16,32,128]{2,1,0:T(8,128)(2,1)S(1)}, f32[16,32,128]{2,1,0:T(8,128)S(1)}) custom-call(bf16[288,384]{1,0:T(8,128)(2,1)S(1)} %get-tuple-element.18.taps_ref, bf16[18,128,128]{2,1,0:T(8,128)(2,1)S(1)} %get-tuple-element.27.volume), custom_call_target="tpu_custom_call" | custom-call | flops 301989888 | tf_op jit(solution)/shard_map/center/pallas_call | solution.py:19
  37.2 0.1 collective-permute-start.12
  37.3 1.9 %collective-permute-done.11.near_ref = bf16[16,32,128]{2,1,0:T(8,128)(2,1)S(1)} collective-permute-done((bf16[16,32,128]{2,1,0:T(8,128)(2,1)S(1)}, bf16[16,32,128]{2,1,0:T(8,128)(2,1)S(1)}, u32[]{:S(2)}, u32[]{:S(2)}) %collective-permute-start.11) | collective-permute-done | bytes 131104 | tf_op jit(solution)/shard_map/ppermute | solution.py:190
  39.2 0.0 collective-permute-done.12.far_ref
  39.2 0.7 %finish.3 = bf16[16,32,128]{2,1,0:T(8,128)(2,1)} custom-call(bf16[16,32,128]{2,1,0:T(8,128)(2,1)S(1)} %collective-permute-done.11.near_ref, f32[16,32,128]{2,1,0:T(8,128)S(1)} %get-tuple-element.28.center_ref, bf16[16,32,128]{2,1,0:T(8,128)(2,1)S(1)} %collective-permute-done.12.far_ref, f32[32,128]{1,0:T(8,128)S(1)} %get-tuple-element.30.bias_ref), custom_call_target="tpu_custom_call" | custom-call | tf_op jit(solution)/shard_map/finish/pallas_call | solution.py:19
  (2 shorter events, 0.0 us)
Async XLA Ops:
  0.0 9.2 %collective-permute-start.2 = (bf16[16,32,128]{2,1,0:T(8,128)(2,1)}, bf16[16,32,128]{2,1,0:T(8,128)(2,1)S(1)}, u32[]{:S(2)}, u32[]{:S(2)}) collective-permute-start(bf16[16,32,128]{2,1,0:T(8,128)(2,1)} %bitcast.6), channel_id=1, source_target_pairs={{0,3},{1,2},{2,1},{3,0},{4,7},{5,6},{6,5},{7,4},{8,11},{9,10},{10,... | collective-permute-start | bytes 393224 | tf_op jit(solution)/shard_map/ppermute | solution.py:215
  4.9 2.9 %collective-permute-start = (bf16[2,32,128]{2,1,0:T(8,128)(2,1)S(1)}, bf16[2,32,128]{2,1,0:T(8,128)(2,1)S(1)}, u32[]{:S(2)}, u32[]{:S(2)}) collective-permute-start(bf16[2,32,128]{2,1,0:T(8,128)(2,1)S(1)} %dynamic-slice_bitcast_fusion), channel_id=1, source_target_pairs={{0,4},{1,5},{2,6},{3,7},{4,0},{5,1},{6,2},{7,3},{8,12},{9,13},{10,... | collective-permute-start | bytes 49160 | tf_op jit(solution)/shard_map/ppermute | solution.py:54
  6.1 3.5 %collective-permute-start.4 = (bf16[2,32,128]{2,1,0:T(8,128)(2,1)S(1)}, bf16[2,32,128]{2,1,0:T(8,128)(2,1)S(1)}, u32[]{:S(2)}, u32[]{:S(2)}) collective-permute-start(bf16[2,32,128]{2,1,0:T(8,128)(2,1)S(1)} %dynamic-slice_bitcast_fusion), channel_id=1, source_target_pairs={{0,5},{1,4},{2,7},{3,6},{4,1},{5,0},{6,3},{7,2},{8,13},{9,12},{10,... | collective-permute-start | bytes 49160 | tf_op jit(solution)/shard_map/ppermute | solution.py:54
  6.1 4.9 %collective-permute-start.1 = (bf16[16,32,128]{2,1,0:T(8,128)(2,1)}, bf16[16,32,128]{2,1,0:T(8,128)(2,1)S(1)}, u32[]{:S(2)}, u32[]{:S(2)}) collective-permute-start(bf16[16,32,128]{2,1,0:T(8,128)(2,1)} %bitcast.7), channel_id=1, source_target_pairs={{0,1},{1,0},{2,3},{3,2},{4,5},{5,4},{6,7},{7,6},{8,9},{9,8},{10,11... | collective-permute-start | bytes 393224 | tf_op jit(solution)/shard_map/ppermute | solution.py:216
  9.2 7.4 %collective-permute-start.3 = (bf16[16,32,128]{2,1,0:T(8,128)(2,1)S(1)}, bf16[16,32,128]{2,1,0:T(8,128)(2,1)S(1)}, u32[]{:S(2)}, u32[]{:S(2)}) collective-permute-start(bf16[16,32,128]{2,1,0:T(8,128)(2,1)S(1)} %broadcast_select_fusion), channel_id=1, source_target_pairs={{0,2},{3,1},{1,0},{2,3},{4,6},{7,5},{5,4},{6,7},{8,10},{11,9},{9,8... | collective-permute-start | bytes 393224 | tf_op jit(solution)/shard_map/ppermute | solution.py:237
  9.6 7.0 %collective-permute-start.5 = (bf16[4,32,128]{2,1,0:T(8,128)(2,1)S(1)}, bf16[4,32,128]{2,1,0:T(8,128)(2,1)S(1)}, u32[]{:S(2)}, u32[]{:S(2)}) collective-permute-start(bf16[4,32,128]{2,1,0:T(8,128)(2,1)S(1)} %pad_maximum_fusion.refs_4_), channel_id=1, source_target_pairs={{0,2},{1,3},{2,0},{3,1},{4,6},{5,7},{6,4},{7,5},{8,10},{9,11},{10,... | collective-permute-start | bytes 98312 | tf_op jit(solution)/shard_map/ppermute | solution.py:241
  17.4 4.7 %collective-permute-start.6 = (bf16[17,32,128]{2,1,0:T(8,128)(2,1)S(1)}, bf16[17,32,128]{2,1,0:T(8,128)(2,1)S(1)}, u32[]{:S(2)}, u32[]{:S(2)}) collective-permute-start(bf16[17,32,128]{2,1,0:T(8,128)(2,1)S(1)} %get-tuple-element.22), channel_id=1, source_target_pairs={{0,8},{8,0},{16,24},{24,16},{1,9},{9,1},{17,25},{25,17},{2,10},{10... | collective-permute-start | bytes 417800 | tf_op jit(solution)/shard_map/ppermute | solution.py:200
  18.5 6.7 %collective-permute-start.7 = (bf16[17,32,128]{2,1,0:T(8,128)(2,1)S(1)}, bf16[17,32,128]{2,1,0:T(8,128)(2,1)S(1)}, u32[]{:S(2)}, u32[]{:S(2)}) collective-permute-start(bf16[17,32,128]{2,1,0:T(8,128)(2,1)S(1)} %get-tuple-element.24), channel_id=1, source_target_pairs={{0,0},{4,4},{24,24},{28,28},{8,16},{12,20},{16,8},{20,12},{1,1},{5... | collective-permute-start | bytes 417800 | tf_op jit(solution)/shard_map/ppermute | solution.py:190
  25.3 8.7 %collective-permute-start.10 = (bf16[17,32,128]{2,1,0:T(8,128)(2,1)S(1)}, bf16[17,32,128]{2,1,0:T(8,128)(2,1)S(1)}, u32[]{:S(2)}, u32[]{:S(2)}) collective-permute-start(bf16[17,32,128]{2,1,0:T(8,128)(2,1)S(1)} %finish.2.refs_0_), channel_id=1, source_target_pairs={{0,2},{1,3},{2,0},{3,1},{4,6},{5,7},{6,4},{7,5},{8,10},{9,11},{10,... | collective-permute-start | bytes 417800 | tf_op jit(solution)/shard_map/ppermute | solution.py:246
  26.1 7.9 %collective-permute-start.9 = (bf16[17,32,128]{2,1,0:T(8,128)(2,1)S(1)}, bf16[17,32,128]{2,1,0:T(8,128)(2,1)S(1)}, u32[]{:S(2)}, u32[]{:S(2)}) collective-permute-start(bf16[17,32,128]{2,1,0:T(8,128)(2,1)S(1)} %finish.2.refs_0_), channel_id=1, source_target_pairs={{0,1},{1,0},{2,3},{3,2},{4,5},{5,4},{6,7},{7,6},{8,9},{9,8},{10,11... | collective-permute-start | bytes 417800 | tf_op jit(solution)/shard_map/ppermute | solution.py:246
  27.5 6.5 %collective-permute-start.8 = (bf16[17,32,128]{2,1,0:T(8,128)(2,1)S(1)}, bf16[17,32,128]{2,1,0:T(8,128)(2,1)S(1)}, u32[]{:S(2)}, u32[]{:S(2)}) collective-permute-start(bf16[17,32,128]{2,1,0:T(8,128)(2,1)S(1)} %finish.2.refs_0_), channel_id=1, source_target_pairs={{0,3},{1,2},{2,1},{3,0},{4,7},{5,6},{6,5},{7,4},{8,11},{9,10},{10,... | collective-permute-start | bytes 417800 | tf_op jit(solution)/shard_map/ppermute | solution.py:246
  34.6 4.6 %collective-permute-start.11 = (bf16[16,32,128]{2,1,0:T(8,128)(2,1)S(1)}, bf16[16,32,128]{2,1,0:T(8,128)(2,1)S(1)}, u32[]{:S(2)}, u32[]{:S(2)}) collective-permute-start(bf16[16,32,128]{2,1,0:T(8,128)(2,1)S(1)} %get-tuple-element.26), channel_id=1, source_target_pairs={{8,16},{12,20},{0,4},{24,28},{16,8},{20,12},{4,0},{28,24},{9,17},{... | collective-permute-start | bytes 393224 | tf_op jit(solution)/shard_map/ppermute | solution.py:190
  37.2 2.0 %collective-permute-start.12 = (bf16[16,32,128]{2,1,0:T(8,128)(2,1)S(1)}, bf16[16,32,128]{2,1,0:T(8,128)(2,1)S(1)}, u32[]{:S(2)}, u32[]{:S(2)}) collective-permute-start(bf16[16,32,128]{2,1,0:T(8,128)(2,1)S(1)} %get-tuple-element.29), channel_id=1, source_target_pairs={{0,8},{8,0},{16,24},{24,16},{1,9},{9,1},{17,25},{25,17},{2,10},{10... | collective-permute-start | bytes 393224 | tf_op jit(solution)/shard_map/ppermute | solution.py:200

commit v6 on v5

--- a/solution.py
+++ b/solution.py
@@ -40,8 +40,18 @@
     return [[(i, i ^ step) for i in range(count)] for step in range(count)]
 
 
-def channel_swaps(block):
-    return [lax.ppermute(block, "ch", pairs) for pairs in partners()[1:]]
+def swapped(step):
+    return lambda place: jnp.bitwise_xor(place, step)
+
+
+def passed(step):
+    count = lax.axis_size("ch")
+    return lambda place: lax.rem(place + (count - step) % count, count)
+
+
+def round_ch(block, step):
+    count = lax.axis_size("ch")
+    return lax.ppermute(block, "ch", [(i, (i + step) % count) for i in range(count)])
 
 
 def edge_moves(edge, step, pairings):
@@ -121,7 +131,7 @@
                 out[y + i] = total.astype(out.dtype)
 
 
-def beside_kernel(count, halo, steps, sent, taps_ref, *refs):
+def beside_kernel(count, halo, sources, sent, taps_ref, *refs):
     blocks, refs = refs[:count], refs[count:]
     outs, volume = refs[-1 - sent : -1], refs[-1]
     halos = refs[: -1 - sent]
@@ -133,21 +143,15 @@
         volume[outside] = jnp.zeros((part * count, depth), volume.dtype)
     else:
         own = halo
-    def channels(step):
-        source = jnp.bitwise_xor(place, step % count)
-        return pl.ds(pl.multiple_of(source * part, part), part)
-
-    for step, block in zip(steps, blocks):
-        volume[pl.ds(own, rows), channels(step), :] = block[...]
-    step = 0
-    for ref in halos:
-        for first in range(0, ref.shape[0], halo):
-            if sides() == 1:
-                at = beside
-            else:
-                at = 0 if step < count else halo + rows
-            volume[pl.ds(at, halo), channels(step), :] = ref[first : first + halo]
-            step += 1
+    def channels(source):
+        return pl.ds(pl.multiple_of(source(place) * part, part), part)
+
+    for source, block in zip(sources, blocks):
+        volume[pl.ds(own, rows), channels(source), :] = block[...]
+    edges = [ref.at[first : first + halo] for ref in halos for first in range(0, ref.shape[0], halo)]
+    for step, edge in enumerate(edges):
+        at = beside if sides() == 1 else 0 if step < count else halo + rows
+        volume[pl.ds(at, halo), channels(swapped(step % count)), :] = edge[...]
     terms(taps_ref[: 3 * sent * outs[0].shape[1]], volume, range(sent), outs)
 
 
@@ -169,7 +173,7 @@
             out_ref[row] = jnp.where(jnp.full(kept.shape, outside), 0.0, kept)
 
 
-def layer(blocks, steps, halos, halo, rows, taps, bias, kernel, out_type, last):
+def layer(blocks, sources, halos, halo, rows, taps, bias, kernel, out_type, last):
     count = len(blocks)
     _, part, depth = blocks[0].shape
     outputs = taps.shape[0] // 9
@@ -178,7 +182,7 @@
     side = VMEM((rows, outputs, depth), jnp.bfloat16)
     sent = SENT[last]
     *outs, volume = call(
-        functools.partial(beside_kernel, count, halo, steps, sent),
+        functools.partial(beside_kernel, count, halo, sources, sent),
         "beside",
         [side] * sent + [VMEM((rows + 2, part * count, depth), jnp.bfloat16)],
         taps,
@@ -209,14 +213,15 @@
     outputs = first_kernel.shape[3]
     count = lax.axis_size("ch")
     pairings = partners()
-    if sides() == 1:
+    one_sided = sides() == 1
+    if one_sided:
         start = jnp.where(lax.axis_index("gy") == 0, rows - 2, 0)
         halos = edge_moves(lax.dynamic_slice_in_dim(density, start, 2, 0), 1, pairings[:2])
-        last = lax.ppermute(density, "ch", pairings[-1])
-        nearest = lax.ppermute(density, "ch", pairings[1])
+        upward, downward = round_ch(density, 1), round_ch(density, -1)
     else:
         halos = edge_moves(density[-2:], 1, pairings) + edge_moves(density[:2], -1, pairings)
-        others = channel_swaps(density)
+        others = [lax.ppermute(density, "ch", pairs) for pairs in pairings[1:]]
+        sources = [swapped(step) for step in range(count)]
     taps_shape = VMEM((9 * outputs, 3 * part * count), jnp.bfloat16)
     bias_shape = VMEM((outputs, depth), jnp.float32)
     first_taps, second_taps, first_bias, second_bias, own = call(
@@ -231,20 +236,18 @@
             *[VMEM((1, outputs), jnp.float32)] * 2,
         ],
     )
-    if sides() == 1:
-        place = lax.axis_index("ch")
-        inner = (place == 1) | (place == 2)
-        handed = lax.ppermute(jnp.where(inner, last, own), "ch", [(0, 2), (3, 1), (1, 0), (2, 3)])
-        others = [nearest, handed, last]
-        pair = jnp.concatenate(halos, axis=0)
-        pair, _ = lax.optimization_barrier((pair, last))
+    if one_sided:
+        others = [downward, round_ch(upward, 1), upward]
+        sources = [passed(step) for step in (0, -1, 2, 1)]
+        pair, _ = lax.optimization_barrier((jnp.concatenate(halos, axis=0), upward))
         halos = [pair, lax.ppermute(pair, "ch", pairings[2])]
     hidden = layer(
-        [own, *others], [*range(count)], halos, 2, rows + sides(), first_taps, first_bias, hidden_kernel, VMEM, 0
+        [own, *others], sources, halos, 2, rows + sides(), first_taps, first_bias, hidden_kernel, VMEM, 0
     )
     order = sorted(range(1, count), key=lambda step: (step != count - 1, step))
     blocks = [hidden] + [lax.ppermute(hidden, "ch", pairings[step]) for step in order]
-    out = layer(blocks, [0, *order], [], 0, rows, second_taps, second_bias, finish_kernel, jax.ShapeDtypeStruct, 1)
+    sources = [swapped(step) for step in (0, *order)]
+    out = layer(blocks, sources, [], 0, rows, second_taps, second_bias, finish_kernel, jax.ShapeDtypeStruct, 1)
     return out[None]
 
 

time: 40.1 us -> 39.2 us (0.978)
  waiting for transfers between devices: 16.3 us -> 14.9 us
  starting transfers between devices: 18.1 us -> 18.6 us
    ppermute x1, waiting for transfers between devices: 5.59 us -> 3.48 us  [per_device(): halos = [pair, lax.ppermute(pair, 'ch', pairings[2])]]
    ppermute x2, starting transfers between devices: 1.2 us -> 2.99 us  [layer(): near = lax.ppermute(outs[1], 'gx', [(i, i ^ 1) for i in range(planes)])]
    ppermute x3, starting transfers between devices: 5.64 us -> 4.32 us  [round_ch(): lax.ppermute(block, 'ch', [(i, (i + step) % count) for i in range(count)])]
    ppermute x2, starting transfers between devices: 1.21 us -> 2.48 us  [edge_moves(): lax.ppermute(edge, ('gy', 'ch'), [(i * channels + c, j * channels + d) fo...]
    ppermute x1, starting transfers between devices: 1.44 us -> 0.28 us  [per_device(): halos = [pair, lax.ppermute(pair, 'ch', pairings[2])]]
    ppermute x2, waiting for transfers between devices: 0.58 us -> 1.22 us  [edge_moves(): lax.ppermute(edge, ('gy', 'ch'), [(i * channels + c, j * channels + d) fo...]
  transfers between devices with their start and end apart: 13 -> 13, of which waited for: 6 -> 5; matrix products, arithmetic and copies ran while one was open for 2% -> 2% of each run, Pallas kernels for 6% -> 6%
where the time goes in v6:
time: 39.2 us; the launch traced here: 39 us
  starting transfers between devices  18.6 us (47%)
  waiting for transfers between devices  14.9 us (38%)
  Pallas kernels  4.63 us (12%)
  local copies, waits for them, and re-layouts  0.75 us (2%)
    ppermute x3, waiting for transfers between devices, per_device(): lax.ppermute(hidden, 'ch', pairings[step])  5.22 us
    ppermute x2, starting transfers between devices, layer(): far = lax.ppermute(outs[0], ('gx', 'gy'), far_pairs(IDLE[last]))  4.94 us
    ppermute x2, waiting for transfers between devices, layer(): far = lax.ppermute(outs[0], ('gx', 'gy'), far_pairs(IDLE[last]))  4.92 us
    pallas_call x7, Pallas kernels, call(): pl.pallas_call(kernel, out_shape=out_shape, in_specs=[pl.BlockSpec(memory...  4.63 us
    ppermute x3, starting transfers between devices, round_ch(): lax.ppermute(block, 'ch', [(i, (i + step) % count) for i in range(count)])  4.32 us
    ppermute x3, starting transfers between devices, per_device(): lax.ppermute(hidden, 'ch', pairings[step])  3.61 us
    ppermute x1, waiting for transfers between devices, per_device(): halos = [pair, lax.ppermute(pair, 'ch', pairings[2])]  3.48 us
    ppermute x2, starting transfers between devices, layer(): near = lax.ppermute(outs[1], 'gx', [(i, i ^ 1) for i in range(planes)])  2.99 us
  transfers between devices with their start and end apart: 13, of which 5 were waited for; matrix products, arithmetic and copies ran while one was open for 2% of the time, Pallas kernels for 6%

profile of v6, /device:TPU:1, one launch (start us, length us, event | category | flops | bytes accessed | tf_op | source)
XLA Modules:
  0.0 39.0 jit_solution(8532245283966447989)
XLA Ops:
  0.0 2.1 %collective-permute-start.2 = (bf16[16,32,128]{2,1,0:T(8,128)(2,1)}, bf16[16,32,128]{2,1,0:T(8,128)(2,1)S(1)}, u32[]{:S(2)}, u32[]{:S(2)}) collective-permute-start(bf16[16,32,128]{2,1,0:T(8,128)(2,1)} %bitcast.6), channel_id=1, source_target_pairs={{0,1},{1,2},{2,3},{3,0},{4,5},{5,6},{6,7},{7,4},{8,9},{9,10},{10,1... | collective-permute-start | bytes 393224 | tf_op jit(solution)/shard_map/ppermute | solution.py:54
  2.1 0.8 %dynamic-slice_bitcast_fusion = bf16[2,32,128]{2,1,0:T(8,128)(2,1)S(1)} fusion(bf16[1,16,32,128]{3,2,1,0:T(8,128)(2,1)} %param.5, s32[]{:T(128)S(6)} %select_n.5), kind=kLoop, calls=%fused_computation.1 | loop fusion | bytes 32772 | tf_op jit(solution)/shard_map/dynamic_slice | solution.py:219
  2.9 2.2 %collective-permute-start.4 = (bf16[2,32,128]{2,1,0:T(8,128)(2,1)S(1)}, bf16[2,32,128]{2,1,0:T(8,128)(2,1)S(1)}, u32[]{:S(2)}, u32[]{:S(2)}) collective-permute-start(bf16[2,32,128]{2,1,0:T(8,128)(2,1)S(1)} %dynamic-slice_bitcast_fusion), channel_id=1, source_target_pairs={{0,5},{1,4},{2,7},{3,6},{4,1},{5,0},{6,3},{7,2},{8,13},{9,12},{10,... | collective-permute-start | bytes 49160 | tf_op jit(solution)/shard_map/ppermute | solution.py:64
  5.1 0.3 collective-permute-start
  5.4 2.2 %collective-permute-start.1 = (bf16[16,32,128]{2,1,0:T(8,128)(2,1)}, bf16[16,32,128]{2,1,0:T(8,128)(2,1)S(1)}, u32[]{:S(2)}, u32[]{:S(2)}) collective-permute-start(bf16[16,32,128]{2,1,0:T(8,128)(2,1)} %bitcast.7), channel_id=1, source_target_pairs={{0,3},{1,0},{2,1},{3,2},{4,7},{5,4},{6,5},{7,6},{8,11},{9,8},{10,9... | collective-permute-start | bytes 393224 | tf_op jit(solution)/shard_map/ppermute | solution.py:54
  7.6 0.0 collective-permute-done.2.refs_3_
  7.6 0.0 collective-permute-start.3
  7.6 1.2 %collective-permute-done.4 = bf16[2,32,128]{2,1,0:T(8,128)(2,1)S(1)} collective-permute-done((bf16[2,32,128]{2,1,0:T(8,128)(2,1)S(1)}, bf16[2,32,128]{2,1,0:T(8,128)(2,1)S(1)}, u32[]{:S(2)}, u32[]{:S(2)}) %collective-permute-start.4) | collective-permute-done | bytes 16416 | tf_op jit(solution)/shard_map/ppermute | solution.py:64
  8.8 0.0 collective-permute-done.refs_5_
  8.8 0.3 collective-permute-start.5
  9.1 1.4 %prepare.1 = (bf16[288,384]{1,0:T(8,128)(2,1)S(1)}, bf16[288,384]{1,0:T(8,128)(2,1)S(1)}, f32[32,128]{1,0:T(8,128)S(1)}, f32[32,128]{1,0:T(8,128)S(1)}, bf16[16,32,128]{2,1,0:T(8,128)(2,1)S(1)}) custom-call(bf16[3,3,3,32,128]{4,3,2,1,0:T(8,128)(2,1)} %refs_0_.1, bf16[3,3,3,32,128]{4,3,2,1,0:T(8,128)(2,1)} %refs_1_.1, f32[1,32]{1,0:T(1,128)} %bitcast.9, ...), custom_call_target="tpu_custom_call" | custom-call | tf_op jit(solution)/shard_map/prepare/pallas_call | solution.py:19
  10.5 0.0 collective-permute-done.1.refs_1_
  10.5 3.5 %collective-permute-done.5.refs_5_ = bf16[4,32,128]{2,1,0:T(8,128)(2,1)S(1)} collective-permute-done((bf16[4,32,128]{2,1,0:T(8,128)(2,1)S(1)}, bf16[4,32,128]{2,1,0:T(8,128)(2,1)S(1)}, u32[]{:S(2)}, u32[]{:S(2)}) %collective-permute-start.5) | collective-permute-done | bytes 32800 | tf_op jit(solution)/shard_map/ppermute | solution.py:243
  14.0 0.0 collective-permute-done.3.refs_2_
  14.0 0.8 %beside.2 = (bf16[17,32,128]{2,1,0:T(8,128)(2,1)S(1)}, bf16[17,32,128]{2,1,0:T(8,128)(2,1)S(1)}, bf16[19,128,128]{2,1,0:T(8,128)(2,1)S(1)}) custom-call(bf16[288,384]{1,0:T(8,128)(2,1)S(1)} %get-tuple-element.19.taps_ref, bf16[16,32,128]{2,1,0:T(8,128)(2,1)S(1)} %get-tuple-element.20.refs_0_, bf16[16,32,128]{2,1,0:T(8,128)(2,1)S(1)} %collective-permute-done.1.refs_1_, ...), custom_call_target="tpu_custom_call" | custom-call | flops 320864256 | tf_op jit(solution)/shard_map/beside/pallas_call | solution.py:19
  14.7 2.9 %collective-permute-start.6 = (bf16[17,32,128]{2,1,0:T(8,128)(2,1)S(1)}, bf16[17,32,128]{2,1,0:T(8,128)(2,1)S(1)}, u32[]{:S(2)}, u32[]{:S(2)}) collective-permute-start(bf16[17,32,128]{2,1,0:T(8,128)(2,1)S(1)} %get-tuple-element.22), channel_id=1, source_target_pairs={{0,8},{8,0},{16,24},{24,16},{1,9},{9,1},{17,25},{25,17},{2,10},{10... | collective-permute-start | bytes 417800 | tf_op jit(solution)/shard_map/ppermute | solution.py:204
  17.6 3.1 %collective-permute-start.7 = (bf16[17,32,128]{2,1,0:T(8,128)(2,1)S(1)}, bf16[17,32,128]{2,1,0:T(8,128)(2,1)S(1)}, u32[]{:S(2)}, u32[]{:S(2)}) collective-permute-start(bf16[17,32,128]{2,1,0:T(8,128)(2,1)S(1)} %get-tuple-element.24), channel_id=1, source_target_pairs={{0,0},{4,4},{24,24},{28,28},{8,16},{12,20},{16,8},{20,12},{1,1},{5... | collective-permute-start | bytes 417800 | tf_op jit(solution)/shard_map/ppermute | solution.py:194
  20.8 0.5 %center.2.center_ref = f32[17,32,128]{2,1,0:T(8,128)S(1)} custom-call(bf16[288,384]{1,0:T(8,128)(2,1)S(1)} %get-tuple-element.19.taps_ref, bf16[19,128,128]{2,1,0:T(8,128)(2,1)S(1)} %get-tuple-element.23.volume), custom_call_target="tpu_custom_call" | custom-call | flops 160432128 | tf_op jit(solution)/shard_map/center/pallas_call | solution.py:19
  21.3 0.0 collective-permute-done.6.near_ref
  21.3 3.0 %collective-permute-done.7.far_ref = bf16[17,32,128]{2,1,0:T(8,128)(2,1)S(1)} collective-permute-done((bf16[17,32,128]{2,1,0:T(8,128)(2,1)S(1)}, bf16[17,32,128]{2,1,0:T(8,128)(2,1)S(1)}, u32[]{:S(2)}, u32[]{:S(2)}) %collective-permute-start.7) | collective-permute-done | bytes 139296 | tf_op jit(solution)/shard_map/ppermute | solution.py:194
  24.3 0.1 finish.2.refs_0_
  24.4 1.4 %collective-permute-start.10 = (bf16[17,32,128]{2,1,0:T(8,128)(2,1)S(1)}, bf16[17,32,128]{2,1,0:T(8,128)(2,1)S(1)}, u32[]{:S(2)}, u32[]{:S(2)}) collective-permute-start(bf16[17,32,128]{2,1,0:T(8,128)(2,1)S(1)} %finish.2.refs_0_), channel_id=1, source_target_pairs={{0,2},{1,3},{2,0},{3,1},{4,6},{5,7},{6,4},{7,5},{8,10},{9,11},{10,... | collective-permute-start | bytes 417800 | tf_op jit(solution)/shard_map/ppermute | solution.py:248
  25.8 0.5 %collective-permute-start.9 = (bf16[17,32,128]{2,1,0:T(8,128)(2,1)S(1)}, bf16[17,32,128]{2,1,0:T(8,128)(2,1)S(1)}, u32[]{:S(2)}, u32[]{:S(2)}) collective-permute-start(bf16[17,32,128]{2,1,0:T(8,128)(2,1)S(1)} %finish.2.refs_0_), channel_id=1, source_target_pairs={{0,1},{1,0},{2,3},{3,2},{4,5},{5,4},{6,7},{7,6},{8,9},{9,8},{10,11... | collective-permute-start | bytes 417800 | tf_op jit(solution)/shard_map/ppermute | solution.py:248
  26.3 1.7 %collective-permute-start.8 = (bf16[17,32,128]{2,1,0:T(8,128)(2,1)S(1)}, bf16[17,32,128]{2,1,0:T(8,128)(2,1)S(1)}, u32[]{:S(2)}, u32[]{:S(2)}) collective-permute-start(bf16[17,32,128]{2,1,0:T(8,128)(2,1)S(1)} %finish.2.refs_0_), channel_id=1, source_target_pairs={{0,3},{1,2},{2,1},{3,0},{4,7},{5,6},{6,5},{7,4},{8,11},{9,10},{10,... | collective-permute-start | bytes 417800 | tf_op jit(solution)/shard_map/ppermute | solution.py:248
  28.0 5.2 %collective-permute-done.10.refs_3_ = bf16[17,32,128]{2,1,0:T(8,128)(2,1)S(1)} collective-permute-done((bf16[17,32,128]{2,1,0:T(8,128)(2,1)S(1)}, bf16[17,32,128]{2,1,0:T(8,128)(2,1)S(1)}, u32[]{:S(2)}, u32[]{:S(2)}) %collective-permute-start.10) | collective-permute-done | bytes 139296 | tf_op jit(solution)/shard_map/ppermute | solution.py:248
  33.2 0.0 collective-permute-done.9.refs_2_
  33.2 0.0 collective-permute-done.8.refs_1_
  33.2 0.6 %beside.3 = (bf16[16,32,128]{2,1,0:T(8,128)(2,1)S(1)}, bf16[18,128,128]{2,1,0:T(8,128)(2,1)S(1)}) custom-call(bf16[288,384]{1,0:T(8,128)(2,1)S(1)} %get-tuple-element.18.taps_ref, bf16[17,32,128]{2,1,0:T(8,128)(2,1)S(1)} %finish.2.refs_0_, bf16[17,32,128]{2,1,0:T(8,128)(2,1)S(1)} %collective-permute-done.8.refs_1_, ...), custom_call_target="tpu_custom_call" | custom-call | flops 150994944 | tf_op jit(solution)/shard_map/beside/pallas_call | solution.py:19
  33.8 1.8 %collective-permute-start.11 = (bf16[16,32,128]{2,1,0:T(8,128)(2,1)S(1)}, bf16[16,32,128]{2,1,0:T(8,128)(2,1)S(1)}, u32[]{:S(2)}, u32[]{:S(2)}) collective-permute-start(bf16[16,32,128]{2,1,0:T(8,128)(2,1)S(1)} %get-tuple-element.26), channel_id=1, source_target_pairs={{8,16},{12,20},{0,4},{24,28},{16,8},{20,12},{4,0},{28,24},{9,17},{... | collective-permute-start | bytes 393224 | tf_op jit(solution)/shard_map/ppermute | solution.py:194
  35.6 0.7 %center.3 = (bf16[16,32,128]{2,1,0:T(8,128)(2,1)S(1)}, f32[16,32,128]{2,1,0:T(8,128)S(1)}) custom-call(bf16[288,384]{1,0:T(8,128)(2,1)S(1)} %get-tuple-element.18.taps_ref, bf16[18,128,128]{2,1,0:T(8,128)(2,1)S(1)} %get-tuple-element.27.volume), custom_call_target="tpu_custom_call" | custom-call | flops 301989888 | tf_op jit(solution)/shard_map/center/pallas_call | solution.py:19
  36.2 0.1 collective-permute-start.12
  36.3 1.9 %collective-permute-done.11.near_ref = bf16[16,32,128]{2,1,0:T(8,128)(2,1)S(1)} collective-permute-done((bf16[16,32,128]{2,1,0:T(8,128)(2,1)S(1)}, bf16[16,32,128]{2,1,0:T(8,128)(2,1)S(1)}, u32[]{:S(2)}, u32[]{:S(2)}) %collective-permute-start.11) | collective-permute-done | bytes 131104 | tf_op jit(solution)/shard_map/ppermute | solution.py:194
  38.2 0.0 collective-permute-done.12.far_ref
  38.2 0.7 %finish.3 = bf16[16,32,128]{2,1,0:T(8,128)(2,1)} custom-call(bf16[16,32,128]{2,1,0:T(8,128)(2,1)S(1)} %collective-permute-done.11.near_ref, f32[16,32,128]{2,1,0:T(8,128)S(1)} %get-tuple-element.28.center_ref, bf16[16,32,128]{2,1,0:T(8,128)(2,1)S(1)} %collective-permute-done.12.far_ref, f32[32,128]{1,0:T(8,128)S(1)} %get-tuple-element.30.bias_ref), custom_call_target="tpu_custom_call" | custom-call | tf_op jit(solution)/shard_map/finish/pallas_call | solution.py:19
  (1 shorter events, 0.0 us)
Async XLA Ops:
  0.0 7.6 %collective-permute-start.2 = (bf16[16,32,128]{2,1,0:T(8,128)(2,1)}, bf16[16,32,128]{2,1,0:T(8,128)(2,1)S(1)}, u32[]{:S(2)}, u32[]{:S(2)}) collective-permute-start(bf16[16,32,128]{2,1,0:T(8,128)(2,1)} %bitcast.6), channel_id=1, source_target_pairs={{0,1},{1,2},{2,3},{3,0},{4,5},{5,6},{6,7},{7,4},{8,9},{9,10},{10,1... | collective-permute-start | bytes 393224 | tf_op jit(solution)/shard_map/ppermute | solution.py:54
  2.9 5.9 %collective-permute-start.4 = (bf16[2,32,128]{2,1,0:T(8,128)(2,1)S(1)}, bf16[2,32,128]{2,1,0:T(8,128)(2,1)S(1)}, u32[]{:S(2)}, u32[]{:S(2)}) collective-permute-start(bf16[2,32,128]{2,1,0:T(8,128)(2,1)S(1)} %dynamic-slice_bitcast_fusion), channel_id=1, source_target_pairs={{0,5},{1,4},{2,7},{3,6},{4,1},{5,0},{6,3},{7,2},{8,13},{9,12},{10,... | collective-permute-start | bytes 49160 | tf_op jit(solution)/shard_map/ppermute | solution.py:64
  5.1 3.7 %collective-permute-start = (bf16[2,32,128]{2,1,0:T(8,128)(2,1)S(1)}, bf16[2,32,128]{2,1,0:T(8,128)(2,1)S(1)}, u32[]{:S(2)}, u32[]{:S(2)}) collective-permute-start(bf16[2,32,128]{2,1,0:T(8,128)(2,1)S(1)} %dynamic-slice_bitcast_fusion), channel_id=1, source_target_pairs={{0,4},{1,5},{2,6},{3,7},{4,0},{5,1},{6,2},{7,3},{8,12},{9,13},{10,... | collective-permute-start | bytes 49160 | tf_op jit(solution)/shard_map/ppermute | solution.py:64
  5.4 5.1 %collective-permute-start.1 = (bf16[16,32,128]{2,1,0:T(8,128)(2,1)}, bf16[16,32,128]{2,1,0:T(8,128)(2,1)S(1)}, u32[]{:S(2)}, u32[]{:S(2)}) collective-permute-start(bf16[16,32,128]{2,1,0:T(8,128)(2,1)} %bitcast.7), channel_id=1, source_target_pairs={{0,3},{1,0},{2,1},{3,2},{4,7},{5,4},{6,5},{7,6},{8,11},{9,8},{10,9... | collective-permute-start | bytes 393224 | tf_op jit(solution)/shard_map/ppermute | solution.py:54
  7.6 6.4 %collective-permute-start.3 = (bf16[16,32,128]{2,1,0:T(8,128)(2,1)S(1)}, bf16[16,32,128]{2,1,0:T(8,128)(2,1)S(1)}, u32[]{:S(2)}, u32[]{:S(2)}) collective-permute-start(bf16[16,32,128]{2,1,0:T(8,128)(2,1)S(1)} %collective-permute-done.2.refs_3_), channel_id=1, source_target_pairs={{0,1},{1,2},{2,3},{3,0},{4,5},{5,6},{6,7},{7,4},{8,9},{9,10},{10,1... | collective-permute-start | bytes 393224 | tf_op jit(solution)/shard_map/ppermute | solution.py:54
  8.8 5.1 %collective-permute-start.5 = (bf16[4,32,128]{2,1,0:T(8,128)(2,1)S(1)}, bf16[4,32,128]{2,1,0:T(8,128)(2,1)S(1)}, u32[]{:S(2)}, u32[]{:S(2)}) collective-permute-start(bf16[4,32,128]{2,1,0:T(8,128)(2,1)S(1)} %pad_maximum_fusion.refs_4_), channel_id=1, source_target_pairs={{0,2},{1,3},{2,0},{3,1},{4,6},{5,7},{6,4},{7,5},{8,10},{9,11},{10,... | collective-permute-start | bytes 98312 | tf_op jit(solution)/shard_map/ppermute | solution.py:243
  14.7 6.6 %collective-permute-start.6 = (bf16[17,32,128]{2,1,0:T(8,128)(2,1)S(1)}, bf16[17,32,128]{2,1,0:T(8,128)(2,1)S(1)}, u32[]{:S(2)}, u32[]{:S(2)}) collective-permute-start(bf16[17,32,128]{2,1,0:T(8,128)(2,1)S(1)} %get-tuple-element.22), channel_id=1, source_target_pairs={{0,8},{8,0},{16,24},{24,16},{1,9},{9,1},{17,25},{25,17},{2,10},{10... | collective-permute-start | bytes 417800 | tf_op jit(solution)/shard_map/ppermute | solution.py:204
  17.6 6.7 %collective-permute-start.7 = (bf16[17,32,128]{2,1,0:T(8,128)(2,1)S(1)}, bf16[17,32,128]{2,1,0:T(8,128)(2,1)S(1)}, u32[]{:S(2)}, u32[]{:S(2)}) collective-permute-start(bf16[17,32,128]{2,1,0:T(8,128)(2,1)S(1)} %get-tuple-element.24), channel_id=1, source_target_pairs={{0,0},{4,4},{24,24},{28,28},{8,16},{12,20},{16,8},{20,12},{1,1},{5... | collective-permute-start | bytes 417800 | tf_op jit(solution)/shard_map/ppermute | solution.py:194
  24.4 8.8 %collective-permute-start.10 = (bf16[17,32,128]{2,1,0:T(8,128)(2,1)S(1)}, bf16[17,32,128]{2,1,0:T(8,128)(2,1)S(1)}, u32[]{:S(2)}, u32[]{:S(2)}) collective-permute-start(bf16[17,32,128]{2,1,0:T(8,128)(2,1)S(1)} %finish.2.refs_0_), channel_id=1, source_target_pairs={{0,2},{1,3},{2,0},{3,1},{4,6},{5,7},{6,4},{7,5},{8,10},{9,11},{10,... | collective-permute-start | bytes 417800 | tf_op jit(solution)/shard_map/ppermute | solution.py:248
  25.8 7.4 %collective-permute-start.9 = (bf16[17,32,128]{2,1,0:T(8,128)(2,1)S(1)}, bf16[17,32,128]{2,1,0:T(8,128)(2,1)S(1)}, u32[]{:S(2)}, u32[]{:S(2)}) collective-permute-start(bf16[17,32,128]{2,1,0:T(8,128)(2,1)S(1)} %finish.2.refs_0_), channel_id=1, source_target_pairs={{0,1},{1,0},{2,3},{3,2},{4,5},{5,4},{6,7},{7,6},{8,9},{9,8},{10,11... | collective-permute-start | bytes 417800 | tf_op jit(solution)/shard_map/ppermute | solution.py:248
  26.3 6.9 %collective-permute-start.8 = (bf16[17,32,128]{2,1,0:T(8,128)(2,1)S(1)}, bf16[17,32,128]{2,1,0:T(8,128)(2,1)S(1)}, u32[]{:S(2)}, u32[]{:S(2)}) collective-permute-start(bf16[17,32,128]{2,1,0:T(8,128)(2,1)S(1)} %finish.2.refs_0_), channel_id=1, source_target_pairs={{0,3},{1,2},{2,1},{3,0},{4,7},{5,6},{6,5},{7,4},{8,11},{9,10},{10,... | collective-permute-start | bytes 417800 | tf_op jit(solution)/shard_map/ppermute | solution.py:248
  33.8 4.5 %collective-permute-start.11 = (bf16[16,32,128]{2,1,0:T(8,128)(2,1)S(1)}, bf16[16,32,128]{2,1,0:T(8,128)(2,1)S(1)}, u32[]{:S(2)}, u32[]{:S(2)}) collective-permute-start(bf16[16,32,128]{2,1,0:T(8,128)(2,1)S(1)} %get-tuple-element.26), channel_id=1, source_target_pairs={{8,16},{12,20},{0,4},{24,28},{16,8},{20,12},{4,0},{28,24},{9,17},{... | collective-permute-start | bytes 393224 | tf_op jit(solution)/shard_map/ppermute | solution.py:194
  36.2 2.0 %collective-permute-start.12 = (bf16[16,32,128]{2,1,0:T(8,128)(2,1)S(1)}, bf16[16,32,128]{2,1,0:T(8,128)(2,1)S(1)}, u32[]{:S(2)}, u32[]{:S(2)}) collective-permute-start(bf16[16,32,128]{2,1,0:T(8,128)(2,1)S(1)} %get-tuple-element.29), channel_id=1, source_target_pairs={{0,8},{8,0},{16,24},{24,16},{1,9},{9,1},{17,25},{25,17},{2,10},{10... | collective-permute-start | bytes 393224 | tf_op jit(solution)/shard_map/ppermute | solution.py:204

commit v7 on v6

--- a/solution.py
+++ b/solution.py
@@ -76,6 +76,13 @@
         pairs += [(i, i, g, g + 1) for i in (0, planes - 1) for g in range(0, rows, 2)]
     there = [(i * rows + g, j * rows + h) for i, j, g, h in pairs]
     return alone + there + [(j, i) for i, j in there]
+
+
+def edge_kernel(density_ref, edge_ref, copied):
+    first = jnp.where(lax.axis_index("gy") == 0, density_ref.shape[0] - 2, 0)
+    move = pltpu.make_async_copy(density_ref.at[pl.ds(first, 2)], edge_ref, copied)
+    move.start()
+    move.wait()
 
 
 def prepare_kernel(*refs):
@@ -151,7 +158,7 @@
     edges = [ref.at[first : first + halo] for ref in halos for first in range(0, ref.shape[0], halo)]
     for step, edge in enumerate(edges):
         at = beside if sides() == 1 else 0 if step < count else halo + rows
-        volume[pl.ds(at, halo), channels(swapped(step % count)), :] = edge[...]
+        volume[pl.ds(at, halo), channels(swapped((0, 2, 1, 3)[step % count] if sides() == 1 else step % count)), :] = edge[...]
     terms(taps_ref[: 3 * sent * outs[0].shape[1]], volume, range(sent), outs)
 
 
@@ -215,8 +222,9 @@
     pairings = partners()
     one_sided = sides() == 1
     if one_sided:
-        start = jnp.where(lax.axis_index("gy") == 0, rows - 2, 0)
-        halos = edge_moves(lax.dynamic_slice_in_dim(density, start, 2, 0), 1, pairings[:2])
+        edge_shape = [VMEM((2, part, depth), density.dtype)]
+        (edge,) = call(edge_kernel, "edge", edge_shape, stored=(density,), scratch=[pltpu.SemaphoreType.DMA])
+        halos = edge_moves(edge, 1, [pairings[0], pairings[2]])
         upward, downward = round_ch(density, 1), round_ch(density, -1)
     else:
         halos = edge_moves(density[-2:], 1, pairings) + edge_moves(density[:2], -1, pairings)
@@ -240,7 +248,7 @@
         others = [downward, round_ch(upward, 1), upward]
         sources = [passed(step) for step in (0, -1, 2, 1)]
         pair, _ = lax.optimization_barrier((jnp.concatenate(halos, axis=0), upward))
-        halos = [pair, lax.ppermute(pair, "ch", pairings[2])]
+        halos = [pair, lax.ppermute(pair, "ch", pairings[1])]
     hidden = layer(
         [own, *others], sources, halos, 2, rows + sides(), first_taps, first_bias, hidden_kernel, VMEM, 0
     )

time: 39.2 us -> 39 us (level)
  starting transfers between devices: 18.6 us -> 17.5 us
  waiting for transfers between devices: 14.9 us -> 15.7 us
  Pallas kernels: 4.63 us -> 5.4 us
  local copies, waits for them, and re-layouts: 0.75 us -> 0.01 us
    ppermute x2, starting transfers between devices: 2.48 us -> 3.56 us  [edge_moves(): lax.ppermute(edge, ('gy', 'ch'), [(i * channels + c, j * channels + d) fo...]
    ppermute x3, starting transfers between devices: 4.32 us -> 3.46 us  [round_ch(): lax.ppermute(block, 'ch', [(i, (i + step) % count) for i in range(count)])]
    pallas_call x7 -> x8, Pallas kernels: 4.63 us -> 5.4 us  [call(): pl.pallas_call(kernel, out_shape=out_shape, in_specs=[pl.BlockSpec(memory...]
    dynamic_slice x1 -> x0, local copies, waits for them, and re-layouts: 0.75 us -> none  [per_device(): lax.dynamic_slice_in_dim(density, start, 2, 0)]
    ppermute x2, starting transfers between devices: 2.99 us -> 2.27 us  [layer(): near = lax.ppermute(outs[1], 'gx', [(i, i ^ 1) for i in range(planes)])]
    ppermute x2, waiting for transfers between devices: 1.22 us -> 1.92 us  [edge_moves(): lax.ppermute(edge, ('gy', 'ch'), [(i * channels + c, j * channels + d) fo...]
    ppermute x1, waiting for transfers between devices: 3.48 us -> 2.99 us  [per_device(): halos = [pair, lax.ppermute(pair, 'ch', pairings[1])]]
  transfers between devices with their start and end apart: 13 -> 13, of which waited for: 5 -> 6; matrix products, arithmetic and copies ran while one was open for 2% -> 0% of each run, Pallas kernels for 6% -> 8%
where the time goes in v7:
time: 39 us; the launch traced here: 38.8 us
  starting transfers between devices  17.5 us (45%)
  waiting for transfers between devices  15.7 us (40%)
  Pallas kernels  5.4 us (14%)
    pallas_call x8, Pallas kernels, call(): pl.pallas_call(kernel, out_shape=out_shape, in_specs=[pl.BlockSpec(memory...  5.4 us
    ppermute x3, waiting for transfers between devices, per_device(): lax.ppermute(hidden, 'ch', pairings[step])  5.38 us
    ppermute x2, waiting for transfers between devices, layer(): far = lax.ppermute(outs[0], ('gx', 'gy'), far_pairs(IDLE[last]))  5.3 us
    ppermute x2, starting transfers between devices, layer(): far = lax.ppermute(outs[0], ('gx', 'gy'), far_pairs(IDLE[last]))  4.56 us
    ppermute x3, starting transfers between devices, per_device(): lax.ppermute(hidden, 'ch', pairings[step])  3.61 us
    ppermute x2, starting transfers between devices, edge_moves(): lax.ppermute(edge, ('gy', 'ch'), [(i * channels + c, j * channels + d) fo...  3.56 us
    ppermute x3, starting transfers between devices, round_ch(): lax.ppermute(block, 'ch', [(i, (i + step) % count) for i in range(count)])  3.46 us
    ppermute x1, waiting for transfers between devices, per_device(): halos = [pair, lax.ppermute(pair, 'ch', pairings[1])]  2.99 us
  transfers between devices with their start and end apart: 13, of which 6 were waited for; matrix products, arithmetic and copies ran while one was open for 0% of the time, Pallas kernels for 8%

profile of v7, /device:TPU:1, one launch (start us, length us, event | category | flops | bytes accessed | tf_op | source)
XLA Modules:
  0.0 38.8 jit_solution(11535404663080963836)
XLA Ops:
  0.0 0.0 copy-start
  0.0 2.1 %collective-permute-start.2 = (bf16[16,32,128]{2,1,0:T(8,128)(2,1)}, bf16[16,32,128]{2,1,0:T(8,128)(2,1)S(1)}, u32[]{:S(2)}, u32[]{:S(2)}) collective-permute-start(bf16[16,32,128]{2,1,0:T(8,128)(2,1)} %bitcast.4), channel_id=1, source_target_pairs={{0,1},{1,2},{2,3},{3,0},{4,5},{5,6},{6,7},{7,4},{8,9},{9,10},{10,1... | collective-permute-start | bytes 393224 | tf_op jit(solution)/shard_map/ppermute | solution.py:54
  2.1 0.8 %edge.1 = bf16[2,32,128]{2,1,0:T(8,128)(2,1)S(1)} custom-call(bf16[16,32,128]{2,1,0:T(8,128)(2,1)} %bitcast.5), custom_call_target="tpu_custom_call" | custom-call | tf_op jit(solution)/shard_map/edge/pallas_call | solution.py:19
  2.9 3.3 %collective-permute-start.4 = (bf16[2,32,128]{2,1,0:T(8,128)(2,1)S(1)}, bf16[2,32,128]{2,1,0:T(8,128)(2,1)S(1)}, u32[]{:S(2)}, u32[]{:S(2)}) collective-permute-start(bf16[2,32,128]{2,1,0:T(8,128)(2,1)S(1)} %edge.1), channel_id=1, source_target_pairs={{0,6},{1,7},{2,4},{3,5},{4,2},{5,3},{6,0},{7,1},{8,14},{9,15},{10,... | collective-permute-start | bytes 49160 | tf_op jit(solution)/shard_map/ppermute | solution.py:64
  6.2 0.3 collective-permute-start
  6.5 0.0 copy-done
  6.5 1.1 %collective-permute-start.1 = (bf16[16,32,128]{2,1,0:T(8,128)(2,1)S(1)}, bf16[16,32,128]{2,1,0:T(8,128)(2,1)S(1)}, u32[]{:S(2)}, u32[]{:S(2)}) collective-permute-start(bf16[16,32,128]{2,1,0:T(8,128)(2,1)S(1)} %bitcast.7), channel_id=1, source_target_pairs={{0,3},{1,0},{2,1},{3,2},{4,7},{5,4},{6,5},{7,6},{8,11},{9,8},{10,9... | collective-permute-start | bytes 393224 | tf_op jit(solution)/shard_map/ppermute | solution.py:54
  7.5 0.1 collective-permute-done.2.refs_3_
  7.7 0.3 collective-permute-start.3
  7.9 1.9 %collective-permute-done.4 = bf16[2,32,128]{2,1,0:T(8,128)(2,1)S(1)} collective-permute-done((bf16[2,32,128]{2,1,0:T(8,128)(2,1)S(1)}, bf16[2,32,128]{2,1,0:T(8,128)(2,1)S(1)}, u32[]{:S(2)}, u32[]{:S(2)}) %collective-permute-start.4) | collective-permute-done | bytes 16416 | tf_op jit(solution)/shard_map/ppermute | solution.py:64
  9.8 0.0 collective-permute-done.refs_5_
  9.9 0.1 collective-permute-start.5
  9.9 1.4 %prepare.1 = (bf16[288,384]{1,0:T(8,128)(2,1)S(1)}, bf16[288,384]{1,0:T(8,128)(2,1)S(1)}, f32[32,128]{1,0:T(8,128)S(1)}, f32[32,128]{1,0:T(8,128)S(1)}, bf16[16,32,128]{2,1,0:T(8,128)(2,1)S(1)}) custom-call(bf16[3,3,3,32,128]{4,3,2,1,0:T(8,128)(2,1)} %refs_0_.1, bf16[3,3,3,32,128]{4,3,2,1,0:T(8,128)(2,1)} %refs_1_.1, f32[1,32]{1,0:T(1,128)} %bitcast.8, ...), custom_call_target="tpu_custom_call" | custom-call | tf_op jit(solution)/shard_map/prepare/pallas_call | solution.py:19
  11.3 0.0 collective-permute-done.1.refs_1_
  11.3 3.0 %collective-permute-done.5.refs_5_ = bf16[4,32,128]{2,1,0:T(8,128)(2,1)S(1)} collective-permute-done((bf16[4,32,128]{2,1,0:T(8,128)(2,1)S(1)}, bf16[4,32,128]{2,1,0:T(8,128)(2,1)S(1)}, u32[]{:S(2)}, u32[]{:S(2)}) %collective-permute-start.5) | collective-permute-done | bytes 32800 | tf_op jit(solution)/shard_map/ppermute | solution.py:251
  14.3 0.0 collective-permute-done.3.refs_2_
  14.3 0.8 %beside.2 = (bf16[17,32,128]{2,1,0:T(8,128)(2,1)S(1)}, bf16[17,32,128]{2,1,0:T(8,128)(2,1)S(1)}, bf16[19,128,128]{2,1,0:T(8,128)(2,1)S(1)}) custom-call(bf16[288,384]{1,0:T(8,128)(2,1)S(1)} %get-tuple-element.19.taps_ref, bf16[16,32,128]{2,1,0:T(8,128)(2,1)S(1)} %get-tuple-element.20.refs_0_, bf16[16,32,128]{2,1,0:T(8,128)(2,1)S(1)} %collective-permute-done.1.refs_1_, ...), custom_call_target="tpu_custom_call" | custom-call | flops 320864256 | tf_op jit(solution)/shard_map/beside/pallas_call | solution.py:19
  15.1 2.2 %collective-permute-start.6 = (bf16[17,32,128]{2,1,0:T(8,128)(2,1)S(1)}, bf16[17,32,128]{2,1,0:T(8,128)(2,1)S(1)}, u32[]{:S(2)}, u32[]{:S(2)}) collective-permute-start(bf16[17,32,128]{2,1,0:T(8,128)(2,1)S(1)} %get-tuple-element.22), channel_id=1, source_target_pairs={{0,8},{8,0},{16,24},{24,16},{1,9},{9,1},{17,25},{25,17},{2,10},{10... | collective-permute-start | bytes 417800 | tf_op jit(solution)/shard_map/ppermute | solution.py:211
  17.3 3.0 %collective-permute-start.7 = (bf16[17,32,128]{2,1,0:T(8,128)(2,1)S(1)}, bf16[17,32,128]{2,1,0:T(8,128)(2,1)S(1)}, u32[]{:S(2)}, u32[]{:S(2)}) collective-permute-start(bf16[17,32,128]{2,1,0:T(8,128)(2,1)S(1)} %get-tuple-element.24), channel_id=1, source_target_pairs={{0,0},{4,4},{24,24},{28,28},{8,16},{12,20},{16,8},{20,12},{1,1},{5... | collective-permute-start | bytes 417800 | tf_op jit(solution)/shard_map/ppermute | solution.py:201
  20.3 0.5 %center.2.center_ref = f32[17,32,128]{2,1,0:T(8,128)S(1)} custom-call(bf16[288,384]{1,0:T(8,128)(2,1)S(1)} %get-tuple-element.19.taps_ref, bf16[19,128,128]{2,1,0:T(8,128)(2,1)S(1)} %get-tuple-element.23.volume), custom_call_target="tpu_custom_call" | custom-call | flops 160432128 | tf_op jit(solution)/shard_map/center/pallas_call | solution.py:19
  20.8 0.0 collective-permute-done.6.near_ref
  20.8 3.1 %collective-permute-done.7.far_ref = bf16[17,32,128]{2,1,0:T(8,128)(2,1)S(1)} collective-permute-done((bf16[17,32,128]{2,1,0:T(8,128)(2,1)S(1)}, bf16[17,32,128]{2,1,0:T(8,128)(2,1)S(1)}, u32[]{:S(2)}, u32[]{:S(2)}) %collective-permute-start.7) | collective-permute-done | bytes 139296 | tf_op jit(solution)/shard_map/ppermute | solution.py:201
  23.9 0.1 finish.2.refs_0_
  24.0 0.3 collective-permute-start.10
  24.4 1.7 %collective-permute-start.9 = (bf16[17,32,128]{2,1,0:T(8,128)(2,1)S(1)}, bf16[17,32,128]{2,1,0:T(8,128)(2,1)S(1)}, u32[]{:S(2)}, u32[]{:S(2)}) collective-permute-start(bf16[17,32,128]{2,1,0:T(8,128)(2,1)S(1)} %finish.2.refs_0_), channel_id=1, source_target_pairs={{0,1},{1,0},{2,3},{3,2},{4,5},{5,4},{6,7},{7,6},{8,9},{9,8},{10,11... | collective-permute-start | bytes 417800 | tf_op jit(solution)/shard_map/ppermute | solution.py:256
  26.1 1.6 %collective-permute-start.8 = (bf16[17,32,128]{2,1,0:T(8,128)(2,1)S(1)}, bf16[17,32,128]{2,1,0:T(8,128)(2,1)S(1)}, u32[]{:S(2)}, u32[]{:S(2)}) collective-permute-start(bf16[17,32,128]{2,1,0:T(8,128)(2,1)S(1)} %finish.2.refs_0_), channel_id=1, source_target_pairs={{0,3},{1,2},{2,1},{3,0},{4,7},{5,6},{6,5},{7,4},{8,11},{9,10},{10,... | collective-permute-start | bytes 417800 | tf_op jit(solution)/shard_map/ppermute | solution.py:256
  27.6 5.4 %collective-permute-done.10.refs_3_ = bf16[17,32,128]{2,1,0:T(8,128)(2,1)S(1)} collective-permute-done((bf16[17,32,128]{2,1,0:T(8,128)(2,1)S(1)}, bf16[17,32,128]{2,1,0:T(8,128)(2,1)S(1)}, u32[]{:S(2)}, u32[]{:S(2)}) %collective-permute-start.10) | collective-permute-done | bytes 139296 | tf_op jit(solution)/shard_map/ppermute | solution.py:256
  33.0 0.0 collective-permute-done.9.refs_2_
  33.0 0.0 collective-permute-done.8.refs_1_
  33.0 0.6 %beside.3 = (bf16[16,32,128]{2,1,0:T(8,128)(2,1)S(1)}, bf16[18,128,128]{2,1,0:T(8,128)(2,1)S(1)}) custom-call(bf16[288,384]{1,0:T(8,128)(2,1)S(1)} %get-tuple-element.18.taps_ref, bf16[17,32,128]{2,1,0:T(8,128)(2,1)S(1)} %finish.2.refs_0_, bf16[17,32,128]{2,1,0:T(8,128)(2,1)S(1)} %collective-permute-done.8.refs_1_, ...), custom_call_target="tpu_custom_call" | custom-call | flops 150994944 | tf_op jit(solution)/shard_map/beside/pallas_call | solution.py:19
  33.6 1.5 %collective-permute-start.11 = (bf16[16,32,128]{2,1,0:T(8,128)(2,1)S(1)}, bf16[16,32,128]{2,1,0:T(8,128)(2,1)S(1)}, u32[]{:S(2)}, u32[]{:S(2)}) collective-permute-start(bf16[16,32,128]{2,1,0:T(8,128)(2,1)S(1)} %get-tuple-element.26), channel_id=1, source_target_pairs={{8,16},{12,20},{0,4},{24,28},{16,8},{20,12},{4,0},{28,24},{9,17},{... | collective-permute-start | bytes 393224 | tf_op jit(solution)/shard_map/ppermute | solution.py:201
  35.1 0.7 %center.3 = (bf16[16,32,128]{2,1,0:T(8,128)(2,1)S(1)}, f32[16,32,128]{2,1,0:T(8,128)S(1)}) custom-call(bf16[288,384]{1,0:T(8,128)(2,1)S(1)} %get-tuple-element.18.taps_ref, bf16[18,128,128]{2,1,0:T(8,128)(2,1)S(1)} %get-tuple-element.27.volume), custom_call_target="tpu_custom_call" | custom-call | flops 301989888 | tf_op jit(solution)/shard_map/center/pallas_call | solution.py:19
  35.8 0.1 collective-permute-start.12
  35.8 2.2 %collective-permute-done.11.near_ref = bf16[16,32,128]{2,1,0:T(8,128)(2,1)S(1)} collective-permute-done((bf16[16,32,128]{2,1,0:T(8,128)(2,1)S(1)}, bf16[16,32,128]{2,1,0:T(8,128)(2,1)S(1)}, u32[]{:S(2)}, u32[]{:S(2)}) %collective-permute-start.11) | collective-permute-done | bytes 131104 | tf_op jit(solution)/shard_map/ppermute | solution.py:201
  38.0 0.0 collective-permute-done.12.far_ref
  38.0 0.7 %finish.3 = bf16[16,32,128]{2,1,0:T(8,128)(2,1)} custom-call(bf16[16,32,128]{2,1,0:T(8,128)(2,1)S(1)} %collective-permute-done.11.near_ref, f32[16,32,128]{2,1,0:T(8,128)S(1)} %get-tuple-element.28.center_ref, bf16[16,32,128]{2,1,0:T(8,128)(2,1)S(1)} %collective-permute-done.12.far_ref, f32[32,128]{1,0:T(8,128)S(1)} %get-tuple-element.30.bias_ref), custom_call_target="tpu_custom_call" | custom-call | tf_op jit(solution)/shard_map/finish/pallas_call | solution.py:19
  (1 shorter events, 0.0 us)
Async XLA Ops:
  0.0 6.5 %copy-start = (bf16[1,16,32,128]{3,2,1,0:T(8,128)(2,1)S(1)}, bf16[1,16,32,128]{3,2,1,0:T(8,128)(2,1)}, u32[]{:S(2)}) copy-start(bf16[1,16,32,128]{3,2,1,0:T(8,128)(2,1)} %param.5) | copy-start | bytes 393220
  0.0 7.7 %collective-permute-start.2 = (bf16[16,32,128]{2,1,0:T(8,128)(2,1)}, bf16[16,32,128]{2,1,0:T(8,128)(2,1)S(1)}, u32[]{:S(2)}, u32[]{:S(2)}) collective-permute-start(bf16[16,32,128]{2,1,0:T(8,128)(2,1)} %bitcast.4), channel_id=1, source_target_pairs={{0,1},{1,2},{2,3},{3,0},{4,5},{5,6},{6,7},{7,4},{8,9},{9,10},{10,1... | collective-permute-start | bytes 393224 | tf_op jit(solution)/shard_map/ppermute | solution.py:54
  2.9 6.9 %collective-permute-start.4 = (bf16[2,32,128]{2,1,0:T(8,128)(2,1)S(1)}, bf16[2,32,128]{2,1,0:T(8,128)(2,1)S(1)}, u32[]{:S(2)}, u32[]{:S(2)}) collective-permute-start(bf16[2,32,128]{2,1,0:T(8,128)(2,1)S(1)} %edge.1), channel_id=1, source_target_pairs={{0,6},{1,7},{2,4},{3,5},{4,2},{5,3},{6,0},{7,1},{8,14},{9,15},{10,... | collective-permute-start | bytes 49160 | tf_op jit(solution)/shard_map/ppermute | solution.py:64
  6.2 3.6 %collective-permute-start = (bf16[2,32,128]{2,1,0:T(8,128)(2,1)S(1)}, bf16[2,32,128]{2,1,0:T(8,128)(2,1)S(1)}, u32[]{:S(2)}, u32[]{:S(2)}) collective-permute-start(bf16[2,32,128]{2,1,0:T(8,128)(2,1)S(1)} %edge.1), channel_id=1, source_target_pairs={{0,4},{1,5},{2,6},{3,7},{4,0},{5,1},{6,2},{7,3},{8,12},{9,13},{10,... | collective-permute-start | bytes 49160 | tf_op jit(solution)/shard_map/ppermute | solution.py:64
  6.5 4.9 %collective-permute-start.1 = (bf16[16,32,128]{2,1,0:T(8,128)(2,1)S(1)}, bf16[16,32,128]{2,1,0:T(8,128)(2,1)S(1)}, u32[]{:S(2)}, u32[]{:S(2)}) collective-permute-start(bf16[16,32,128]{2,1,0:T(8,128)(2,1)S(1)} %bitcast.7), channel_id=1, source_target_pairs={{0,3},{1,0},{2,1},{3,2},{4,7},{5,4},{6,5},{7,6},{8,11},{9,8},{10,9... | collective-permute-start | bytes 393224 | tf_op jit(solution)/shard_map/ppermute | solution.py:54
  7.7 6.7 %collective-permute-start.3 = (bf16[16,32,128]{2,1,0:T(8,128)(2,1)S(1)}, bf16[16,32,128]{2,1,0:T(8,128)(2,1)S(1)}, u32[]{:S(2)}, u32[]{:S(2)}) collective-permute-start(bf16[16,32,128]{2,1,0:T(8,128)(2,1)S(1)} %collective-permute-done.2.refs_3_), channel_id=1, source_target_pairs={{0,1},{1,2},{2,3},{3,0},{4,5},{5,6},{6,7},{7,4},{8,9},{9,10},{10,1... | collective-permute-start | bytes 393224 | tf_op jit(solution)/shard_map/ppermute | solution.py:54
  9.9 4.5 %collective-permute-start.5 = (bf16[4,32,128]{2,1,0:T(8,128)(2,1)S(1)}, bf16[4,32,128]{2,1,0:T(8,128)(2,1)S(1)}, u32[]{:S(2)}, u32[]{:S(2)}) collective-permute-start(bf16[4,32,128]{2,1,0:T(8,128)(2,1)S(1)} %pad_maximum_fusion.refs_4_), channel_id=1, source_target_pairs={{0,1},{1,0},{2,3},{3,2},{4,5},{5,4},{6,7},{7,6},{8,9},{9,8},{10,11... | collective-permute-start | bytes 98312 | tf_op jit(solution)/shard_map/ppermute | solution.py:251
  15.1 5.8 %collective-permute-start.6 = (bf16[17,32,128]{2,1,0:T(8,128)(2,1)S(1)}, bf16[17,32,128]{2,1,0:T(8,128)(2,1)S(1)}, u32[]{:S(2)}, u32[]{:S(2)}) collective-permute-start(bf16[17,32,128]{2,1,0:T(8,128)(2,1)S(1)} %get-tuple-element.22), channel_id=1, source_target_pairs={{0,8},{8,0},{16,24},{24,16},{1,9},{9,1},{17,25},{25,17},{2,10},{10... | collective-permute-start | bytes 417800 | tf_op jit(solution)/shard_map/ppermute | solution.py:211
  17.3 6.7 %collective-permute-start.7 = (bf16[17,32,128]{2,1,0:T(8,128)(2,1)S(1)}, bf16[17,32,128]{2,1,0:T(8,128)(2,1)S(1)}, u32[]{:S(2)}, u32[]{:S(2)}) collective-permute-start(bf16[17,32,128]{2,1,0:T(8,128)(2,1)S(1)} %get-tuple-element.24), channel_id=1, source_target_pairs={{0,0},{4,4},{24,24},{28,28},{8,16},{12,20},{16,8},{20,12},{1,1},{5... | collective-permute-start | bytes 417800 | tf_op jit(solution)/shard_map/ppermute | solution.py:201
  24.0 9.0 %collective-permute-start.10 = (bf16[17,32,128]{2,1,0:T(8,128)(2,1)S(1)}, bf16[17,32,128]{2,1,0:T(8,128)(2,1)S(1)}, u32[]{:S(2)}, u32[]{:S(2)}) collective-permute-start(bf16[17,32,128]{2,1,0:T(8,128)(2,1)S(1)} %finish.2.refs_0_), channel_id=1, source_target_pairs={{0,2},{1,3},{2,0},{3,1},{4,6},{5,7},{6,4},{7,5},{8,10},{9,11},{10,... | collective-permute-start | bytes 417800 | tf_op jit(solution)/shard_map/ppermute | solution.py:256
  24.4 8.7 %collective-permute-start.9 = (bf16[17,32,128]{2,1,0:T(8,128)(2,1)S(1)}, bf16[17,32,128]{2,1,0:T(8,128)(2,1)S(1)}, u32[]{:S(2)}, u32[]{:S(2)}) collective-permute-start(bf16[17,32,128]{2,1,0:T(8,128)(2,1)S(1)} %finish.2.refs_0_), channel_id=1, source_target_pairs={{0,1},{1,0},{2,3},{3,2},{4,5},{5,4},{6,7},{7,6},{8,9},{9,8},{10,11... | collective-permute-start | bytes 417800 | tf_op jit(solution)/shard_map/ppermute | solution.py:256
  26.1 6.9 %collective-permute-start.8 = (bf16[17,32,128]{2,1,0:T(8,128)(2,1)S(1)}, bf16[17,32,128]{2,1,0:T(8,128)(2,1)S(1)}, u32[]{:S(2)}, u32[]{:S(2)}) collective-permute-start(bf16[17,32,128]{2,1,0:T(8,128)(2,1)S(1)} %finish.2.refs_0_), channel_id=1, source_target_pairs={{0,3},{1,2},{2,1},{3,0},{4,7},{5,6},{6,5},{7,4},{8,11},{9,10},{10,... | collective-permute-start | bytes 417800 | tf_op jit(solution)/shard_map/ppermute | solution.py:256
  33.6 4.5 %collective-permute-start.11 = (bf16[16,32,128]{2,1,0:T(8,128)(2,1)S(1)}, bf16[16,32,128]{2,1,0:T(8,128)(2,1)S(1)}, u32[]{:S(2)}, u32[]{:S(2)}) collective-permute-start(bf16[16,32,128]{2,1,0:T(8,128)(2,1)S(1)} %get-tuple-element.26), channel_id=1, source_target_pairs={{8,16},{12,20},{0,4},{24,28},{16,8},{20,12},{4,0},{28,24},{9,17},{... | collective-permute-start | bytes 393224 | tf_op jit(solution)/shard_map/ppermute | solution.py:201
  35.8 2.3 %collective-permute-start.12 = (bf16[16,32,128]{2,1,0:T(8,128)(2,1)S(1)}, bf16[16,32,128]{2,1,0:T(8,128)(2,1)S(1)}, u32[]{:S(2)}, u32[]{:S(2)}) collective-permute-start(bf16[16,32,128]{2,1,0:T(8,128)(2,1)S(1)} %get-tuple-element.29), channel_id=1, source_target_pairs={{0,8},{8,0},{16,24},{24,16},{1,9},{9,1},{17,25},{25,17},{2,10},{10... | collective-permute-start | bytes 393224 | tf_op jit(solution)/shard_map/ppermute | solution.py:211

commit v8 on v7

--- a/solution.py
+++ b/solution.py
@@ -236,7 +236,7 @@
         prepare_kernel,
         "prepare",
         [taps_shape, taps_shape, bias_shape, bias_shape, VMEM(density.shape, density.dtype)],
-        halos[0],
+        halos[1],
         stored=(first_kernel, second_kernel, first_bias.reshape(1, -1), second_bias.reshape(1, -1), density),
         scratch=[
             pltpu.SemaphoreType.DMA((5,)),

time: 39 us -> 39 us (level)
  starting transfers between devices: 17.5 us -> 18.4 us
  waiting for transfers between devices: 15.7 us -> 14.9 us
    ppermute x2, waiting for transfers between devices: 1.92 us -> 1.37 us  [edge_moves(): lax.ppermute(edge, ('gy', 'ch'), [(i * channels + c, j * channels + d) fo...]
    ppermute x1, starting transfers between devices: 0.07 us -> 0.56 us  [per_device(): halos = [pair, lax.ppermute(pair, 'ch', pairings[1])]]
where the time goes in v8:
time: 39 us; the launch traced here: 38.8 us
  starting transfers between devices  18.4 us (47%)
  waiting for transfers between devices  14.9 us (38%)
  Pallas kernels  5.39 us (14%)
    pallas_call x8, Pallas kernels, call(): pl.pallas_call(kernel, out_shape=out_shape, in_specs=[pl.BlockSpec(memory...  5.39 us
    ppermute x3, waiting for transfers between devices, per_device(): lax.ppermute(hidden, 'ch', pairings[step])  5.38 us
    ppermute x2, waiting for transfers between devices, layer(): far = lax.ppermute(outs[0], ('gx', 'gy'), far_pairs(IDLE[last]))  5.15 us
    ppermute x2, starting transfers between devices, layer(): far = lax.ppermute(outs[0], ('gx', 'gy'), far_pairs(IDLE[last]))  4.7 us
    ppermute x3, starting transfers between devices, per_device(): lax.ppermute(hidden, 'ch', pairings[step])  3.61 us
    ppermute x2, starting transfers between devices, edge_moves(): lax.ppermute(edge, ('gy', 'ch'), [(i * channels + c, j * channels + d) fo...  3.56 us
    ppermute x3, starting transfers between devices, round_ch(): lax.ppermute(block, 'ch', [(i, (i + step) % count) for i in range(count)])  3.46 us
    ppermute x1, waiting for transfers between devices, per_device(): halos = [pair, lax.ppermute(pair, 'ch', pairings[1])]  2.85 us
  transfers between devices with their start and end apart: 13, of which 6 were waited for; matrix products, arithmetic and copies ran while one was open for 0% of the time, Pallas kernels for 8%

profile of v8, /device:TPU:1, one launch (start us, length us, event | category | flops | bytes accessed | tf_op | source)
XLA Modules:
  0.0 38.8 jit_solution(13750211175984089344)
XLA Ops:
  0.0 0.0 copy-start
  0.0 2.1 %collective-permute-start.2 = (bf16[16,32,128]{2,1,0:T(8,128)(2,1)}, bf16[16,32,128]{2,1,0:T(8,128)(2,1)S(1)}, u32[]{:S(2)}, u32[]{:S(2)}) collective-permute-start(bf16[16,32,128]{2,1,0:T(8,128)(2,1)} %bitcast.4), channel_id=1, source_target_pairs={{0,1},{1,2},{2,3},{3,0},{4,5},{5,6},{6,7},{7,4},{8,9},{9,10},{10,1... | collective-permute-start | bytes 393224 | tf_op jit(solution)/shard_map/ppermute | solution.py:54
  2.1 0.8 %edge.1 = bf16[2,32,128]{2,1,0:T(8,128)(2,1)S(1)} custom-call(bf16[16,32,128]{2,1,0:T(8,128)(2,1)} %bitcast.5), custom_call_target="tpu_custom_call" | custom-call | tf_op jit(solution)/shard_map/edge/pallas_call | solution.py:19
  2.9 1.3 %collective-permute-start.4 = (bf16[2,32,128]{2,1,0:T(8,128)(2,1)S(1)}, bf16[2,32,128]{2,1,0:T(8,128)(2,1)S(1)}, u32[]{:S(2)}, u32[]{:S(2)}) collective-permute-start(bf16[2,32,128]{2,1,0:T(8,128)(2,1)S(1)} %edge.1), channel_id=1, source_target_pairs={{0,4},{1,5},{2,6},{3,7},{4,0},{5,1},{6,2},{7,3},{8,12},{9,13},{10,... | collective-permute-start | bytes 49160 | tf_op jit(solution)/shard_map/ppermute | solution.py:64
  4.2 2.3 %collective-permute-start = (bf16[2,32,128]{2,1,0:T(8,128)(2,1)S(1)}, bf16[2,32,128]{2,1,0:T(8,128)(2,1)S(1)}, u32[]{:S(2)}, u32[]{:S(2)}) collective-permute-start(bf16[2,32,128]{2,1,0:T(8,128)(2,1)S(1)} %edge.1), channel_id=1, source_target_pairs={{0,6},{1,7},{2,4},{3,5},{4,2},{5,3},{6,0},{7,1},{8,14},{9,15},{10,... | collective-permute-start | bytes 49160 | tf_op jit(solution)/shard_map/ppermute | solution.py:64
  6.5 0.0 copy-done
  6.5 1.1 %collective-permute-start.1 = (bf16[16,32,128]{2,1,0:T(8,128)(2,1)S(1)}, bf16[16,32,128]{2,1,0:T(8,128)(2,1)S(1)}, u32[]{:S(2)}, u32[]{:S(2)}) collective-permute-start(bf16[16,32,128]{2,1,0:T(8,128)(2,1)S(1)} %bitcast.7), channel_id=1, source_target_pairs={{0,3},{1,0},{2,1},{3,2},{4,7},{5,4},{6,5},{7,6},{8,11},{9,8},{10,9... | collective-permute-start | bytes 393224 | tf_op jit(solution)/shard_map/ppermute | solution.py:54
  7.5 0.1 collective-permute-done.2.refs_3_
  7.7 0.3 collective-permute-start.3
  7.9 0.0 collective-permute-done.4
  7.9 1.4 %collective-permute-done.refs_5_ = bf16[2,32,128]{2,1,0:T(8,128)(2,1)S(1)} collective-permute-done((bf16[2,32,128]{2,1,0:T(8,128)(2,1)S(1)}, bf16[2,32,128]{2,1,0:T(8,128)(2,1)S(1)}, u32[]{:S(2)}, u32[]{:S(2)}) %collective-permute-start) | collective-permute-done | bytes 16416 | tf_op jit(solution)/shard_map/ppermute | solution.py:64
  9.3 0.6 %collective-permute-start.5 = (bf16[4,32,128]{2,1,0:T(8,128)(2,1)S(1)}, bf16[4,32,128]{2,1,0:T(8,128)(2,1)S(1)}, u32[]{:S(2)}, u32[]{:S(2)}) collective-permute-start(bf16[4,32,128]{2,1,0:T(8,128)(2,1)S(1)} %pad_maximum_fusion.refs_4_), channel_id=1, source_target_pairs={{0,1},{1,0},{2,3},{3,2},{4,5},{5,4},{6,7},{7,6},{8,9},{9,8},{10,11... | collective-permute-start | bytes 98312 | tf_op jit(solution)/shard_map/ppermute | solution.py:251
  9.9 1.4 %prepare.1 = (bf16[288,384]{1,0:T(8,128)(2,1)S(1)}, bf16[288,384]{1,0:T(8,128)(2,1)S(1)}, f32[32,128]{1,0:T(8,128)S(1)}, f32[32,128]{1,0:T(8,128)S(1)}, bf16[16,32,128]{2,1,0:T(8,128)(2,1)S(1)}) custom-call(bf16[3,3,3,32,128]{4,3,2,1,0:T(8,128)(2,1)} %refs_0_.1, bf16[3,3,3,32,128]{4,3,2,1,0:T(8,128)(2,1)} %refs_1_.1, f32[1,32]{1,0:T(1,128)} %bitcast.8, ...), custom_call_target="tpu_custom_call" | custom-call | tf_op jit(solution)/shard_map/prepare/pallas_call | solution.py:19
  11.2 0.0 collective-permute-done.1.refs_1_
  11.2 2.9 %collective-permute-done.5.refs_5_ = bf16[4,32,128]{2,1,0:T(8,128)(2,1)S(1)} collective-permute-done((bf16[4,32,128]{2,1,0:T(8,128)(2,1)S(1)}, bf16[4,32,128]{2,1,0:T(8,128)(2,1)S(1)}, u32[]{:S(2)}, u32[]{:S(2)}) %collective-permute-start.5) | collective-permute-done | bytes 32800 | tf_op jit(solution)/shard_map/ppermute | solution.py:251
  14.1 0.0 collective-permute-done.3.refs_2_
  14.1 0.8 %beside.2 = (bf16[17,32,128]{2,1,0:T(8,128)(2,1)S(1)}, bf16[17,32,128]{2,1,0:T(8,128)(2,1)S(1)}, bf16[19,128,128]{2,1,0:T(8,128)(2,1)S(1)}) custom-call(bf16[288,384]{1,0:T(8,128)(2,1)S(1)} %get-tuple-element.19.taps_ref, bf16[16,32,128]{2,1,0:T(8,128)(2,1)S(1)} %get-tuple-element.20.refs_0_, bf16[16,32,128]{2,1,0:T(8,128)(2,1)S(1)} %collective-permute-done.1.refs_1_, ...), custom_call_target="tpu_custom_call" | custom-call | flops 320864256 | tf_op jit(solution)/shard_map/beside/pallas_call | solution.py:19
  14.9 2.4 %collective-permute-start.6 = (bf16[17,32,128]{2,1,0:T(8,128)(2,1)S(1)}, bf16[17,32,128]{2,1,0:T(8,128)(2,1)S(1)}, u32[]{:S(2)}, u32[]{:S(2)}) collective-permute-start(bf16[17,32,128]{2,1,0:T(8,128)(2,1)S(1)} %get-tuple-element.22), channel_id=1, source_target_pairs={{0,8},{8,0},{16,24},{24,16},{1,9},{9,1},{17,25},{25,17},{2,10},{10... | collective-permute-start | bytes 417800 | tf_op jit(solution)/shard_map/ppermute | solution.py:211
  17.3 3.0 %collective-permute-start.7 = (bf16[17,32,128]{2,1,0:T(8,128)(2,1)S(1)}, bf16[17,32,128]{2,1,0:T(8,128)(2,1)S(1)}, u32[]{:S(2)}, u32[]{:S(2)}) collective-permute-start(bf16[17,32,128]{2,1,0:T(8,128)(2,1)S(1)} %get-tuple-element.24), channel_id=1, source_target_pairs={{0,0},{4,4},{24,24},{28,28},{8,16},{12,20},{16,8},{20,12},{1,1},{5... | collective-permute-start | bytes 417800 | tf_op jit(solution)/shard_map/ppermute | solution.py:201
  20.3 0.5 %center.2.center_ref = f32[17,32,128]{2,1,0:T(8,128)S(1)} custom-call(bf16[288,384]{1,0:T(8,128)(2,1)S(1)} %get-tuple-element.19.taps_ref, bf16[19,128,128]{2,1,0:T(8,128)(2,1)S(1)} %get-tuple-element.23.volume), custom_call_target="tpu_custom_call" | custom-call | flops 160432128 | tf_op jit(solution)/shard_map/center/pallas_call | solution.py:19
  20.8 0.0 collective-permute-done.6.near_ref
  20.8 3.1 %collective-permute-done.7.far_ref = bf16[17,32,128]{2,1,0:T(8,128)(2,1)S(1)} collective-permute-done((bf16[17,32,128]{2,1,0:T(8,128)(2,1)S(1)}, bf16[17,32,128]{2,1,0:T(8,128)(2,1)S(1)}, u32[]{:S(2)}, u32[]{:S(2)}) %collective-permute-start.7) | collective-permute-done | bytes 139296 | tf_op jit(solution)/shard_map/ppermute | solution.py:201
  23.9 0.1 finish.2.refs_0_
  24.0 1.0 %collective-permute-start.10 = (bf16[17,32,128]{2,1,0:T(8,128)(2,1)S(1)}, bf16[17,32,128]{2,1,0:T(8,128)(2,1)S(1)}, u32[]{:S(2)}, u32[]{:S(2)}) collective-permute-start(bf16[17,32,128]{2,1,0:T(8,128)(2,1)S(1)} %finish.2.refs_0_), channel_id=1, source_target_pairs={{0,2},{1,3},{2,0},{3,1},{4,6},{5,7},{6,4},{7,5},{8,10},{9,11},{10,... | collective-permute-start | bytes 417800 | tf_op jit(solution)/shard_map/ppermute | solution.py:256
  25.0 1.1 %collective-permute-start.9 = (bf16[17,32,128]{2,1,0:T(8,128)(2,1)S(1)}, bf16[17,32,128]{2,1,0:T(8,128)(2,1)S(1)}, u32[]{:S(2)}, u32[]{:S(2)}) collective-permute-start(bf16[17,32,128]{2,1,0:T(8,128)(2,1)S(1)} %finish.2.refs_0_), channel_id=1, source_target_pairs={{0,1},{1,0},{2,3},{3,2},{4,5},{5,4},{6,7},{7,6},{8,9},{9,8},{10,11... | collective-permute-start | bytes 417800 | tf_op jit(solution)/shard_map/ppermute | solution.py:256
  26.1 1.5 %collective-permute-start.8 = (bf16[17,32,128]{2,1,0:T(8,128)(2,1)S(1)}, bf16[17,32,128]{2,1,0:T(8,128)(2,1)S(1)}, u32[]{:S(2)}, u32[]{:S(2)}) collective-permute-start(bf16[17,32,128]{2,1,0:T(8,128)(2,1)S(1)} %finish.2.refs_0_), channel_id=1, source_target_pairs={{0,3},{1,2},{2,1},{3,0},{4,7},{5,6},{6,5},{7,4},{8,11},{9,10},{10,... | collective-permute-start | bytes 417800 | tf_op jit(solution)/shard_map/ppermute | solution.py:256
  27.6 5.4 %collective-permute-done.10.refs_3_ = bf16[17,32,128]{2,1,0:T(8,128)(2,1)S(1)} collective-permute-done((bf16[17,32,128]{2,1,0:T(8,128)(2,1)S(1)}, bf16[17,32,128]{2,1,0:T(8,128)(2,1)S(1)}, u32[]{:S(2)}, u32[]{:S(2)}) %collective-permute-start.10) | collective-permute-done | bytes 139296 | tf_op jit(solution)/shard_map/ppermute | solution.py:256
  33.0 0.0 collective-permute-done.9.refs_2_
  33.0 0.0 collective-permute-done.8.refs_1_
  33.0 0.6 %beside.3 = (bf16[16,32,128]{2,1,0:T(8,128)(2,1)S(1)}, bf16[18,128,128]{2,1,0:T(8,128)(2,1)S(1)}) custom-call(bf16[288,384]{1,0:T(8,128)(2,1)S(1)} %get-tuple-element.18.taps_ref, bf16[17,32,128]{2,1,0:T(8,128)(2,1)S(1)} %finish.2.refs_0_, bf16[17,32,128]{2,1,0:T(8,128)(2,1)S(1)} %collective-permute-done.8.refs_1_, ...), custom_call_target="tpu_custom_call" | custom-call | flops 150994944 | tf_op jit(solution)/shard_map/beside/pallas_call | solution.py:19
  33.6 1.7 %collective-permute-start.11 = (bf16[16,32,128]{2,1,0:T(8,128)(2,1)S(1)}, bf16[16,32,128]{2,1,0:T(8,128)(2,1)S(1)}, u32[]{:S(2)}, u32[]{:S(2)}) collective-permute-start(bf16[16,32,128]{2,1,0:T(8,128)(2,1)S(1)} %get-tuple-element.26), channel_id=1, source_target_pairs={{8,16},{12,20},{0,4},{24,28},{16,8},{20,12},{4,0},{28,24},{9,17},{... | collective-permute-start | bytes 393224 | tf_op jit(solution)/shard_map/ppermute | solution.py:201
  35.2 0.7 %center.3 = (bf16[16,32,128]{2,1,0:T(8,128)(2,1)S(1)}, f32[16,32,128]{2,1,0:T(8,128)S(1)}) custom-call(bf16[288,384]{1,0:T(8,128)(2,1)S(1)} %get-tuple-element.18.taps_ref, bf16[18,128,128]{2,1,0:T(8,128)(2,1)S(1)} %get-tuple-element.27.volume), custom_call_target="tpu_custom_call" | custom-call | flops 301989888 | tf_op jit(solution)/shard_map/center/pallas_call | solution.py:19
  35.9 0.1 collective-permute-start.12
  36.0 2.1 %collective-permute-done.11.near_ref = bf16[16,32,128]{2,1,0:T(8,128)(2,1)S(1)} collective-permute-done((bf16[16,32,128]{2,1,0:T(8,128)(2,1)S(1)}, bf16[16,32,128]{2,1,0:T(8,128)(2,1)S(1)}, u32[]{:S(2)}, u32[]{:S(2)}) %collective-permute-start.11) | collective-permute-done | bytes 131104 | tf_op jit(solution)/shard_map/ppermute | solution.py:201
  38.0 0.0 collective-permute-done.12.far_ref
  38.0 0.7 %finish.3 = bf16[16,32,128]{2,1,0:T(8,128)(2,1)} custom-call(bf16[16,32,128]{2,1,0:T(8,128)(2,1)S(1)} %collective-permute-done.11.near_ref, f32[16,32,128]{2,1,0:T(8,128)S(1)} %get-tuple-element.28.center_ref, bf16[16,32,128]{2,1,0:T(8,128)(2,1)S(1)} %collective-permute-done.12.far_ref, f32[32,128]{1,0:T(8,128)S(1)} %get-tuple-element.30.bias_ref), custom_call_target="tpu_custom_call" | custom-call | tf_op jit(solution)/shard_map/finish/pallas_call | solution.py:19
  (1 shorter events, 0.0 us)
Async XLA Ops:
  0.0 6.5 %copy-start = (bf16[1,16,32,128]{3,2,1,0:T(8,128)(2,1)S(1)}, bf16[1,16,32,128]{3,2,1,0:T(8,128)(2,1)}, u32[]{:S(2)}) copy-start(bf16[1,16,32,128]{3,2,1,0:T(8,128)(2,1)} %param.5) | copy-start | bytes 393220
  0.0 7.7 %collective-permute-start.2 = (bf16[16,32,128]{2,1,0:T(8,128)(2,1)}, bf16[16,32,128]{2,1,0:T(8,128)(2,1)S(1)}, u32[]{:S(2)}, u32[]{:S(2)}) collective-permute-start(bf16[16,32,128]{2,1,0:T(8,128)(2,1)} %bitcast.4), channel_id=1, source_target_pairs={{0,1},{1,2},{2,3},{3,0},{4,5},{5,6},{6,7},{7,4},{8,9},{9,10},{10,1... | collective-permute-start | bytes 393224 | tf_op jit(solution)/shard_map/ppermute | solution.py:54
  2.9 5.0 %collective-permute-start.4 = (bf16[2,32,128]{2,1,0:T(8,128)(2,1)S(1)}, bf16[2,32,128]{2,1,0:T(8,128)(2,1)S(1)}, u32[]{:S(2)}, u32[]{:S(2)}) collective-permute-start(bf16[2,32,128]{2,1,0:T(8,128)(2,1)S(1)} %edge.1), channel_id=1, source_target_pairs={{0,4},{1,5},{2,6},{3,7},{4,0},{5,1},{6,2},{7,3},{8,12},{9,13},{10,... | collective-permute-start | bytes 49160 | tf_op jit(solution)/shard_map/ppermute | solution.py:64
  4.2 5.1 %collective-permute-start = (bf16[2,32,128]{2,1,0:T(8,128)(2,1)S(1)}, bf16[2,32,128]{2,1,0:T(8,128)(2,1)S(1)}, u32[]{:S(2)}, u32[]{:S(2)}) collective-permute-start(bf16[2,32,128]{2,1,0:T(8,128)(2,1)S(1)} %edge.1), channel_id=1, source_target_pairs={{0,6},{1,7},{2,4},{3,5},{4,2},{5,3},{6,0},{7,1},{8,14},{9,15},{10,... | collective-permute-start | bytes 49160 | tf_op jit(solution)/shard_map/ppermute | solution.py:64
  6.5 4.8 %collective-permute-start.1 = (bf16[16,32,128]{2,1,0:T(8,128)(2,1)S(1)}, bf16[16,32,128]{2,1,0:T(8,128)(2,1)S(1)}, u32[]{:S(2)}, u32[]{:S(2)}) collective-permute-start(bf16[16,32,128]{2,1,0:T(8,128)(2,1)S(1)} %bitcast.7), channel_id=1, source_target_pairs={{0,3},{1,0},{2,1},{3,2},{4,7},{5,4},{6,5},{7,6},{8,11},{9,8},{10,9... | collective-permute-start | bytes 393224 | tf_op jit(solution)/shard_map/ppermute | solution.py:54
  7.7 6.4 %collective-permute-start.3 = (bf16[16,32,128]{2,1,0:T(8,128)(2,1)S(1)}, bf16[16,32,128]{2,1,0:T(8,128)(2,1)S(1)}, u32[]{:S(2)}, u32[]{:S(2)}) collective-permute-start(bf16[16,32,128]{2,1,0:T(8,128)(2,1)S(1)} %collective-permute-done.2.refs_3_), channel_id=1, source_target_pairs={{0,1},{1,2},{2,3},{3,0},{4,5},{5,6},{6,7},{7,4},{8,9},{9,10},{10,1... | collective-permute-start | bytes 393224 | tf_op jit(solution)/shard_map/ppermute | solution.py:54
  9.3 4.8 %collective-permute-start.5 = (bf16[4,32,128]{2,1,0:T(8,128)(2,1)S(1)}, bf16[4,32,128]{2,1,0:T(8,128)(2,1)S(1)}, u32[]{:S(2)}, u32[]{:S(2)}) collective-permute-start(bf16[4,32,128]{2,1,0:T(8,128)(2,1)S(1)} %pad_maximum_fusion.refs_4_), channel_id=1, source_target_pairs={{0,1},{1,0},{2,3},{3,2},{4,5},{5,4},{6,7},{7,6},{8,9},{9,8},{10,11... | collective-permute-start | bytes 98312 | tf_op jit(solution)/shard_map/ppermute | solution.py:251
  14.9 6.0 %collective-permute-start.6 = (bf16[17,32,128]{2,1,0:T(8,128)(2,1)S(1)}, bf16[17,32,128]{2,1,0:T(8,128)(2,1)S(1)}, u32[]{:S(2)}, u32[]{:S(2)}) collective-permute-start(bf16[17,32,128]{2,1,0:T(8,128)(2,1)S(1)} %get-tuple-element.22), channel_id=1, source_target_pairs={{0,8},{8,0},{16,24},{24,16},{1,9},{9,1},{17,25},{25,17},{2,10},{10... | collective-permute-start | bytes 417800 | tf_op jit(solution)/shard_map/ppermute | solution.py:211
  17.3 6.7 %collective-permute-start.7 = (bf16[17,32,128]{2,1,0:T(8,128)(2,1)S(1)}, bf16[17,32,128]{2,1,0:T(8,128)(2,1)S(1)}, u32[]{:S(2)}, u32[]{:S(2)}) collective-permute-start(bf16[17,32,128]{2,1,0:T(8,128)(2,1)S(1)} %get-tuple-element.24), channel_id=1, source_target_pairs={{0,0},{4,4},{24,24},{28,28},{8,16},{12,20},{16,8},{20,12},{1,1},{5... | collective-permute-start | bytes 417800 | tf_op jit(solution)/shard_map/ppermute | solution.py:201
  24.0 9.0 %collective-permute-start.10 = (bf16[17,32,128]{2,1,0:T(8,128)(2,1)S(1)}, bf16[17,32,128]{2,1,0:T(8,128)(2,1)S(1)}, u32[]{:S(2)}, u32[]{:S(2)}) collective-permute-start(bf16[17,32,128]{2,1,0:T(8,128)(2,1)S(1)} %finish.2.refs_0_), channel_id=1, source_target_pairs={{0,2},{1,3},{2,0},{3,1},{4,6},{5,7},{6,4},{7,5},{8,10},{9,11},{10,... | collective-permute-start | bytes 417800 | tf_op jit(solution)/shard_map/ppermute | solution.py:256
  25.0 8.0 %collective-permute-start.9 = (bf16[17,32,128]{2,1,0:T(8,128)(2,1)S(1)}, bf16[17,32,128]{2,1,0:T(8,128)(2,1)S(1)}, u32[]{:S(2)}, u32[]{:S(2)}) collective-permute-start(bf16[17,32,128]{2,1,0:T(8,128)(2,1)S(1)} %finish.2.refs_0_), channel_id=1, source_target_pairs={{0,1},{1,0},{2,3},{3,2},{4,5},{5,4},{6,7},{7,6},{8,9},{9,8},{10,11... | collective-permute-start | bytes 417800 | tf_op jit(solution)/shard_map/ppermute | solution.py:256
  26.1 6.9 %collective-permute-start.8 = (bf16[17,32,128]{2,1,0:T(8,128)(2,1)S(1)}, bf16[17,32,128]{2,1,0:T(8,128)(2,1)S(1)}, u32[]{:S(2)}, u32[]{:S(2)}) collective-permute-start(bf16[17,32,128]{2,1,0:T(8,128)(2,1)S(1)} %finish.2.refs_0_), channel_id=1, source_target_pairs={{0,3},{1,2},{2,1},{3,0},{4,7},{5,6},{6,5},{7,4},{8,11},{9,10},{10,... | collective-permute-start | bytes 417800 | tf_op jit(solution)/shard_map/ppermute | solution.py:256
  33.6 4.5 %collective-permute-start.11 = (bf16[16,32,128]{2,1,0:T(8,128)(2,1)S(1)}, bf16[16,32,128]{2,1,0:T(8,128)(2,1)S(1)}, u32[]{:S(2)}, u32[]{:S(2)}) collective-permute-start(bf16[16,32,128]{2,1,0:T(8,128)(2,1)S(1)} %get-tuple-element.26), channel_id=1, source_target_pairs={{8,16},{12,20},{0,4},{24,28},{16,8},{20,12},{4,0},{28,24},{9,17},{... | collective-permute-start | bytes 393224 | tf_op jit(solution)/shard_map/ppermute | solution.py:201
  35.9 2.1 %collective-permute-start.12 = (bf16[16,32,128]{2,1,0:T(8,128)(2,1)S(1)}, bf16[16,32,128]{2,1,0:T(8,128)(2,1)S(1)}, u32[]{:S(2)}, u32[]{:S(2)}) collective-permute-start(bf16[16,32,128]{2,1,0:T(8,128)(2,1)S(1)} %get-tuple-element.29), channel_id=1, source_target_pairs={{0,8},{8,0},{16,24},{24,16},{1,9},{9,1},{17,25},{25,17},{2,10},{10... | collective-permute-start | bytes 393224 | tf_op jit(solution)/shard_map/ppermute | solution.py:211
